TPU v7x, 512 devices: a whole 4x8x8 slice. The times are simulated.
512 devices in a mesh: gx: 16 (over y_lo, z), gy: 8 (over y_hi, core), gz: 4 (over x).
Axes of the slice: x: 4, y: 8 (y_hi: 4, y_lo: 2; y = y_hi * 2 + y_lo), z: 8, core: 2. Of those that a mesh axis runs over, the one named last changes fastest.
Arguments:
- fields: float32 [4, 128, 256, 512], P(None, 'gx', 'gy', 'gz'), may hold values from -6 to 6
- velocity: float32 [3, 128, 256, 512], P(None, 'gx', 'gy', 'gz'), may hold values from -3 to 3
- diffusivity: float32 [4], replicated, may hold values from 0.05 to 0.5
- coupling: float32 [4, 4], replicated, may hold values from -1 to 1
- factor_x: float32 [128, 32], P('gx'), may hold values from -1 to 1, as said below
- factor_y: float32 [256, 32], P('gy'), may hold values from -1 to 1, as said below
- factor_z: float32 [512, 32], P('gz'), may hold values from -1 to 1, as said below
Outputs:
- core_tensor: float32 [4, 32, 32, 32], P(None, 'gx', 'gy', 'gz')
Inputs may be any that keep to these rules, and one draw needn't show every extreme that they name: `factor_x`: the columns of each factor are orthonormal. `factor_y`: the columns of each factor are orthonormal. `factor_z`: the columns of each factor are orthonormal.
All inputs are finite; a program needn't handle non-finite values.
Results may differ from a plain program's by a relative error of at most 0.0003.
Values sent between devices are 32-bit elements; how exact they have to be, the bound alone decides.
No kernel may reach another device: no remote copies, remote signals or barrier semaphores. Data moves between devices by JAX's collectives and lax.ppermute only.
A program may use at most 64 MiB of HBM per device.

v0:
```python
import jax
import jax.numpy as jnp
from jax import lax
from jax.sharding import PartitionSpec as P

STEPS = 2


time_step = 0.2


def padded_2(shard, sides, width):
    edges = {}
    for axis, dim in sides:
        devices, length = (lax.axis_size(axis), shard.shape[dim])
        up = [(i, (i + 1) % devices) for i in range(devices - 1)]
        last = lax.slice_in_dim(shard, length - width, length, axis=dim)
        initial = lax.slice_in_dim(shard, 0, width, axis=dim)
        edges[dim] = (
            lax.ppermute(last, axis, up),
            lax.ppermute(initial, axis, [(b, a) for a, b in up]),
        )
    done = []
    for _, dim in sides:
        low, high = edges[dim]
        around = [(width, width) if d in done else (0, 0) for d in range(shard.ndim)]
        shard = jnp.concatenate([jnp.pad(low, around), shard, jnp.pad(high, around)], axis=dim)
        done.append(dim)
    return shard


def in_blocks(shard, dim, devices):
    before, after = (shard.shape[:dim], shard.shape[dim + 1 :])
    return jnp.moveaxis(shard.reshape(*before, devices, -1, *after), dim, 0)


def sent_and_summed(shard, axis, dim):
    devices = lax.axis_size(axis)
    tiles = lax.all_to_all(in_blocks(shard, dim, devices), axis, 0, 0, tiled=True)
    return jnp.sum(tiles, axis=0)


def offset_view(padded, dimension, offset):
    indices = [slice(None)]
    for other in (1, 2, 3):
        if other == dimension:
            first_cell = 2 + offset
            indices.append(slice(first_cell, first_cell + padded.shape[other] - 4))
        else:
            indices.append(slice(2, padded.shape[other] - 2))
    return padded[tuple(indices)]


def tendency(padded, velocity, diffusivity, coupling):
    center = offset_view(padded, 1, 0)
    transport = jnp.zeros_like(center)
    laplace = jnp.zeros_like(center)
    for dimension in (1, 2, 3):
        gradient = (
            8.0 * (offset_view(padded, dimension, 1) - offset_view(padded, dimension, -1))
            - (offset_view(padded, dimension, 2) - offset_view(padded, dimension, -2))
        ) / 12.0
        transport = transport + velocity[dimension - 1][None] * gradient
        laplace = (
            laplace
            + offset_view(padded, dimension, 1)
            + offset_view(padded, dimension, -1)
            - 2.0 * center
        )
    mixing = jnp.einsum("vw,wxyz->vxyz", coupling, center, precision=lax.Precision.HIGHEST)
    return -transport + diffusivity[:, None, None, None] * laplace + center * mixing


def with_edges(values):
    return padded_2(values, (("gx", 1), ("gy", 2), ("gz", 3)), 2)


def local(fields, velocity, diffusivity, coupling, factor_x, factor_y, factor_z):
    state = fields
    for repeat in range(STEPS):
        section = state + time_step * tendency(with_edges(state), velocity, diffusivity, coupling)
        state = 0.5 * (
            state
            + section
            + time_step * tendency(with_edges(section), velocity, diffusivity, coupling)
        )
    highest = lax.Precision.HIGHEST
    partial_value = jnp.einsum("vxyz,zc->vxyc", state, factor_z, precision=highest)
    partial_value = sent_and_summed(partial_value, "gz", 3)
    partial_value = jnp.einsum("vxyc,yb->vxbc", partial_value, factor_y, precision=highest)
    partial_value = sent_and_summed(partial_value, "gy", 2)
    partial_value = jnp.einsum("vxbc,xa->vabc", partial_value, factor_x, precision=highest)
    core_tensor = sent_and_summed(partial_value, "gx", 1)
    return core_tensor


def solution(mesh):
    return jax.shard_map(
        local,
        mesh=mesh,
        in_specs=(
            P(None, "gx", "gy", "gz"),
            P(None, "gx", "gy", "gz"),
            P(),
            P(),
            P("gx", None),
            P("gy", None),
            P("gz", None),
        ),
        out_specs=P(None, "gx", "gy", "gz"),
        check_vma=False,
    )
```

profile of v0, /device:TPU:1, one launch (start us, length us, event | category | flops | bytes accessed | tf_op | source)
XLA Modules:
  0.0 196.0 jit_solution(8741000714206542600)
XLA Ops:
  3.3 8.7 %collective-permute-start.2 = (f32[4,8,2,128]{3,0,2,1:T(4,128)S(1)}, f32[4,8,2,128]{3,0,2,1:T(4,128)S(1)}, u32[]{:S(2)}, u32[]{:S(2)}) collective-permute-start(f32[4,8,2,128]{3,0,2,1:T(4,128)S(1)} %copy.83), channel_id=1, source_target_pairs={{4,0},{8,4},{12,8},{16,12},{20,16},{24,20},{28,24},{5,1},{9,5},{13... | collective-permute-start | bytes 98312 | tf_op jit(solution)/shard_map/ppermute | solution.py:21
  17.2 4.3 %collective-permute-start.5 = (f32[4,8,32,2]{3,0,2,1:T(4,128)S(1)}, f32[4,8,32,2]{3,0,2,1:T(4,128)S(1)}, u32[]{:S(2)}, u32[]{:S(2)}) collective-permute-start(f32[4,8,32,2]{3,0,2,1:T(4,128)S(1)} %copy.82), channel_id=1, source_target_pairs={{0,1},{1,2},{2,3},{4,5},{5,6},{6,7},{8,9},{9,10},{10,11},{12,13},{... | collective-permute-start | bytes 24584 | tf_op jit(solution)/shard_map/ppermute | solution.py:20
  22.3 10.0 %collective-permute-done.5 = f32[4,8,32,2]{3,0,2,1:T(4,128)S(1)} collective-permute-done((f32[4,8,32,2]{3,0,2,1:T(4,128)S(1)}, f32[4,8,32,2]{3,0,2,1:T(4,128)S(1)}, u32[]{:S(2)}, u32[]{:S(2)}) %collective-permute-start.5) | collective-permute-done | bytes 8224 | tf_op jit(solution)/shard_map/ppermute | solution.py:20
  34.1 2.9 %fusion.2 = f32[4,8,32,128]{3,0,2,1:T(4,128)S(1)} fusion(f32[4,12,36,130]{3,0,2,1:T(4,128)S(1)} %get-tuple-element.12, f32[4,12,36,130]{3,0,2,1:T(4,128)S(1)} %get-tuple-element.11, f32[4,12,32,128]{3,0,2,1:T(4,128)S(1)} %get-tuple-element.50, f32[4,12,2,128]{3,0,2,1:T(4,128)S(1)} %pad.51, f32[4,12,2,128]{3,0,2,1:T(4,128)S(1)} %pad.50, ...), kind=kOutput, calls=%fused_computation.13 | convolution fusion | flops 11141120 | bytes 7047680 | tf_op jit(solution)/shard_map/vw,wxyz->vxyz/dot_general | solution.py:70
  37.0 3.3 %collective-permute-start.8 = (f32[4,8,2,128]{3,0,2,1:T(4,128)S(1)}, f32[4,8,2,128]{3,0,2,1:T(4,128)S(1)}, u32[]{:S(2)}, u32[]{:S(2)}) collective-permute-start(f32[4,8,2,128]{3,0,2,1:T(4,128)S(1)} %get-tuple-element.34), channel_id=1, source_target_pairs={{4,0},{8,4},{12,8},{16,12},{20,16},{24,20},{28,24},{5,1},{9,5},{13... | collective-permute-start | bytes 98312 | tf_op jit(solution)/shard_map/ppermute | solution.py:21
  41.6 5.1 %collective-permute-start.7 = (f32[4,2,32,128]{3,0,2,1:T(4,128)S(1)}, f32[4,2,32,128]{3,0,2,1:T(4,128)S(1)}, u32[]{:S(2)}, u32[]{:S(2)}) collective-permute-start(f32[4,2,32,128]{3,0,2,1:T(4,128)S(1)} %get-tuple-element.35), channel_id=1, source_target_pairs={{0,32},{32,64},{64,96},{96,128},{128,160},{160,192},{192,224},{224... | collective-permute-start | bytes 393224 | tf_op jit(solution)/shard_map/ppermute | solution.py:20
  46.7 4.0 %collective-permute-start.9 = (f32[4,8,2,128]{3,0,2,1:T(4,128)S(1)}, f32[4,8,2,128]{3,0,2,1:T(4,128)S(1)}, u32[]{:S(2)}, u32[]{:S(2)}) collective-permute-start(f32[4,8,2,128]{3,0,2,1:T(4,128)S(1)} %get-tuple-element.33), channel_id=1, source_target_pairs={{0,4},{4,8},{8,12},{12,16},{16,20},{20,24},{24,28},{1,5},{5,9},{9,... | collective-permute-start | bytes 98312 | tf_op jit(solution)/shard_map/ppermute | solution.py:20
  52.3 4.8 %collective-permute-start.11 = (f32[4,8,32,2]{3,0,2,1:T(4,128)S(1)}, f32[4,8,32,2]{3,0,2,1:T(4,128)S(1)}, u32[]{:S(2)}, u32[]{:S(2)}) collective-permute-start(f32[4,8,32,2]{3,0,2,1:T(4,128)S(1)} %get-tuple-element.32), channel_id=1, source_target_pairs={{0,1},{1,2},{2,3},{4,5},{5,6},{6,7},{8,9},{9,10},{10,11},{12,13},{... | collective-permute-start | bytes 24584 | tf_op jit(solution)/shard_map/ppermute | solution.py:20
  57.4 8.5 %collective-permute-done.10 = f32[4,8,32,2]{3,0,2,1:T(4,128)S(1)} collective-permute-done((f32[4,8,32,2]{3,0,2,1:T(4,128)S(1)}, f32[4,8,32,2]{3,0,2,1:T(4,128)S(1)}, u32[]{:S(2)}, u32[]{:S(2)}) %collective-permute-start.10) | collective-permute-done | bytes 8224 | tf_op jit(solution)/shard_map/ppermute | solution.py:21
  67.7 3.1 %select_maximum_fusion.5 = (f32[4,12,36,130]{3,0,2,1:T(4,128)S(1)}, f32[4,12,36,130]{3,0,2,1:T(4,128)S(1)}) fusion(f32[4,8,32,2]{3,0,2,1:T(4,128)S(1)} %collective-permute-done.10, f32[4,12,2,128]{3,0,2,1:T(4,128)S(1)} %pad.54, f32[4,2,32,128]{3,0,2,1:T(4,128)S(1)} %collective-permute-done.6, f32[4,8,32,128]{3,0,2,1:T(4,128)S(1)} %fusion.2, ...), kind=kLoop, calls=%fused_computation.5 | loop fusion | flops 3144960 | bytes 2698240 | tf_op jit(solution)/shard_map/concatenate | solution.py:27
  70.8 2.8 %broadcast_multiply_fusion = (f32[4,8,32,128]{3,0,2,1:T(4,128)S(1)}, f32[4,8,32,128]{3,0,2,1:T(4,128)S(1)}) fusion(f32[4,8,32,128]{3,0,2,1:T(4,128)S(1)} %fusion.2, f32[4,4]{1,0:T(4,128)S(1)} %copy-done.5, f32[4]{0:T(128)S(1)} %copy-done.6, f32[8,32,128]{2,1,0:T(8,128)S(1)} %get-tuple-element.47, f32[4,12,36,130]{3,0,2,1:T(4,128)S(1)} %get-tuple-element.10, ...), kind=kOutput, calls=%fused_computation.133 | convolution fusion | flops 11403264 | bytes 7473664 | tf_op jit(solution)/shard_map/vw,wxyz->vxyz/dot_general | solution.py:70
  76.9 4.0 %collective-permute-start.13 = (f32[4,2,32,128]{3,0,2,1:T(4,128)S(1)}, f32[4,2,32,128]{3,0,2,1:T(4,128)S(1)}, u32[]{:S(2)}, u32[]{:S(2)}) collective-permute-start(f32[4,2,32,128]{3,0,2,1:T(4,128)S(1)} %get-tuple-element.29), channel_id=1, source_target_pairs={{0,32},{32,64},{64,96},{96,128},{128,160},{160,192},{192,224},{224... | collective-permute-start | bytes 393224 | tf_op jit(solution)/shard_map/ppermute | solution.py:20
  80.9 5.1 %collective-permute-start.15 = (f32[4,8,2,128]{3,0,2,1:T(4,128)S(1)}, f32[4,8,2,128]{3,0,2,1:T(4,128)S(1)}, u32[]{:S(2)}, u32[]{:S(2)}) collective-permute-start(f32[4,8,2,128]{3,0,2,1:T(4,128)S(1)} %get-tuple-element.27), channel_id=1, source_target_pairs={{0,4},{4,8},{8,12},{12,16},{16,20},{20,24},{24,28},{1,5},{5,9},{9,... | collective-permute-start | bytes 98312 | tf_op jit(solution)/shard_map/ppermute | solution.py:20
  87.7 4.5 %collective-permute-start.17 = (f32[4,8,32,2]{3,0,2,1:T(4,128)S(1)}, f32[4,8,32,2]{3,0,2,1:T(4,128)S(1)}, u32[]{:S(2)}, u32[]{:S(2)}) collective-permute-start(f32[4,8,32,2]{3,0,2,1:T(4,128)S(1)} %get-tuple-element.26), channel_id=1, source_target_pairs={{0,1},{1,2},{2,3},{4,5},{5,6},{6,7},{8,9},{9,10},{10,11},{12,13},{... | collective-permute-start | bytes 24584 | tf_op jit(solution)/shard_map/ppermute | solution.py:20
  92.5 7.4 %collective-permute-done.16 = f32[4,8,32,2]{3,0,2,1:T(4,128)S(1)} collective-permute-done((f32[4,8,32,2]{3,0,2,1:T(4,128)S(1)}, f32[4,8,32,2]{3,0,2,1:T(4,128)S(1)}, u32[]{:S(2)}, u32[]{:S(2)}) %collective-permute-start.16) | collective-permute-done | bytes 8224 | tf_op jit(solution)/shard_map/ppermute | solution.py:21
  101.6 3.1 %select_maximum_fusion.3 = (f32[4,12,36,130]{3,0,2,1:T(4,128)S(1)}, f32[4,12,36,130]{3,0,2,1:T(4,128)S(1)}) fusion(f32[4,8,32,2]{3,0,2,1:T(4,128)S(1)} %collective-permute-done.16, f32[4,12,2,128]{3,0,2,1:T(4,128)S(1)} %pad.58, f32[4,2,32,128]{3,0,2,1:T(4,128)S(1)} %collective-permute-done.12, f32[4,8,32,128]{3,0,2,1:T(4,128)S(1)} %get-tuple-element.53, ...), kind=kLoop, calls=%fused_computation.3 | loop fusion | flops 3144960 | bytes 2698240 | tf_op jit(solution)/shard_map/concatenate | solution.py:27
  110.3 4.3 %collective-permute-start.19 = (f32[4,2,32,128]{3,0,2,1:T(4,128)S(1)}, f32[4,2,32,128]{3,0,2,1:T(4,128)S(1)}, u32[]{:S(2)}, u32[]{:S(2)}) collective-permute-start(f32[4,2,32,128]{3,0,2,1:T(4,128)S(1)} %get-tuple-element.23), channel_id=1, source_target_pairs={{0,32},{32,64},{64,96},{96,128},{128,160},{160,192},{192,224},{224... | collective-permute-start | bytes 393224 | tf_op jit(solution)/shard_map/ppermute | solution.py:20
  114.6 5.0 %collective-permute-start.21 = (f32[4,8,2,128]{3,0,2,1:T(4,128)S(1)}, f32[4,8,2,128]{3,0,2,1:T(4,128)S(1)}, u32[]{:S(2)}, u32[]{:S(2)}) collective-permute-start(f32[4,8,2,128]{3,0,2,1:T(4,128)S(1)} %get-tuple-element.21), channel_id=1, source_target_pairs={{0,4},{4,8},{8,12},{12,16},{16,20},{20,24},{24,28},{1,5},{5,9},{9,... | collective-permute-start | bytes 98312 | tf_op jit(solution)/shard_map/ppermute | solution.py:20
  121.3 4.5 %collective-permute-start.23 = (f32[4,8,32,2]{3,0,2,1:T(4,128)S(1)}, f32[4,8,32,2]{3,0,2,1:T(4,128)S(1)}, u32[]{:S(2)}, u32[]{:S(2)}) collective-permute-start(f32[4,8,32,2]{3,0,2,1:T(4,128)S(1)} %get-tuple-element.20), channel_id=1, source_target_pairs={{0,1},{1,2},{2,3},{4,5},{5,6},{6,7},{8,9},{9,10},{10,11},{12,13},{... | collective-permute-start | bytes 24584 | tf_op jit(solution)/shard_map/ppermute | solution.py:20
  126.1 7.6 %collective-permute-done.22 = f32[4,8,32,2]{3,0,2,1:T(4,128)S(1)} collective-permute-done((f32[4,8,32,2]{3,0,2,1:T(4,128)S(1)}, f32[4,8,32,2]{3,0,2,1:T(4,128)S(1)}, u32[]{:S(2)}, u32[]{:S(2)}) %collective-permute-start.22) | collective-permute-done | bytes 8224 | tf_op jit(solution)/shard_map/ppermute | solution.py:21
  135.5 3.1 %select_maximum_fusion.1 = (f32[4,12,36,130]{3,0,2,1:T(4,128)S(1)}, f32[4,12,36,130]{3,0,2,1:T(4,128)S(1)}) fusion(f32[4,8,32,2]{3,0,2,1:T(4,128)S(1)} %collective-permute-done.22, f32[4,12,2,128]{3,0,2,1:T(4,128)S(1)} %pad.62, f32[4,2,32,128]{3,0,2,1:T(4,128)S(1)} %collective-permute-done.18, f32[4,8,32,128]{3,0,2,1:T(4,128)S(1)} %fusion.9, ...), kind=kLoop, calls=%fused_computation.1 | loop fusion | flops 3144960 | bytes 2698240 | tf_op jit(solution)/shard_map/concatenate | solution.py:27
  143.9 11.0 %all_to_all.15 = f32[4,1,8192]{2,1,0:T(1,128)S(1)} all-to-all(f32[4,1,8192]{2,1,0:T(1,128)S(1)} %reshape.23), channel_id=1, replica_groups=mesh['gx'=16,'gy'=8,'gz'=4] {'gz'}, dimensions={0} | all-to-all | bytes 262144 | tf_op jit(solution)/shard_map/all_to_all | solution.py:39
  157.4 15.6 %all_to_all.16 = f32[8,1,1024]{2,1,0:T(1,128)S(1)} all-to-all(f32[8,1,1024]{2,1,0:T(1,128)S(1)} %reshape.25), channel_id=1, replica_groups=mesh['gx'=16,'gy'=8,'gz'=4] {'gy'}, dimensions={0} | all-to-all | bytes 65536 | tf_op jit(solution)/shard_map/all_to_all | solution.py:39
  175.1 19.1 %all_to_all.17 = f32[16,1,256]{2,1,0:T(1,128)S(1)} all-to-all(f32[16,1,256]{2,1,0:T(1,128)S(1)} %reshape.27), channel_id=1, replica_groups=mesh['gx'=16,'gy'=8,'gz'=4] {'gx'}, dimensions={0} | all-to-all | bytes 32768 | tf_op jit(solution)/shard_map/all_to_all | solution.py:39
  (104 shorter events, 43.5 us)
Async XLA Ops:
  1.9 20.3 %collective-permute-start.4 = (f32[4,8,32,2]{3,0,2,1:T(4,128)S(1)}, f32[4,8,32,2]{3,0,2,1:T(4,128)S(1)}, u32[]{:S(2)}, u32[]{:S(2)}) collective-permute-start(f32[4,8,32,2]{3,0,2,1:T(4,128)S(1)} %copy.87), channel_id=1, source_target_pairs={{1,0},{2,1},{3,2},{5,4},{6,5},{7,6},{9,8},{10,9},{11,10},{13,12},{... | collective-permute-start | bytes 24584 | tf_op jit(solution)/shard_map/ppermute | solution.py:21
  3.3 13.9 %collective-permute-start.2 = (f32[4,8,2,128]{3,0,2,1:T(4,128)S(1)}, f32[4,8,2,128]{3,0,2,1:T(4,128)S(1)}, u32[]{:S(2)}, u32[]{:S(2)}) collective-permute-start(f32[4,8,2,128]{3,0,2,1:T(4,128)S(1)} %copy.83), channel_id=1, source_target_pairs={{4,0},{8,4},{12,8},{16,12},{20,16},{24,20},{28,24},{5,1},{9,5},{13... | collective-permute-start | bytes 98312 | tf_op jit(solution)/shard_map/ppermute | solution.py:21
  12.2 9.4 %collective-permute-start.1 = (f32[4,2,32,128]{3,0,2,1:T(4,128)S(1)}, f32[4,2,32,128]{3,0,2,1:T(4,128)S(1)}, u32[]{:S(2)}, u32[]{:S(2)}) collective-permute-start(f32[4,2,32,128]{3,0,2,1:T(4,128)S(1)} %copy.84), channel_id=1, source_target_pairs={{0,32},{32,64},{64,96},{96,128},{128,160},{160,192},{192,224},{224... | collective-permute-start | bytes 393224 | tf_op jit(solution)/shard_map/ppermute | solution.py:20
  13.6 8.6 %collective-permute-start = (f32[4,2,32,128]{3,0,2,1:T(4,128)S(1)}, f32[4,2,32,128]{3,0,2,1:T(4,128)S(1)}, u32[]{:S(2)}, u32[]{:S(2)}) collective-permute-start(f32[4,2,32,128]{3,0,2,1:T(4,128)S(1)} %copy.85), channel_id=1, source_target_pairs={{32,0},{64,32},{96,64},{128,96},{160,128},{192,160},{224,192},{256... | collective-permute-start | bytes 393224 | tf_op jit(solution)/shard_map/ppermute | solution.py:21
  14.9 6.7 %collective-permute-start.3 = (f32[4,8,2,128]{3,0,2,1:T(4,128)S(1)}, f32[4,8,2,128]{3,0,2,1:T(4,128)S(1)}, u32[]{:S(2)}, u32[]{:S(2)}) collective-permute-start(f32[4,8,2,128]{3,0,2,1:T(4,128)S(1)} %copy.86), channel_id=1, source_target_pairs={{0,4},{4,8},{8,12},{12,16},{16,20},{20,24},{24,28},{1,5},{5,9},{9,... | collective-permute-start | bytes 98312 | tf_op jit(solution)/shard_map/ppermute | solution.py:20
  17.2 15.0 %collective-permute-start.5 = (f32[4,8,32,2]{3,0,2,1:T(4,128)S(1)}, f32[4,8,32,2]{3,0,2,1:T(4,128)S(1)}, u32[]{:S(2)}, u32[]{:S(2)}) collective-permute-start(f32[4,8,32,2]{3,0,2,1:T(4,128)S(1)} %copy.82), channel_id=1, source_target_pairs={{0,1},{1,2},{2,3},{4,5},{5,6},{6,7},{8,9},{9,10},{10,11},{12,13},{... | collective-permute-start | bytes 24584 | tf_op jit(solution)/shard_map/ppermute | solution.py:20
  37.0 15.3 %collective-permute-start.8 = (f32[4,8,2,128]{3,0,2,1:T(4,128)S(1)}, f32[4,8,2,128]{3,0,2,1:T(4,128)S(1)}, u32[]{:S(2)}, u32[]{:S(2)}) collective-permute-start(f32[4,8,2,128]{3,0,2,1:T(4,128)S(1)} %get-tuple-element.34), channel_id=1, source_target_pairs={{4,0},{8,4},{12,8},{16,12},{20,16},{24,20},{28,24},{5,1},{9,5},{13... | collective-permute-start | bytes 98312 | tf_op jit(solution)/shard_map/ppermute | solution.py:21
  40.3 16.8 %collective-permute-start.6 = (f32[4,2,32,128]{3,0,2,1:T(4,128)S(1)}, f32[4,2,32,128]{3,0,2,1:T(4,128)S(1)}, u32[]{:S(2)}, u32[]{:S(2)}) collective-permute-start(f32[4,2,32,128]{3,0,2,1:T(4,128)S(1)} %get-tuple-element.36), channel_id=1, source_target_pairs={{32,0},{64,32},{96,64},{128,96},{160,128},{192,160},{224,192},{256... | collective-permute-start | bytes 393224 | tf_op jit(solution)/shard_map/ppermute | solution.py:21
  41.6 15.6 %collective-permute-start.7 = (f32[4,2,32,128]{3,0,2,1:T(4,128)S(1)}, f32[4,2,32,128]{3,0,2,1:T(4,128)S(1)}, u32[]{:S(2)}, u32[]{:S(2)}) collective-permute-start(f32[4,2,32,128]{3,0,2,1:T(4,128)S(1)} %get-tuple-element.35), channel_id=1, source_target_pairs={{0,32},{32,64},{64,96},{96,128},{128,160},{160,192},{192,224},{224... | collective-permute-start | bytes 393224 | tf_op jit(solution)/shard_map/ppermute | solution.py:20
  46.7 10.4 %collective-permute-start.9 = (f32[4,8,2,128]{3,0,2,1:T(4,128)S(1)}, f32[4,8,2,128]{3,0,2,1:T(4,128)S(1)}, u32[]{:S(2)}, u32[]{:S(2)}) collective-permute-start(f32[4,8,2,128]{3,0,2,1:T(4,128)S(1)} %get-tuple-element.33), channel_id=1, source_target_pairs={{0,4},{4,8},{8,12},{12,16},{16,20},{20,24},{24,28},{1,5},{5,9},{9,... | collective-permute-start | bytes 98312 | tf_op jit(solution)/shard_map/ppermute | solution.py:20
  51.0 14.9 %collective-permute-start.10 = (f32[4,8,32,2]{3,0,2,1:T(4,128)S(1)}, f32[4,8,32,2]{3,0,2,1:T(4,128)S(1)}, u32[]{:S(2)}, u32[]{:S(2)}) collective-permute-start(f32[4,8,32,2]{3,0,2,1:T(4,128)S(1)} %get-tuple-element.31), channel_id=1, source_target_pairs={{1,0},{2,1},{3,2},{5,4},{6,5},{7,6},{9,8},{10,9},{11,10},{13,12},{... | collective-permute-start | bytes 24584 | tf_op jit(solution)/shard_map/ppermute | solution.py:21
  52.3 15.4 %collective-permute-start.11 = (f32[4,8,32,2]{3,0,2,1:T(4,128)S(1)}, f32[4,8,32,2]{3,0,2,1:T(4,128)S(1)}, u32[]{:S(2)}, u32[]{:S(2)}) collective-permute-start(f32[4,8,32,2]{3,0,2,1:T(4,128)S(1)} %get-tuple-element.32), channel_id=1, source_target_pairs={{0,1},{1,2},{2,3},{4,5},{5,6},{6,7},{8,9},{9,10},{10,11},{12,13},{... | collective-permute-start | bytes 24584 | tf_op jit(solution)/shard_map/ppermute | solution.py:20
  73.7 14.0 %collective-permute-start.14 = (f32[4,8,2,128]{3,0,2,1:T(4,128)S(1)}, f32[4,8,2,128]{3,0,2,1:T(4,128)S(1)}, u32[]{:S(2)}, u32[]{:S(2)}) collective-permute-start(f32[4,8,2,128]{3,0,2,1:T(4,128)S(1)} %get-tuple-element.28), channel_id=1, source_target_pairs={{4,0},{8,4},{12,8},{16,12},{20,16},{24,20},{28,24},{5,1},{9,5},{13... | collective-permute-start | bytes 98312 | tf_op jit(solution)/shard_map/ppermute | solution.py:21
  75.6 16.6 %collective-permute-start.12 = (f32[4,2,32,128]{3,0,2,1:T(4,128)S(1)}, f32[4,2,32,128]{3,0,2,1:T(4,128)S(1)}, u32[]{:S(2)}, u32[]{:S(2)}) collective-permute-start(f32[4,2,32,128]{3,0,2,1:T(4,128)S(1)} %get-tuple-element.30), channel_id=1, source_target_pairs={{32,0},{64,32},{96,64},{128,96},{160,128},{192,160},{224,192},{256... | collective-permute-start | bytes 393224 | tf_op jit(solution)/shard_map/ppermute | solution.py:21
  76.9 15.3 %collective-permute-start.13 = (f32[4,2,32,128]{3,0,2,1:T(4,128)S(1)}, f32[4,2,32,128]{3,0,2,1:T(4,128)S(1)}, u32[]{:S(2)}, u32[]{:S(2)}) collective-permute-start(f32[4,2,32,128]{3,0,2,1:T(4,128)S(1)} %get-tuple-element.29), channel_id=1, source_target_pairs={{0,32},{32,64},{64,96},{96,128},{128,160},{160,192},{192,224},{224... | collective-permute-start | bytes 393224 | tf_op jit(solution)/shard_map/ppermute | solution.py:20
  80.9 11.3 %collective-permute-start.15 = (f32[4,8,2,128]{3,0,2,1:T(4,128)S(1)}, f32[4,8,2,128]{3,0,2,1:T(4,128)S(1)}, u32[]{:S(2)}, u32[]{:S(2)}) collective-permute-start(f32[4,8,2,128]{3,0,2,1:T(4,128)S(1)} %get-tuple-element.27), channel_id=1, source_target_pairs={{0,4},{4,8},{8,12},{12,16},{16,20},{20,24},{24,28},{1,5},{5,9},{9,... | collective-permute-start | bytes 98312 | tf_op jit(solution)/shard_map/ppermute | solution.py:20
  86.4 13.5 %collective-permute-start.16 = (f32[4,8,32,2]{3,0,2,1:T(4,128)S(1)}, f32[4,8,32,2]{3,0,2,1:T(4,128)S(1)}, u32[]{:S(2)}, u32[]{:S(2)}) collective-permute-start(f32[4,8,32,2]{3,0,2,1:T(4,128)S(1)} %get-tuple-element.25), channel_id=1, source_target_pairs={{1,0},{2,1},{3,2},{5,4},{6,5},{7,6},{9,8},{10,9},{11,10},{13,12},{... | collective-permute-start | bytes 24584 | tf_op jit(solution)/shard_map/ppermute | solution.py:21
  87.7 13.9 %collective-permute-start.17 = (f32[4,8,32,2]{3,0,2,1:T(4,128)S(1)}, f32[4,8,32,2]{3,0,2,1:T(4,128)S(1)}, u32[]{:S(2)}, u32[]{:S(2)}) collective-permute-start(f32[4,8,32,2]{3,0,2,1:T(4,128)S(1)} %get-tuple-element.26), channel_id=1, source_target_pairs={{0,1},{1,2},{2,3},{4,5},{5,6},{6,7},{8,9},{9,10},{10,11},{12,13},{... | collective-permute-start | bytes 24584 | tf_op jit(solution)/shard_map/ppermute | solution.py:20
  107.1 14.2 %collective-permute-start.20 = (f32[4,8,2,128]{3,0,2,1:T(4,128)S(1)}, f32[4,8,2,128]{3,0,2,1:T(4,128)S(1)}, u32[]{:S(2)}, u32[]{:S(2)}) collective-permute-start(f32[4,8,2,128]{3,0,2,1:T(4,128)S(1)} %get-tuple-element.22), channel_id=1, source_target_pairs={{4,0},{8,4},{12,8},{16,12},{20,16},{24,20},{28,24},{5,1},{9,5},{13... | collective-permute-start | bytes 98312 | tf_op jit(solution)/shard_map/ppermute | solution.py:21
  109.0 16.8 %collective-permute-start.18 = (f32[4,2,32,128]{3,0,2,1:T(4,128)S(1)}, f32[4,2,32,128]{3,0,2,1:T(4,128)S(1)}, u32[]{:S(2)}, u32[]{:S(2)}) collective-permute-start(f32[4,2,32,128]{3,0,2,1:T(4,128)S(1)} %get-tuple-element.24), channel_id=1, source_target_pairs={{32,0},{64,32},{96,64},{128,96},{160,128},{192,160},{224,192},{256... | collective-permute-start | bytes 393224 | tf_op jit(solution)/shard_map/ppermute | solution.py:21
  110.3 15.5 %collective-permute-start.19 = (f32[4,2,32,128]{3,0,2,1:T(4,128)S(1)}, f32[4,2,32,128]{3,0,2,1:T(4,128)S(1)}, u32[]{:S(2)}, u32[]{:S(2)}) collective-permute-start(f32[4,2,32,128]{3,0,2,1:T(4,128)S(1)} %get-tuple-element.23), channel_id=1, source_target_pairs={{0,32},{32,64},{64,96},{96,128},{128,160},{160,192},{192,224},{224... | collective-permute-start | bytes 393224 | tf_op jit(solution)/shard_map/ppermute | solution.py:20
  114.6 11.2 %collective-permute-start.21 = (f32[4,8,2,128]{3,0,2,1:T(4,128)S(1)}, f32[4,8,2,128]{3,0,2,1:T(4,128)S(1)}, u32[]{:S(2)}, u32[]{:S(2)}) collective-permute-start(f32[4,8,2,128]{3,0,2,1:T(4,128)S(1)} %get-tuple-element.21), channel_id=1, source_target_pairs={{0,4},{4,8},{8,12},{12,16},{16,20},{20,24},{24,28},{1,5},{5,9},{9,... | collective-permute-start | bytes 98312 | tf_op jit(solution)/shard_map/ppermute | solution.py:20
  120.0 13.8 %collective-permute-start.22 = (f32[4,8,32,2]{3,0,2,1:T(4,128)S(1)}, f32[4,8,32,2]{3,0,2,1:T(4,128)S(1)}, u32[]{:S(2)}, u32[]{:S(2)}) collective-permute-start(f32[4,8,32,2]{3,0,2,1:T(4,128)S(1)} %get-tuple-element.19), channel_id=1, source_target_pairs={{1,0},{2,1},{3,2},{5,4},{6,5},{7,6},{9,8},{10,9},{11,10},{13,12},{... | collective-permute-start | bytes 24584 | tf_op jit(solution)/shard_map/ppermute | solution.py:21
  121.3 14.2 %collective-permute-start.23 = (f32[4,8,32,2]{3,0,2,1:T(4,128)S(1)}, f32[4,8,32,2]{3,0,2,1:T(4,128)S(1)}, u32[]{:S(2)}, u32[]{:S(2)}) collective-permute-start(f32[4,8,32,2]{3,0,2,1:T(4,128)S(1)} %get-tuple-element.20), channel_id=1, source_target_pairs={{0,1},{1,2},{2,3},{4,5},{5,6},{6,7},{8,9},{9,10},{10,11},{12,13},{... | collective-permute-start | bytes 24584 | tf_op jit(solution)/shard_map/ppermute | solution.py:20
  (7 other events, 195.0 us)
where the time goes:
time: 197 us; the launch traced here: 196 us
  starting transfers between devices  74.8 us (38%)
  blocking collectives  45.7 us (23%)
  waiting for transfers between devices  38.9 us (20%)
  other arithmetic  14.4 us (7%)
  matrix products  13.5 us (7%)
  local copies, waits for them, and re-layouts  7.88 us (4%)
    ppermute x12, starting transfers between devices, padded_2(): lax.ppermute(last, axis, up)  48.7 us
    all_to_all x3, blocking collectives, sent_and_summed(): lax.all_to_all(in_blocks(shard, dim, devices), axis, 0, 0, tiled=True)  45.7 us
    ppermute x12, starting transfers between devices, padded_2(): lax.ppermute(initial, axis, [(b, a) for a, b in up])  26.2 us
    ppermute x12, waiting for transfers between devices, padded_2(): lax.ppermute(initial, axis, [(b, a) for a, b in up])  23.5 us
    ppermute x12, waiting for transfers between devices, padded_2(): lax.ppermute(last, axis, up)  15.3 us
    concatenate x7, other arithmetic, padded_2(): jnp.concatenate([jnp.pad(low, around), shard, jnp.pad(high, around)], axi...  11.8 us
    dot_general x4, matrix products, tendency(): jnp.einsum('vw,wxyz->vxyz', coupling, center, precision=lax.Precision.HIG...  10.5 us
  transfers between devices with their start and end apart: 24, of which 7 were waited for; matrix products, arithmetic and copies ran while one was open for 2% of the time, Pallas kernels for 0%

commit v1 on v0

v1 whole, which is shorter than its diff:
```python
import jax
import jax.numpy as jnp
from jax import lax
from jax.experimental import pallas as pl
from jax.experimental.pallas import tpu as pltpu
from jax.sharding import PartitionSpec as P

TIME_STEP = 0.2
F32 = jnp.float32
HIGHEST = lax.Precision.HIGHEST
PLANES, ROWS = 24, 64
LOW, HIGH = 8, 16


def vmem():
    return pl.BlockSpec(memory_space=pltpu.VMEM)


def smem():
    return pl.BlockSpec(memory_space=pltpu.SMEM)


def f32(*shape):
    return jax.ShapeDtypeStruct(shape, F32)


def call(kernel, out_shape, in_specs, name, scratch=(), work=1000000):
    many = isinstance(out_shape, (list, tuple))
    return pl.pallas_call(
        kernel,
        out_shape=out_shape,
        in_specs=in_specs,
        out_specs=[vmem() for _ in out_shape] if many else vmem(),
        scratch_shapes=list(scratch),
        cost_estimate=pl.CostEstimate(flops=work, bytes_accessed=work, transcendentals=0),
        name=name,
    )


def lanes_of(rows):
    return lax.broadcasted_iota(jnp.int32, (rows, 128), 1)


def within(lane, first, size):
    return (lane >= first) & (lane < first + size)


def pack_xz(f, v, x_up, x_down, z_up, z_down):
    lane = lanes_of(32)
    for i in range(4):
        for x in range(8):
            plane = f[i, x]
            x_up[i * 8 + x] = plane
            x_down[i * 8 + x] = plane
    for a in range(3):
        for j in range(6):
            x_up[32 + a * 6 + j] = v[a, 2 + j]
            x_down[32 + a * 6 + j] = v[a, j]

    def plane_edges(x, carry):
        up = jnp.zeros((32, 128), F32)
        down = jnp.zeros((32, 128), F32)
        for i in range(4):
            plane = f[i, x]
            up = jnp.where(within(lane, 32 * i, 8), pltpu.roll(plane, (32 * i + 8) % 128, 1), up)
            down = jnp.where(within(lane, 32 * i + 24, 8), pltpu.roll(plane, 32 * i + 24, 1), down)
        for a in range(3):
            plane = v[a, x]
            up = jnp.where(within(lane, 32 * a + 8, 8), pltpu.roll(plane, 32 * a + 16, 1), up)
            down = jnp.where(within(lane, 32 * a + 16, 8), pltpu.roll(plane, 32 * a + 16, 1), down)
        z_up[x] = up
        z_down[x] = down
        return carry

    lax.fori_loop(0, 8, plane_edges, 0)


def pack_y(f, v, z_left, z_right, y_up, y_down):
    for out, row in ((y_up, 24), (y_down, 0)):
        for x in range(8):
            for i in range(4):
                out[i * 8 + x] = f[i, x, row : row + 8]
            for a in range(3):
                out[32 + a * 8 + x] = v[a, x, row : row + 8]
            out[56 + x] = z_left[x, row : row + 8] + z_right[x, row : row + 8]


def pack_x2(z_left, z_right, y_low, y_high, up, down):
    for out, first, first4 in ((up, 2, 4), (down, 0, 0)):
        for side, rows in ((0, y_low), (1, y_high)):
            for i in range(4):
                for j in range(6):
                    out[(i * 6 + j) * 2 + side] = rows[i * 8 + first + j]
            for a in range(3):
                for j in range(4):
                    out[48 + (a * 4 + j) * 2 + side] = rows[32 + a * 8 + first4 + j]
            for j in range(4):
                out[96 + j * 2 + side] = rows[56 + first4 + j]
        for j in range(6):
            halo = z_left[first + j] + z_right[first + j]
            for t in range(4):
                out[72 + j * 4 + t] = halo[8 * t : 8 * t + 8]


def spread_factor(fz, out):
    lane = lanes_of(128)
    wide = jnp.concatenate([fz[...], jnp.zeros((128, 96), F32)], axis=1)
    for v in range(4):
        placed = jnp.zeros((128, 128), F32)
        for k in range(4):
            rolled = pltpu.roll(wide, (24 * k + 8 * v) % 128, 1)
            placed = jnp.where(within(lane, 32 * k + 8 * v, 8), rolled, placed)
        out[v] = placed


def advance(
    d, c, f, v, z_left, z_right, x_low, x_high, y_low, y_high, e_low, e_high, rhs, fy,
    out, state, section, edge, edge2, wind, edge_wind, zm, final, mixed,
):
    gx, gy, gz = (lax.axis_index(n) for n in ("gx", "gy", "gz"))
    last_x, last_y, last_z = (lax.axis_size(n) - 1 for n in ("gx", "gy", "gz"))
    x_first, x_end = jnp.where(gx == 0, LOW, 0), jnp.where(gx == last_x, HIGH, PLANES)
    y_first, y_end = jnp.where(gy == 0, 16, 0), jnp.where(gy == last_y, 48, ROWS)
    scale = TIME_STEP / 12.0

    for i in range(4):
        for x in range(8):
            state[i, 8 + x, 16:48] = f[i, x]
            state[i, x, 16:48] = x_low[i * 8 + x]
            state[i, 16 + x, 16:48] = x_high[i * 8 + x]
            state[i, 8 + x, 8:16] = y_low[i * 8 + x]
            state[i, 8 + x, 48:56] = y_high[i * 8 + x]
        for j in range(6):
            for first, e in ((2, e_low), (16, e_high)):
                state[i, first + j, 8:16] = e[(i * 6 + j) * 2]
                state[i, first + j, 48:56] = e[(i * 6 + j) * 2 + 1]
    for a in range(3):
        for x in range(8):
            wind[a, 8 + x, 16:48] = v[a, x] * scale
            wind[a, 8 + x, 8:16] = y_low[32 + a * 8 + x] * scale
            wind[a, 8 + x, 48:56] = y_high[32 + a * 8 + x] * scale
        for j in range(6):
            wind[a, 2 + j, 16:48] = x_low[32 + a * 6 + j] * scale
            wind[a, 16 + j, 16:48] = x_high[32 + a * 6 + j] * scale
        for j in range(4):
            for first, e in ((4, e_low), (16, e_high)):
                wind[a, first + j, 8:16] = e[48 + (a * 4 + j) * 2] * scale
                wind[a, first + j, 48:56] = e[48 + (a * 4 + j) * 2 + 1] * scale
    for x in range(8):
        zm[8 + x, 16:48] = z_left[x] + z_right[x]
        zm[8 + x, 8:16] = y_low[56 + x]
        zm[8 + x, 48:56] = y_high[56 + x]
    for j in range(6):
        for first, e in ((2, e_low), (16, e_high)):
            for t in range(4):
                zm[first + j, 16 + 8 * t : 24 + 8 * t] = e[72 + j * 4 + t]
    for j in range(4):
        for first, e in ((4, e_low), (16, e_high)):
            zm[first + j, 8:16] = e[96 + j * 2]
            zm[first + j, 48:56] = e[96 + j * 2 + 1]

    def chunk(rows):
        lane = lanes_of(rows)
        return lane, lane % 32, lax.broadcasted_iota(jnp.int32, (rows, 128), 0)

    def roll(value, by):
        return pltpu.roll(value, by % 128, 1)

    def slabs(x, r, rows, winds):
        lane, in_group, _ = chunk(rows)
        halo = zm[x, r : r + rows]
        tile = halo
        for i in range(4):
            q = state[i, x, r : r + rows]
            tile = jnp.where(within(lane, 32 * i + 8, 8), roll(q, 32 * i + 8), tile)
            tile = jnp.where(within(lane, 32 * i + 16, 8), roll(q, 32 * i + 24), tile)
        edge[x, r : r + rows] = tile
        if winds:
            halo = halo * scale
            packed = jnp.where(in_group < 8, roll(halo, -8), roll(halo, 8))
            for a in range(3):
                q = wind[a, x, r : r + rows]
                packed = jnp.where(within(lane, 32 * a + 8, 8), roll(q, 32 * a + 8), packed)
                packed = jnp.where(within(lane, 32 * a + 16, 8), roll(q, 32 * a + 24), packed)
            for a in range(3):
                one = jnp.where(within(lane, 32 * a, 32), packed, 0.0)
                one = one + roll(one, 32)
                edge_wind[a, x, r : r + rows] = one + roll(one, 64)

    @pl.loop(4, 20)
    def _(x):
        for r in (8, 24, 40):
            slabs(x, r, 16, True)

    @pl.loop(0, 4)
    def _(j):
        x = jnp.where(j < 2, 2 + j, 18 + j)
        for r in (16, 32):
            slabs(x, r, 16, False)

    dd = [d[i] * TIME_STEP for i in range(4)]
    cc = [[c[i, w] * TIME_STEP for w in range(4)] for i in range(4)]

    def terms(plus, minus, plus2, minus2):
        return 8.0 * (plus - minus) - (plus2 - minus2), plus + minus

    def tendencies(src, slab, x, r, rows):
        lane, in_group, _ = chunk(rows)
        at = slice(r, r + rows)
        u = [wind[a, x, at] for a in range(3)]
        q = [src[i, x, at] for i in range(4)]
        s = slab[x, at]
        s = jnp.where(in_group >= 24, s, roll(s, 16))
        results = []
        for i in range(4):
            ends = roll(s, -24 - 32 * i)
            gz_, lz = terms(
                roll(jnp.where(lane == 0, ends, q[i]), -1),
                roll(jnp.where(lane == 127, ends, q[i]), 1),
                roll(jnp.where(lane < 2, ends, q[i]), -2),
                roll(jnp.where(lane >= 126, ends, q[i]), 2),
            )
            gx_, lx = terms(src[i, x + 1, at], src[i, x - 1, at], src[i, x + 2, at], src[i, x - 2, at])
            gy_, ly = terms(*(src[i, x, r + o : r + o + rows] for o in (1, -1, 2, -2)))
            mix = cc[i][0] * q[0] + cc[i][1] * q[1] + (cc[i][2] * q[2] + cc[i][3] * q[3])
            moved = u[0] * gx_ + u[1] * gy_ + u[2] * gz_
            results.append(dd[i] * (lx + ly + lz) - moved + q[i] * (mix - 6.0 * dd[i]))
        return q, results

    def slab_tendency(slab, x, r, rows):
        lane, _, _ = chunk(rows)
        group = lane // 32
        at = slice(r, r + rows)

        def by_group(values):
            return jnp.where(group < 2, jnp.where(group == 0, values[0], values[1]),
                             jnp.where(group == 2, values[2], values[3]))

        q = slab[x, at]
        gz_, lz = terms(roll(q, -1), roll(q, 1), roll(q, -2), roll(q, 2))
        gx_, lx = terms(slab[x + 1, at], slab[x - 1, at], slab[x + 2, at], slab[x - 2, at])
        gy_, ly = terms(*(slab[x, r + o : r + o + rows] for o in (1, -1, 2, -2)))
        mix = -6.0 * by_group(dd)
        for k in range(4):
            mix = mix + by_group([cc[i][(i - k) % 4] for i in range(4)]) * roll(q, 32 * k)
        moved = edge_wind[0, x, at] * gx_ + edge_wind[1, x, at] * gy_ + edge_wind[2, x, at] * gz_
        return q, by_group(dd) * (lx + ly + lz) - moved + q * mix

    def inside(x, r, rows):
        _, in_group, row = chunk(rows)
        first = jnp.where((x >= x_first) & (x < x_end), y_first, ROWS)
        ok = (row + r >= first) & (row + r < y_end)
        z_ok = ((in_group >= 8) | (gz != 0)) & ((in_group < 24) | (gz != last_z))
        return ok, z_ok

    def half(base, q, t):
        return 0.5 * (base + q + t)

    def stage(x, rows_at, slab_rows, src, slab, dst, slab_dst, mean):
        for r in rows_at:
            at = slice(r, r + 16)
            ok, _ = inside(x, r, 16)
            q, t = tendencies(src, slab, x, r, 16)
            for i in range(4):
                new = half(dst[i, x, at], q[i], t[i]) if mean else q[i] + t[i]
                dst[i, x, at] = jnp.where(ok, new, 0.0)
        for r in slab_rows:
            at = slice(r, r + 16)
            ok, z_ok = inside(x, r, 16)
            q, t = slab_tendency(slab, x, r, 16)
            new = half(slab_dst[x, at], q, t) if mean else q + t
            slab_dst[x, at] = jnp.where(ok & z_ok, new, 0.0)

    full, own = (8, 24, 40), (16, 32)

    @pl.loop(4, 20)
    def _(x):
        stage(x, full, full, state, edge, section, edge2, False)

    @pl.loop(0, 4)
    def _(j):
        stage(jnp.where(j < 2, 2 + j, 18 + j), own, (), state, edge, section, edge2, False)

    @pl.loop(6, 18)
    def _(x):
        stage(x, full, full, section, edge2, state, edge, True)

    @pl.loop(0, 4)
    def _(j):
        stage(jnp.where(j < 2, 4 + j, 16 + j), own, (), section, edge2, state, edge, True)

    @pl.loop(8, 16)
    def _(x):
        stage(x, full, own, state, edge, section, edge2, False)

    @pl.loop(0, 4)
    def _(j):
        stage(jnp.where(j < 2, 6 + j, 14 + j), own, (), state, edge, section, edge2, False)

    @pl.loop(0, 8)
    def _(x):
        for r in own:
            q, t = tendencies(section, edge2, 8 + x, r, 16)
            for i in range(4):
                row = pl.multiple_of(x * 32 + (r - 16), 16)
                final[i, pl.ds(row, 16)] = half(state[i, 8 + x, r : r + 16], q[i], t[i])

    total = jnp.dot(final[0], rhs[0], precision=HIGHEST, preferred_element_type=F32)
    for i in range(1, 4):
        total = total + jnp.dot(final[i], rhs[i], precision=HIGHEST, preferred_element_type=F32)
    for x in range(8):
        mixed[x * 32 : x * 32 + 32] = jnp.dot(
            fy[...], total[x * 32 : x * 32 + 32], precision=HIGHEST, preferred_element_type=F32
        )
    lane = lanes_of(8)
    for j in range(8):
        tiles = [mixed[pl.ds(4 * j + b, 8, stride=32), :] for b in range(4)]
        for k in range(4):
            tile = jnp.zeros((8, 128), F32)
            for b in range(4):
                tile = jnp.where(within(lane, 32 * b, 32), roll(tiles[b], 32 * (b - k)), tile)
            out[j * 4 + k] = tile


def contract_x(parts, fx, out):
    total = parts[0]
    for p in range(1, parts.shape[0]):
        total = total + parts[p]
    out[...] = jnp.dot(fx[...], total, precision=HIGHEST, preferred_element_type=F32)


def local(fields, velocity, diffusivity, coupling, factor_x, factor_y, factor_z):
    def both_ways(axis, up, down):
        pairs = [(i, i + 1) for i in range(lax.axis_size(axis) - 1)]
        return (
            lax.ppermute(up, axis, pairs),
            lax.ppermute(down, axis, [(b, a) for a, b in pairs]),
        )

    x_up, x_down, z_up, z_down = call(
        pack_xz, [f32(50, 32, 128)] * 2 + [f32(8, 32, 128)] * 2, [vmem()] * 2, "pack_xz"
    )(fields, velocity)
    x_low, x_high = both_ways("gx", x_up, x_down)
    z_left, z_right = both_ways("gz", z_up, z_down)
    y_up, y_down = call(pack_y, [f32(64, 8, 128)] * 2, [vmem()] * 4, "pack_y")(
        fields, velocity, z_left, z_right
    )
    y_low, y_high = both_ways("gy", y_up, y_down)
    e_up, e_down = call(pack_x2, [f32(104, 8, 128)] * 2, [vmem()] * 4, "pack_x2")(
        z_left, z_right, y_low, y_high
    )
    e_low, e_high = both_ways("gx", e_up, e_down)
    rhs = call(spread_factor, f32(4, 128, 128), [vmem()], "spread_factor")(factor_z)

    def tiles(*lead):
        return pltpu.VMEM((*lead, ROWS, 128), F32)

    gy, gz, gx = (lax.axis_size(n) for n in ("gy", "gz", "gx"))
    parts = call(
        advance,
        f32(32, 8, 128),
        [smem()] * 2 + [vmem()] * 12,
        "advance",
        scratch=[
            tiles(4, PLANES), tiles(4, PLANES), tiles(PLANES), tiles(PLANES),
            tiles(3, PLANES), tiles(3, PLANES), tiles(PLANES),
            pltpu.VMEM((4, 256, 128), F32), pltpu.VMEM((256, 128), F32),
        ],
        work=10000000,
    )(
        diffusivity, coupling, fields, velocity, z_left, z_right, x_low, x_high, y_low, y_high,
        e_low, e_high, rhs, factor_y.T,
    )
    parts = lax.all_to_all(parts, ("gy", "gz"), 0, 0, tiled=True)
    slices = call(contract_x, f32(32, 128), [vmem()] * 2, "contract_x")(parts, factor_x.T)
    slices = lax.all_to_all(slices, "gx", 0, 0, tiled=True)
    core = jnp.sum(slices.reshape(gx, 32 // gx, 4, 4, 8), axis=0)
    return core.transpose(2, 0, 1, 3)


def solution(mesh):
    return jax.shard_map(
        local,
        mesh=mesh,
        in_specs=(
            P(None, "gx", "gy", "gz"),
            P(None, "gx", "gy", "gz"),
            P(),
            P(),
            P("gx", None),
            P("gy", None),
            P("gz", None),
        ),
        out_specs=P(None, "gx", "gy", "gz"),
        check_vma=False,
    )
```

time: 197 us -> 130 us (0.66)
  Pallas kernels: 0 us -> 38.8 us
  starting transfers between devices: 74.8 us -> 40.9 us
  blocking collectives: 45.7 us -> 21.5 us
  waiting for transfers between devices: 38.9 us -> 21.9 us
  other arithmetic: 14.4 us -> 0.03 us
  matrix products: 13.5 us -> 0 us
    ppermute x24 -> x8, starting transfers between devices: 74.8 us -> 26.4 us  [the longest x4 20.6 us: both_ways(): lax.ppermute(up, axis, pairs)]
    pallas_call x0 -> x6, Pallas kernels: none -> 38.8 us  [the longest x1 27.7 us: local(): call(advance, f32(32, 8, 128), [smem()] * 2 + [vmem()] * 12, 'advance', s...]
    ppermute x24 -> x8, waiting for transfers between devices: 38.9 us -> 12.1 us  [the longest x4 9.67 us: both_ways(): lax.ppermute(down, axis, [(b, a) for a, b in pairs])]
    all_to_all x3 -> x1, blocking collectives: 45.7 us -> 21.5 us  [local(): slices = lax.all_to_all(slices, 'gx', 0, 0, tiled=True)]
    all_to_all x0 -> x1, starting transfers between devices: none -> 14.5 us  [local(): parts = lax.all_to_all(parts, ('gy', 'gz'), 0, 0, tiled=True)]
    dot_general x7 -> x0, matrix products: 13.5 us -> none  [the longest x4 10.5 us: tendency(): jnp.einsum('vw,wxyz->vxyz', coupling, center, precision=lax.Precision.HIG...]
    concatenate x7 -> x0, other arithmetic: 11.8 us -> none  [padded_2(): jnp.concatenate([jnp.pad(low, around), shard, jnp.pad(high, around)], axi...]
    all_to_all x0 -> x1, waiting for transfers between devices: none -> 9.73 us  [local(): parts = lax.all_to_all(parts, ('gy', 'gz'), 0, 0, tiled=True)]
  transfers between devices with their start and end apart: 24 -> 9, of which waited for: 7 -> 5; matrix products, arithmetic and copies ran while one was open for 2% -> 2% of each run, Pallas kernels for 0% -> 5%
where the time goes in v1:
time: 130 us; the launch traced here: 129 us
  starting transfers between devices  40.9 us (31%)
  Pallas kernels  38.8 us (30%)
  waiting for transfers between devices  21.9 us (17%)
  blocking collectives  21.5 us (17%)
  local copies, waits for them, and re-layouts  6.22 us (5%)
    pallas_call x1, Pallas kernels, local(): call(advance, f32(32, 8, 128), [smem()] * 2 + [vmem()] * 12, 'advance', s...  27.7 us
    all_to_all x1, blocking collectives, local(): slices = lax.all_to_all(slices, 'gx', 0, 0, tiled=True)  21.5 us
    ppermute x4, starting transfers between devices, both_ways(): lax.ppermute(up, axis, pairs)  20.6 us
    all_to_all x1, starting transfers between devices, local(): parts = lax.all_to_all(parts, ('gy', 'gz'), 0, 0, tiled=True)  14.5 us
    all_to_all x1, waiting for transfers between devices, local(): parts = lax.all_to_all(parts, ('gy', 'gz'), 0, 0, tiled=True)  9.73 us
    ppermute x4, waiting for transfers between devices, both_ways(): lax.ppermute(down, axis, [(b, a) for a, b in pairs])  9.67 us
    ppermute x4, starting transfers between devices, both_ways(): lax.ppermute(down, axis, [(b, a) for a, b in pairs])  5.8 us
    unnamed x27, local copies, waits for them, and re-layouts  5.51 us
  transfers between devices with their start and end apart: 9, of which 5 were waited for; matrix products, arithmetic and copies ran while one was open for 2% of the time, Pallas kernels for 5%

profile of v1, /device:TPU:1, one launch (start us, length us, event | category | flops | bytes accessed | tf_op | source)
XLA Modules:
  0.0 129.5 jit_solution(15999193851729661785)
XLA Ops:
  0.0 3.3 %pack_xz.1 = (f32[50,32,128]{2,1,0:T(8,128)}, f32[50,32,128]{2,1,0:T(8,128)}, f32[8,32,128]{2,1,0:T(8,128)}, f32[8,32,128]{2,1,0:T(8,128)}) custom-call(f32[4,8,32,128]{3,2,1,0:T(8,128)} %f.5, f32[3,8,32,128]{3,2,1,0:T(8,128)} %v.5), custom_call_target="tpu_custom_call" | custom-call | flops 1000000 | bytes 1000000 | tf_op jit(solution)/shard_map/pack_xz/pallas_call | solution.py:340
  3.3 3.9 %collective-permute-start = (f32[8,32,128]{2,1,0:T(8,128)}, f32[8,32,128]{2,1,0:T(8,128)S(1)}, u32[]{:S(2)}, u32[]{:S(2)}) collective-permute-start(f32[8,32,128]{2,1,0:T(8,128)} %get-tuple-element.13), channel_id=1, source_target_pairs={{0,1},{1,2},{2,3},{4,5},{5,6},{6,7},{8,9},{9,10},{10,11},{12,13},{... | collective-permute-start | bytes 393224 | tf_op jit(solution)/shard_map/ppermute | solution.py:336
  7.3 1.3 collective-permute-start.1
  8.6 4.0 %collective-permute-start.2 = (f32[50,32,128]{2,1,0:T(8,128)}, f32[50,32,128]{2,1,0:T(8,128)S(1)}, u32[]{:S(2)}, u32[]{:S(2)}) collective-permute-start(f32[50,32,128]{2,1,0:T(8,128)} %get-tuple-element.15), channel_id=1, source_target_pairs={{0,32},{32,64},{64,96},{96,128},{128,160},{160,192},{192,224},{224... | collective-permute-start | bytes 2457608 | tf_op jit(solution)/shard_map/ppermute | solution.py:336
  12.6 1.3 collective-permute-start.3
  15.2 2.1 %pack_y.1 = (f32[64,8,128]{2,1,0:T(8,128)}, f32[64,8,128]{2,1,0:T(8,128)}) custom-call(f32[4,8,32,128]{3,2,1,0:T(8,128)} %f.5, f32[3,8,32,128]{3,2,1,0:T(8,128)} %v.5, f32[8,32,128]{2,1,0:T(8,128)} %copy-done, f32[8,32,128]{2,1,0:T(8,128)} %copy-done.1), custom_call_target="tpu_custom_call" | custom-call | flops 1000000 | bytes 1000000 | tf_op jit(solution)/shard_map/pack_y/pallas_call | solution.py:345
  17.3 5.3 %collective-permute-start.4 = (f32[64,8,128]{2,1,0:T(8,128)}, f32[64,8,128]{2,1,0:T(8,128)S(1)}, u32[]{:S(2)}, u32[]{:S(2)}) collective-permute-start(f32[64,8,128]{2,1,0:T(8,128)} %get-tuple-element.17), channel_id=1, source_target_pairs={{0,4},{4,8},{8,12},{12,16},{16,20},{20,24},{24,28},{1,5},{5,9},{9,... | collective-permute-start | bytes 786440 | tf_op jit(solution)/shard_map/ppermute | solution.py:336
  22.6 1.9 %collective-permute-start.5 = (f32[64,8,128]{2,1,0:T(8,128)}, f32[64,8,128]{2,1,0:T(8,128)S(1)}, u32[]{:S(2)}, u32[]{:S(2)}) collective-permute-start(f32[64,8,128]{2,1,0:T(8,128)} %get-tuple-element.18), channel_id=1, source_target_pairs={{4,0},{8,4},{12,8},{16,12},{20,16},{24,20},{28,24},{5,1},{9,5},{13... | collective-permute-start | bytes 786440 | tf_op jit(solution)/shard_map/ppermute | solution.py:337
  24.6 1.7 %collective-permute-done.4.y_low = f32[64,8,128]{2,1,0:T(8,128)S(1)} collective-permute-done((f32[64,8,128]{2,1,0:T(8,128)}, f32[64,8,128]{2,1,0:T(8,128)S(1)}, u32[]{:S(2)}, u32[]{:S(2)}) %collective-permute-start.4) | collective-permute-done | bytes 262176 | tf_op jit(solution)/shard_map/ppermute | solution.py:336
  26.2 5.3 %collective-permute-done.5.y_high = f32[64,8,128]{2,1,0:T(8,128)S(1)} collective-permute-done((f32[64,8,128]{2,1,0:T(8,128)}, f32[64,8,128]{2,1,0:T(8,128)S(1)}, u32[]{:S(2)}, u32[]{:S(2)}) %collective-permute-start.5) | collective-permute-done | bytes 262176 | tf_op jit(solution)/shard_map/ppermute | solution.py:337
  31.6 0.7 copy-done.3
  32.3 2.1 %pack_x2.1 = (f32[104,8,128]{2,1,0:T(8,128)}, f32[104,8,128]{2,1,0:T(8,128)}) custom-call(f32[8,32,128]{2,1,0:T(8,128)} %copy-done, f32[8,32,128]{2,1,0:T(8,128)} %copy-done.1, f32[64,8,128]{2,1,0:T(8,128)} %copy-done.2, f32[64,8,128]{2,1,0:T(8,128)} %copy-done.3), custom_call_target="tpu_custom_call" | custom-call | flops 1000000 | bytes 1000000 | tf_op jit(solution)/shard_map/pack_x2/pallas_call | solution.py:349
  34.4 7.3 %collective-permute-start.6 = (f32[104,8,128]{2,1,0:T(8,128)}, f32[104,8,128]{2,1,0:T(8,128)S(1)}, u32[]{:S(2)}, u32[]{:S(2)}) collective-permute-start(f32[104,8,128]{2,1,0:T(8,128)} %get-tuple-element.19), channel_id=1, source_target_pairs={{0,32},{32,64},{64,96},{96,128},{128,160},{160,192},{192,224},{224... | collective-permute-start | bytes 1277960 | tf_op jit(solution)/shard_map/ppermute | solution.py:336
  41.7 1.3 collective-permute-start.7
  43.0 0.7 copy.11.fz
  44.4 1.8 %spread_factor.1.rhs = f32[4,128,128]{2,1,0:T(8,128)} custom-call(f32[128,32]{1,0:T(8,128)} %copy.11.fz), custom_call_target="tpu_custom_call" | custom-call | flops 1000000 | bytes 1000000 | tf_op jit(solution)/shard_map/spread_factor/pallas_call | solution.py:353
  46.3 0.8 collective-permute-done.6.e_low
  47.1 4.4 %collective-permute-done.7.e_high = f32[104,8,128]{2,1,0:T(8,128)S(1)} collective-permute-done((f32[104,8,128]{2,1,0:T(8,128)}, f32[104,8,128]{2,1,0:T(8,128)S(1)}, u32[]{:S(2)}, u32[]{:S(2)}) %collective-permute-start.7) | collective-permute-done | bytes 426016 | tf_op jit(solution)/shard_map/ppermute | solution.py:337
  51.4 0.7 copy-done.8
  52.2 27.7 %advance.1 = f32[32,8,128]{2,1,0:T(8,128)} custom-call(f32[4]{0:T(128)} %d.1, f32[4,4]{1,0:T(4,128)} %c.1, f32[4,8,32,128]{3,2,1,0:T(8,128)} %f.5, f32[3,8,32,128]{3,2,1,0:T(8,128)} %v.5, f32[8,32,128]{2,1,0:T(8,128)} %copy-done, f32[8,32,128]{2,1,0:T(8,128)} %copy-done.1, f32[50,32,128]{2,1,0:T(8,128)} %copy-done.4, f32[50,32,128]{2,1,0:T(8,128)} %copy-done.5, ...), custom_call_target="tpu_custom_call" | custom-call | flops 10000000 | bytes 10000000 | tf_op jit(solution)/shard_map/advance/pallas_call | solution.py:359
  79.9 14.5 %all-to-all-start = ((f32[32,8,128]{2,1,0:T(8,128)}), f32[32,8,128]{2,1,0:T(8,128)S(1)}, u32[]{:S(2)}, u32[]{:S(2)}) async-start(f32[32,8,128]{2,1,0:T(8,128)} %advance.1), calls=%async_computation | async-start | bytes 262144 | tf_op jit(solution)/shard_map/all_to_all | solution.py:374
  95.2 9.7 %all-to-all-done.parts = f32[32,8,128]{2,1,0:T(8,128)S(1)} async-done(((f32[32,8,128]{2,1,0:T(8,128)}), f32[32,8,128]{2,1,0:T(8,128)S(1)}, u32[]{:S(2)}, u32[]{:S(2)}) %all-to-all-start) | async-done | bytes 131104 | tf_op jit(solution)/shard_map/all_to_all | solution.py:374
  105.5 1.7 %contract_x.1 = f32[32,128]{1,0:T(8,128)} custom-call(f32[32,8,128]{2,1,0:T(8,128)} %copy-done.6, f32[32,8]{1,0:T(8,128)} %bitcast.5), custom_call_target="tpu_custom_call" | custom-call | flops 1000000 | bytes 1000000 | tf_op jit(solution)/shard_map/contract_x/pallas_call | solution.py:375
  107.2 21.5 %all_to_all.14 = f32[16,2,128]{2,1,0:T(2,128)S(1)} all-to-all(f32[16,2,128]{2,1,0:T(2,128)} %bitcast.6), channel_id=1, replica_groups=mesh['gx'=16,'gy'=8,'gz'=4] {'gx'}, dimensions={0} | all-to-all | bytes 32768 | tf_op jit(solution)/shard_map/all_to_all | solution.py:376
  (31 shorter events, 4.1 us)
Async XLA Ops:
  3.3 10.6 %collective-permute-start = (f32[8,32,128]{2,1,0:T(8,128)}, f32[8,32,128]{2,1,0:T(8,128)S(1)}, u32[]{:S(2)}, u32[]{:S(2)}) collective-permute-start(f32[8,32,128]{2,1,0:T(8,128)} %get-tuple-element.13), channel_id=1, source_target_pairs={{0,1},{1,2},{2,3},{4,5},{5,6},{6,7},{8,9},{9,10},{10,11},{12,13},{... | collective-permute-start | bytes 393224 | tf_op jit(solution)/shard_map/ppermute | solution.py:336
  7.3 6.7 %collective-permute-start.1 = (f32[8,32,128]{2,1,0:T(8,128)}, f32[8,32,128]{2,1,0:T(8,128)S(1)}, u32[]{:S(2)}, u32[]{:S(2)}) collective-permute-start(f32[8,32,128]{2,1,0:T(8,128)} %get-tuple-element.14), channel_id=1, source_target_pairs={{1,0},{2,1},{3,2},{5,4},{6,5},{7,6},{9,8},{10,9},{11,10},{13,12},{... | collective-permute-start | bytes 393224 | tf_op jit(solution)/shard_map/ppermute | solution.py:337
  8.6 37.7 %collective-permute-start.2 = (f32[50,32,128]{2,1,0:T(8,128)}, f32[50,32,128]{2,1,0:T(8,128)S(1)}, u32[]{:S(2)}, u32[]{:S(2)}) collective-permute-start(f32[50,32,128]{2,1,0:T(8,128)} %get-tuple-element.15), channel_id=1, source_target_pairs={{0,32},{32,64},{64,96},{96,128},{128,160},{160,192},{192,224},{224... | collective-permute-start | bytes 2457608 | tf_op jit(solution)/shard_map/ppermute | solution.py:336
  12.6 33.6 %collective-permute-start.3 = (f32[50,32,128]{2,1,0:T(8,128)}, f32[50,32,128]{2,1,0:T(8,128)S(1)}, u32[]{:S(2)}, u32[]{:S(2)}) collective-permute-start(f32[50,32,128]{2,1,0:T(8,128)} %get-tuple-element.16), channel_id=1, source_target_pairs={{32,0},{64,32},{96,64},{128,96},{160,128},{192,160},{224,192},{256... | collective-permute-start | bytes 2457608 | tf_op jit(solution)/shard_map/ppermute | solution.py:337
  13.9 0.6 copy-start
  14.6 0.6 copy-start.1
  17.3 8.9 %collective-permute-start.4 = (f32[64,8,128]{2,1,0:T(8,128)}, f32[64,8,128]{2,1,0:T(8,128)S(1)}, u32[]{:S(2)}, u32[]{:S(2)}) collective-permute-start(f32[64,8,128]{2,1,0:T(8,128)} %get-tuple-element.17), channel_id=1, source_target_pairs={{0,4},{4,8},{8,12},{12,16},{16,20},{20,24},{24,28},{1,5},{5,9},{9,... | collective-permute-start | bytes 786440 | tf_op jit(solution)/shard_map/ppermute | solution.py:336
  22.6 20.4 %copy-start.9 = (f32[128,32]{0,1:T(8,128)S(1)}, f32[128,32]{0,1:T(8,128)}, u32[]{:S(2)}) copy-start(f32[128,32]{0,1:T(8,128)} %param.13) | copy-start | bytes 49156
  22.6 8.9 %collective-permute-start.5 = (f32[64,8,128]{2,1,0:T(8,128)}, f32[64,8,128]{2,1,0:T(8,128)S(1)}, u32[]{:S(2)}, u32[]{:S(2)}) collective-permute-start(f32[64,8,128]{2,1,0:T(8,128)} %get-tuple-element.18), channel_id=1, source_target_pairs={{4,0},{8,4},{12,8},{16,12},{20,16},{24,20},{28,24},{5,1},{9,5},{13... | collective-permute-start | bytes 786440 | tf_op jit(solution)/shard_map/ppermute | solution.py:337
  26.2 5.3 %copy-start.2 = (f32[64,8,128]{2,1,0:T(8,128)}, f32[64,8,128]{2,1,0:T(8,128)S(1)}, u32[]{:S(2)}) copy-start(f32[64,8,128]{2,1,0:T(8,128)S(1)} %collective-permute-done.4.y_low) | copy-start | bytes 786436
  31.6 0.7 copy-start.3
  34.4 12.7 %collective-permute-start.6 = (f32[104,8,128]{2,1,0:T(8,128)}, f32[104,8,128]{2,1,0:T(8,128)S(1)}, u32[]{:S(2)}, u32[]{:S(2)}) collective-permute-start(f32[104,8,128]{2,1,0:T(8,128)} %get-tuple-element.19), channel_id=1, source_target_pairs={{0,32},{32,64},{64,96},{96,128},{128,160},{160,192},{192,224},{224... | collective-permute-start | bytes 1277960 | tf_op jit(solution)/shard_map/ppermute | solution.py:336
  41.7 2.0 %copy-start.10 = (f32[32,32]{1,0:T(8,128)S(1)}, f32[32,32]{1,0:T(8,128)}, u32[]{:S(2)}) copy-start(f32[32,32]{1,0:T(8,128)} %param.12) | copy-start | bytes 12292
  41.7 9.7 %collective-permute-start.7 = (f32[104,8,128]{2,1,0:T(8,128)}, f32[104,8,128]{2,1,0:T(8,128)S(1)}, u32[]{:S(2)}, u32[]{:S(2)}) collective-permute-start(f32[104,8,128]{2,1,0:T(8,128)} %get-tuple-element.20), channel_id=1, source_target_pairs={{32,0},{64,32},{96,64},{128,96},{160,128},{192,160},{224,192},{256... | collective-permute-start | bytes 1277960 | tf_op jit(solution)/shard_map/ppermute | solution.py:337
  46.2 5.2 %copy-start.4 = (f32[50,32,128]{2,1,0:T(8,128)}, f32[50,32,128]{2,1,0:T(8,128)S(1)}, u32[]{:S(2)}) copy-start(f32[50,32,128]{2,1,0:T(8,128)S(1)} %collective-permute-done.2.x_low) | copy-start | bytes 2457604
  46.3 5.2 %copy-start.5 = (f32[50,32,128]{2,1,0:T(8,128)}, f32[50,32,128]{2,1,0:T(8,128)S(1)}, u32[]{:S(2)}) copy-start(f32[50,32,128]{2,1,0:T(8,128)S(1)} %collective-permute-done.3.x_high) | copy-start | bytes 2457604
  47.1 4.4 %copy-start.7 = (f32[104,8,128]{2,1,0:T(8,128)}, f32[104,8,128]{2,1,0:T(8,128)S(1)}, u32[]{:S(2)}) copy-start(f32[104,8,128]{2,1,0:T(8,128)S(1)} %collective-permute-done.6.e_low) | copy-start | bytes 1277956
  51.4 0.8 copy-start.8
  79.9 14.6 %copy-start.11 = (f32[8,32]{1,0:T(8,128)S(1)}, f32[8,32]{1,0:T(8,128)}, u32[]{:S(2)}) copy-start(f32[8,32]{1,0:T(8,128)} %param.11) | copy-start | bytes 3076
  79.9 25.0 %all-to-all-start = ((f32[32,8,128]{2,1,0:T(8,128)}), f32[32,8,128]{2,1,0:T(8,128)S(1)}, u32[]{:S(2)}, u32[]{:S(2)}) async-start(f32[32,8,128]{2,1,0:T(8,128)} %advance.1), calls=%async_computation | async-start | bytes 262144 | tf_op jit(solution)/shard_map/all_to_all | solution.py:374
  104.9 0.6 copy-start.6

commit v2 on v1

--- a/solution.py
+++ b/solution.py
@@ -24,7 +24,7 @@
     return jax.ShapeDtypeStruct(shape, F32)
 
 
-def call(kernel, out_shape, in_specs, name, scratch=(), work=1000000):
+def call(kernel, out_shape, in_specs, name, scratch=(), work=1000000, mib=8):
     many = isinstance(out_shape, (list, tuple))
     return pl.pallas_call(
         kernel,
@@ -32,6 +32,7 @@
         in_specs=in_specs,
         out_specs=[vmem() for _ in out_shape] if many else vmem(),
         scratch_shapes=list(scratch),
+        compiler_params=pltpu.CompilerParams(vmem_limit_bytes=mib << 20),
         cost_estimate=pl.CostEstimate(flops=work, bytes_accessed=work, transcendentals=0),
         name=name,
     )
@@ -43,6 +44,12 @@
 
 def within(lane, first, size):
     return (lane >= first) & (lane < first + size)
+
+
+def dot(a, b, a_dim, b_dim):
+    return lax.dot_general(
+        a, b, (((a_dim,), (b_dim,)), ((), ())), precision=HIGHEST, preferred_element_type=F32
+    )
 
 
 def pack_xz(f, v, x_up, x_down, z_up, z_down):
@@ -102,20 +109,9 @@
                 out[72 + j * 4 + t] = halo[8 * t : 8 * t + 8]
 
 
-def spread_factor(fz, out):
-    lane = lanes_of(128)
-    wide = jnp.concatenate([fz[...], jnp.zeros((128, 96), F32)], axis=1)
-    for v in range(4):
-        placed = jnp.zeros((128, 128), F32)
-        for k in range(4):
-            rolled = pltpu.roll(wide, (24 * k + 8 * v) % 128, 1)
-            placed = jnp.where(within(lane, 32 * k + 8 * v, 8), rolled, placed)
-        out[v] = placed
-
-
 def advance(
-    d, c, f, v, z_left, z_right, x_low, x_high, y_low, y_high, e_low, e_high, rhs, fy,
-    out, state, section, edge, edge2, wind, edge_wind, zm, final, mixed,
+    d, c, f, v, z_left, z_right, x_low, x_high, y_low, y_high, e_low, e_high, fz, fy,
+    out, state, section, edge, edge2, wind, edge_wind, zm, final, mixed, rhs,
 ):
     gx, gy, gz = (lax.axis_index(n) for n in ("gx", "gy", "gz"))
     last_x, last_y, last_z = (lax.axis_size(n) - 1 for n in ("gx", "gy", "gz"))
@@ -305,13 +301,15 @@
                 row = pl.multiple_of(x * 32 + (r - 16), 16)
                 final[i, pl.ds(row, 16)] = half(state[i, 8 + x, r : r + 16], q[i], t[i])
 
-    total = jnp.dot(final[0], rhs[0], precision=HIGHEST, preferred_element_type=F32)
+    rhs[...] = jnp.zeros((4, 128, 128), F32)
+    for i in range(4):
+        for k in range(4):
+            rhs[i, 32 * k + 8 * i : 32 * k + 8 * i + 8] = fz[8 * k : 8 * k + 8]
+    total = dot(final[0], rhs[0], 1, 1)
     for i in range(1, 4):
-        total = total + jnp.dot(final[i], rhs[i], precision=HIGHEST, preferred_element_type=F32)
+        total = total + dot(final[i], rhs[i], 1, 1)
     for x in range(8):
-        mixed[x * 32 : x * 32 + 32] = jnp.dot(
-            fy[...], total[x * 32 : x * 32 + 32], precision=HIGHEST, preferred_element_type=F32
-        )
+        mixed[x * 32 : x * 32 + 32] = dot(fy[...], total[x * 32 : x * 32 + 32], 0, 0)
     lane = lanes_of(8)
     for j in range(8):
         tiles = [mixed[pl.ds(4 * j + b, 8, stride=32), :] for b in range(4)]
@@ -326,7 +324,7 @@
     total = parts[0]
     for p in range(1, parts.shape[0]):
         total = total + parts[p]
-    out[...] = jnp.dot(fx[...], total, precision=HIGHEST, preferred_element_type=F32)
+    out[...] = dot(fx[...], total, 0, 0)
 
 
 def local(fields, velocity, diffusivity, coupling, factor_x, factor_y, factor_z):
@@ -350,7 +348,6 @@
         z_left, z_right, y_low, y_high
     )
     e_low, e_high = both_ways("gx", e_up, e_down)
-    rhs = call(spread_factor, f32(4, 128, 128), [vmem()], "spread_factor")(factor_z)
 
     def tiles(*lead):
         return pltpu.VMEM((*lead, ROWS, 128), F32)
@@ -365,14 +362,16 @@
             tiles(4, PLANES), tiles(4, PLANES), tiles(PLANES), tiles(PLANES),
             tiles(3, PLANES), tiles(3, PLANES), tiles(PLANES),
             pltpu.VMEM((4, 256, 128), F32), pltpu.VMEM((256, 128), F32),
+            pltpu.VMEM((4, 128, 128), F32),
         ],
         work=10000000,
+        mib=24,
     )(
         diffusivity, coupling, fields, velocity, z_left, z_right, x_low, x_high, y_low, y_high,
-        e_low, e_high, rhs, factor_y.T,
+        e_low, e_high, factor_z.T, factor_y,
     )
     parts = lax.all_to_all(parts, ("gy", "gz"), 0, 0, tiled=True)
-    slices = call(contract_x, f32(32, 128), [vmem()] * 2, "contract_x")(parts, factor_x.T)
+    slices = call(contract_x, f32(32, 128), [vmem()] * 2, "contract_x")(parts, factor_x)
     slices = lax.all_to_all(slices, "gx", 0, 0, tiled=True)
     core = jnp.sum(slices.reshape(gx, 32 // gx, 4, 4, 8), axis=0)
     return core.transpose(2, 0, 1, 3)

time: 130 us -> 123 us (0.946)
  blocking collectives: 21.5 us -> 51.4 us
  starting transfers between devices: 40.9 us -> 26.9 us
  Pallas kernels: 38.8 us -> 26.7 us
  waiting for transfers between devices: 21.9 us -> 14.6 us
  local copies, waits for them, and re-layouts: 6.22 us -> 2.79 us
    all_to_all x0 -> x1, blocking collectives: none -> 24.6 us  [local(): parts = lax.all_to_all(parts, ('gy', 'gz'), 0, 0, tiled=True)]
    all_to_all x1 -> x0, starting transfers between devices: 14.5 us -> none  [local(): parts = lax.all_to_all(parts, ('gy', 'gz'), 0, 0, tiled=True)]
    all_to_all x1 -> x0, waiting for transfers between devices: 9.73 us -> none  [local(): parts = lax.all_to_all(parts, ('gy', 'gz'), 0, 0, tiled=True)]
    all_to_all x1, blocking collectives: 21.5 us -> 26.8 us  [local(): slices = lax.all_to_all(slices, 'gx', 0, 0, tiled=True)]
    unnamed x27 -> x18, local copies, waits for them, and re-layouts: 5.51 us -> 2.08 us
    pallas_call x2 -> x1, Pallas kernels: 3.48 us -> 0.2 us  [local(): call(contract_x, f32(32, 128), [vmem()] * 2, 'contract_x')(parts, factor_x)]
    pallas_call x1, Pallas kernels: 27.7 us -> 25.4 us  [local(): call(advance, f32(32, 8, 128), [smem()] * 2 + [vmem()] * 12, 'advance', s...]
    pallas_call x1, Pallas kernels: 3.35 us -> 1.01 us  [local(): call(pack_xz, [f32(50, 32, 128)] * 2 + [f32(8, 32, 128)] * 2, [vmem()] *...]
  transfers between devices with their start and end apart: 9 -> 8, of which waited for: 5 -> 4; matrix products, arithmetic and copies ran while one was open for 2% -> 0% of each run, Pallas kernels for 5% -> 0%
where the time goes in v2:
time: 123 us
  blocking collectives  51.4 us (42%)
  starting transfers between devices  26.9 us (22%)
  Pallas kernels  26.7 us (22%)
  waiting for transfers between devices  14.6 us (12%)
  local copies, waits for them, and re-layouts  2.79 us (2%)
    all_to_all x1, blocking collectives, local(): slices = lax.all_to_all(slices, 'gx', 0, 0, tiled=True)  26.8 us
    pallas_call x1, Pallas kernels, local(): call(advance, f32(32, 8, 128), [smem()] * 2 + [vmem()] * 12, 'advance', s...  25.4 us
    all_to_all x1, blocking collectives, local(): parts = lax.all_to_all(parts, ('gy', 'gz'), 0, 0, tiled=True)  24.6 us
    ppermute x4, starting transfers between devices, both_ways(): lax.ppermute(up, axis, pairs)  20.8 us
    ppermute x4, waiting for transfers between devices, both_ways(): lax.ppermute(down, axis, [(b, a) for a, b in pairs])  9.87 us
    ppermute x4, starting transfers between devices, both_ways(): lax.ppermute(down, axis, [(b, a) for a, b in pairs])  6.12 us
    ppermute x4, waiting for transfers between devices, both_ways(): lax.ppermute(up, axis, pairs)  4.75 us
  transfers between devices with their start and end apart: 8, of which 4 were waited for; matrix products, arithmetic and copies ran while one was open for 0% of the time, Pallas kernels for 0%

profile of v2, /device:TPU:1, one launch (start us, length us, event | category | flops | bytes accessed | tf_op | source)
XLA Modules:
  0.0 122.7 jit_solution(14471328073200706081)
XLA Ops:
  0.0 1.0 copy-done
  1.0 1.0 copy-done.2
  2.0 1.0 pack_xz.1
  3.1 3.9 %collective-permute-start = (f32[8,32,128]{2,1,0:T(8,128)S(1)}, f32[8,32,128]{2,1,0:T(8,128)S(1)}, u32[]{:S(2)}, u32[]{:S(2)}) collective-permute-start(f32[8,32,128]{2,1,0:T(8,128)S(1)} %get-tuple-element.13), channel_id=1, source_target_pairs={{0,1},{1,2},{2,3},{4,5},{5,6},{6,7},{8,9},{9,10},{10,11},{12,13},{... | collective-permute-start | bytes 393224 | tf_op jit(solution)/shard_map/ppermute | solution.py:334
  7.0 1.3 %collective-permute-start.1 = (f32[8,32,128]{2,1,0:T(8,128)S(1)}, f32[8,32,128]{2,1,0:T(8,128)S(1)}, u32[]{:S(2)}, u32[]{:S(2)}) collective-permute-start(f32[8,32,128]{2,1,0:T(8,128)S(1)} %get-tuple-element.14), channel_id=1, source_target_pairs={{1,0},{2,1},{3,2},{5,4},{6,5},{7,6},{9,8},{10,9},{11,10},{13,12},{... | collective-permute-start | bytes 393224 | tf_op jit(solution)/shard_map/ppermute | solution.py:335
  8.3 4.0 %collective-permute-start.2 = (f32[50,32,128]{2,1,0:T(8,128)S(1)}, f32[50,32,128]{2,1,0:T(8,128)S(1)}, u32[]{:S(2)}, u32[]{:S(2)}) collective-permute-start(f32[50,32,128]{2,1,0:T(8,128)S(1)} %get-tuple-element.15), channel_id=1, source_target_pairs={{0,32},{32,64},{64,96},{96,128},{128,160},{160,192},{192,224},{224... | collective-permute-start | bytes 2457608 | tf_op jit(solution)/shard_map/ppermute | solution.py:334
  12.4 1.3 %collective-permute-start.3 = (f32[50,32,128]{2,1,0:T(8,128)S(1)}, f32[50,32,128]{2,1,0:T(8,128)S(1)}, u32[]{:S(2)}, u32[]{:S(2)}) collective-permute-start(f32[50,32,128]{2,1,0:T(8,128)S(1)} %get-tuple-element.16), channel_id=1, source_target_pairs={{32,0},{64,32},{96,64},{128,96},{160,128},{192,160},{224,192},{256... | collective-permute-start | bytes 2457608 | tf_op jit(solution)/shard_map/ppermute | solution.py:335
  13.7 0.1 pack_y.1
  13.8 5.5 %collective-permute-start.4 = (f32[64,8,128]{2,1,0:T(8,128)S(1)}, f32[64,8,128]{2,1,0:T(8,128)S(1)}, u32[]{:S(2)}, u32[]{:S(2)}) collective-permute-start(f32[64,8,128]{2,1,0:T(8,128)S(1)} %get-tuple-element.17), channel_id=1, source_target_pairs={{0,4},{4,8},{8,12},{12,16},{16,20},{20,24},{24,28},{1,5},{5,9},{9,... | collective-permute-start | bytes 786440 | tf_op jit(solution)/shard_map/ppermute | solution.py:334
  19.2 2.2 %collective-permute-start.5 = (f32[64,8,128]{2,1,0:T(8,128)S(1)}, f32[64,8,128]{2,1,0:T(8,128)S(1)}, u32[]{:S(2)}, u32[]{:S(2)}) collective-permute-start(f32[64,8,128]{2,1,0:T(8,128)S(1)} %get-tuple-element.18), channel_id=1, source_target_pairs={{4,0},{8,4},{12,8},{16,12},{20,16},{24,20},{28,24},{5,1},{9,5},{13... | collective-permute-start | bytes 786440 | tf_op jit(solution)/shard_map/ppermute | solution.py:335
  21.5 1.0 collective-permute-done.4.y_low
  22.5 5.4 %collective-permute-done.5.y_high = f32[64,8,128]{2,1,0:T(8,128)S(1)} collective-permute-done((f32[64,8,128]{2,1,0:T(8,128)S(1)}, f32[64,8,128]{2,1,0:T(8,128)S(1)}, u32[]{:S(2)}, u32[]{:S(2)}) %collective-permute-start.5) | collective-permute-done | bytes 262176 | tf_op jit(solution)/shard_map/ppermute | solution.py:335
  27.9 0.1 pack_x2.1
  28.0 0.0 copy-start.7
  28.0 7.3 %collective-permute-start.6 = (f32[104,8,128]{2,1,0:T(8,128)S(1)}, f32[104,8,128]{2,1,0:T(8,128)S(1)}, u32[]{:S(2)}, u32[]{:S(2)}) collective-permute-start(f32[104,8,128]{2,1,0:T(8,128)S(1)} %get-tuple-element.19), channel_id=1, source_target_pairs={{0,32},{32,64},{64,96},{96,128},{128,160},{160,192},{192,224},{224... | collective-permute-start | bytes 1277960 | tf_op jit(solution)/shard_map/ppermute | solution.py:334
  35.4 1.3 %collective-permute-start.7 = (f32[104,8,128]{2,1,0:T(8,128)S(1)}, f32[104,8,128]{2,1,0:T(8,128)S(1)}, u32[]{:S(2)}, u32[]{:S(2)}) collective-permute-start(f32[104,8,128]{2,1,0:T(8,128)S(1)} %get-tuple-element.20), channel_id=1, source_target_pairs={{32,0},{64,32},{96,64},{128,96},{160,128},{192,160},{224,192},{256... | collective-permute-start | bytes 1277960 | tf_op jit(solution)/shard_map/ppermute | solution.py:335
  36.7 3.7 %collective-permute-done.6.e_low = f32[104,8,128]{2,1,0:T(8,128)S(1)} collective-permute-done((f32[104,8,128]{2,1,0:T(8,128)S(1)}, f32[104,8,128]{2,1,0:T(8,128)S(1)}, u32[]{:S(2)}, u32[]{:S(2)}) %collective-permute-start.6) | collective-permute-done | bytes 426016 | tf_op jit(solution)/shard_map/ppermute | solution.py:334
  40.4 4.5 %collective-permute-done.7.e_high = f32[104,8,128]{2,1,0:T(8,128)S(1)} collective-permute-done((f32[104,8,128]{2,1,0:T(8,128)S(1)}, f32[104,8,128]{2,1,0:T(8,128)S(1)}, u32[]{:S(2)}, u32[]{:S(2)}) %collective-permute-start.7) | collective-permute-done | bytes 426016 | tf_op jit(solution)/shard_map/ppermute | solution.py:335
  44.9 25.4 %advance.1 = f32[32,8,128]{2,1,0:T(8,128)S(1)} custom-call(f32[4]{0:T(128)S(1)} %copy-done.8, f32[4,4]{1,0:T(4,128)S(1)} %copy-done.7, f32[4,8,32,128]{3,2,1,0:T(8,128)S(1)} %copy-done.1, f32[3,8,32,128]{3,2,1,0:T(8,128)S(1)} %copy-done.3, f32[8,32,128]{2,1,0:T(8,128)S(1)} %collective-permute-done.z_left, f32[8,32,128]{2,1,0:T(8,128)S(1)} %collective-permute-done.1.z_right, ...), custom_call_target="tpu_custom_call" | custom-call | flops 10000000 | bytes 10000000 | tf_op jit(solution)/shard_map/advance/pallas_call | solution.py:356
  70.3 24.6 %all_to_all.14.parts = f32[32,8,128]{2,1,0:T(8,128)S(1)} all-to-all(f32[32,8,128]{2,1,0:T(8,128)S(1)} %advance.1), channel_id=1, replica_groups=mesh['gx'=16,'gy'=8,'gz'=4] {'gy','gz'}, dimensions={0} | all-to-all | bytes 262144 | tf_op jit(solution)/shard_map/all_to_all | solution.py:373
  94.9 0.2 contract_x.1
  95.1 26.8 %all_to_all.15 = f32[16,2,128]{2,1,0:T(2,128)S(1)} all-to-all(f32[16,2,128]{2,1,0:T(2,128)S(1)} %bitcast.3), channel_id=1, replica_groups=mesh['gx'=16,'gy'=8,'gz'=4] {'gx'}, dimensions={0} | all-to-all | bytes 32768 | tf_op jit(solution)/shard_map/all_to_all | solution.py:375
  122.0 0.1 reduce_sum.12
  122.1 0.6 copy.8
  (20 shorter events, 0.1 us)
Async XLA Ops:
  0.0 1.0 copy-start
  1.0 1.0 copy-start.2
  3.1 10.6 %collective-permute-start = (f32[8,32,128]{2,1,0:T(8,128)S(1)}, f32[8,32,128]{2,1,0:T(8,128)S(1)}, u32[]{:S(2)}, u32[]{:S(2)}) collective-permute-start(f32[8,32,128]{2,1,0:T(8,128)S(1)} %get-tuple-element.13), channel_id=1, source_target_pairs={{0,1},{1,2},{2,3},{4,5},{5,6},{6,7},{8,9},{9,10},{10,11},{12,13},{... | collective-permute-start | bytes 393224 | tf_op jit(solution)/shard_map/ppermute | solution.py:334
  7.0 6.7 %collective-permute-start.1 = (f32[8,32,128]{2,1,0:T(8,128)S(1)}, f32[8,32,128]{2,1,0:T(8,128)S(1)}, u32[]{:S(2)}, u32[]{:S(2)}) collective-permute-start(f32[8,32,128]{2,1,0:T(8,128)S(1)} %get-tuple-element.14), channel_id=1, source_target_pairs={{1,0},{2,1},{3,2},{5,4},{6,5},{7,6},{9,8},{10,9},{11,10},{13,12},{... | collective-permute-start | bytes 393224 | tf_op jit(solution)/shard_map/ppermute | solution.py:335
  8.3 28.3 %collective-permute-start.2 = (f32[50,32,128]{2,1,0:T(8,128)S(1)}, f32[50,32,128]{2,1,0:T(8,128)S(1)}, u32[]{:S(2)}, u32[]{:S(2)}) collective-permute-start(f32[50,32,128]{2,1,0:T(8,128)S(1)} %get-tuple-element.15), channel_id=1, source_target_pairs={{0,32},{32,64},{64,96},{96,128},{128,160},{160,192},{192,224},{224... | collective-permute-start | bytes 2457608 | tf_op jit(solution)/shard_map/ppermute | solution.py:334
  12.4 24.3 %collective-permute-start.3 = (f32[50,32,128]{2,1,0:T(8,128)S(1)}, f32[50,32,128]{2,1,0:T(8,128)S(1)}, u32[]{:S(2)}, u32[]{:S(2)}) collective-permute-start(f32[50,32,128]{2,1,0:T(8,128)S(1)} %get-tuple-element.16), channel_id=1, source_target_pairs={{32,0},{64,32},{96,64},{128,96},{160,128},{192,160},{224,192},{256... | collective-permute-start | bytes 2457608 | tf_op jit(solution)/shard_map/ppermute | solution.py:335
  13.7 31.2 %copy-start.3 = (f32[3,8,32,128]{3,2,1,0:T(8,128)S(1)}, f32[3,8,32,128]{3,2,1,0:T(8,128)}, u32[]{:S(2)}) copy-start(f32[3,8,32,128]{3,2,1,0:T(8,128)} %v.5) | copy-start | bytes 1179652
  13.8 31.1 %copy-start.1 = (f32[4,8,32,128]{3,2,1,0:T(8,128)S(1)}, f32[4,8,32,128]{3,2,1,0:T(8,128)}, u32[]{:S(2)}) copy-start(f32[4,8,32,128]{3,2,1,0:T(8,128)} %f.5) | copy-start | bytes 1572868
  13.8 8.8 %collective-permute-start.4 = (f32[64,8,128]{2,1,0:T(8,128)S(1)}, f32[64,8,128]{2,1,0:T(8,128)S(1)}, u32[]{:S(2)}, u32[]{:S(2)}) collective-permute-start(f32[64,8,128]{2,1,0:T(8,128)S(1)} %get-tuple-element.17), channel_id=1, source_target_pairs={{0,4},{4,8},{8,12},{12,16},{16,20},{20,24},{24,28},{1,5},{5,9},{9,... | collective-permute-start | bytes 786440 | tf_op jit(solution)/shard_map/ppermute | solution.py:334
  19.2 8.7 %collective-permute-start.5 = (f32[64,8,128]{2,1,0:T(8,128)S(1)}, f32[64,8,128]{2,1,0:T(8,128)S(1)}, u32[]{:S(2)}, u32[]{:S(2)}) collective-permute-start(f32[64,8,128]{2,1,0:T(8,128)S(1)} %get-tuple-element.18), channel_id=1, source_target_pairs={{4,0},{8,4},{12,8},{16,12},{20,16},{24,20},{28,24},{5,1},{9,5},{13... | collective-permute-start | bytes 786440 | tf_op jit(solution)/shard_map/ppermute | solution.py:335
  27.9 16.9 %copy-start.4 = (f32[128,32]{0,1:T(8,128)S(1)}, f32[128,32]{0,1:T(8,128)}, u32[]{:S(2)}) copy-start(f32[128,32]{0,1:T(8,128)} %param.13) | copy-start | bytes 49156
  27.9 16.9 %copy-start.5 = (f32[32,32]{1,0:T(8,128)S(1)}, f32[32,32]{1,0:T(8,128)}, u32[]{:S(2)}) copy-start(f32[32,32]{1,0:T(8,128)} %fy.1) | copy-start | bytes 12292
  28.0 16.9 %copy-start.7 = (f32[4,4]{1,0:T(4,128)S(1)}, f32[4,4]{1,0:T(4,128)}, u32[]{:S(2)}) copy-start(f32[4,4]{1,0:T(4,128)} %c.1) | copy-start | bytes 196
  28.0 12.3 %collective-permute-start.6 = (f32[104,8,128]{2,1,0:T(8,128)S(1)}, f32[104,8,128]{2,1,0:T(8,128)S(1)}, u32[]{:S(2)}, u32[]{:S(2)}) collective-permute-start(f32[104,8,128]{2,1,0:T(8,128)S(1)} %get-tuple-element.19), channel_id=1, source_target_pairs={{0,32},{32,64},{64,96},{96,128},{128,160},{160,192},{192,224},{224... | collective-permute-start | bytes 1277960 | tf_op jit(solution)/shard_map/ppermute | solution.py:334
  35.3 9.5 %copy-start.8 = (f32[4]{0:T(128)S(1)}, f32[4]{0:T(128)}, u32[]{:S(2)}) copy-start(f32[4]{0:T(128)} %d.1) | copy-start | bytes 52
  35.4 9.5 %collective-permute-start.7 = (f32[104,8,128]{2,1,0:T(8,128)S(1)}, f32[104,8,128]{2,1,0:T(8,128)S(1)}, u32[]{:S(2)}, u32[]{:S(2)}) collective-permute-start(f32[104,8,128]{2,1,0:T(8,128)S(1)} %get-tuple-element.20), channel_id=1, source_target_pairs={{32,0},{64,32},{96,64},{128,96},{160,128},{192,160},{224,192},{256... | collective-permute-start | bytes 1277960 | tf_op jit(solution)/shard_map/ppermute | solution.py:335
  70.3 24.7 %copy-start.6 = (f32[8,32]{1,0:T(8,128)S(1)}, f32[8,32]{1,0:T(8,128)}, u32[]{:S(2)}) copy-start(f32[8,32]{1,0:T(8,128)} %fx.1) | copy-start | bytes 3076

commit v3 on v2

--- a/solution.py
+++ b/solution.py
@@ -52,17 +52,20 @@
     )
 
 
-def pack_xz(f, v, x_up, x_down, z_up, z_down):
+def padded(rows):
+    return jnp.concatenate([rows, jnp.zeros((rows.shape[0], 128 - rows.shape[1]), F32)], axis=1)
+
+
+def pack_xz(f, v, fz, x_up, x_down, z_up, z_down):
     lane = lanes_of(32)
-    for i in range(4):
-        for x in range(8):
-            plane = f[i, x]
-            x_up[i * 8 + x] = plane
-            x_down[i * 8 + x] = plane
-    for a in range(3):
-        for j in range(6):
-            x_up[32 + a * 6 + j] = v[a, 2 + j]
-            x_down[32 + a * 6 + j] = v[a, j]
+    for j in range(6):
+        for i in range(4):
+            x_up[i * 6 + j] = f[i, 2 + j]
+            x_down[i * 6 + j] = f[i, j]
+    for j in range(4):
+        for a in range(3):
+            x_up[24 + a * 4 + j] = v[a, 4 + j]
+            x_down[24 + a * 4 + j] = v[a, j]
 
     def plane_edges(x, carry):
         up = jnp.zeros((32, 128), F32)
@@ -71,10 +74,10 @@
             plane = f[i, x]
             up = jnp.where(within(lane, 32 * i, 8), pltpu.roll(plane, (32 * i + 8) % 128, 1), up)
             down = jnp.where(within(lane, 32 * i + 24, 8), pltpu.roll(plane, 32 * i + 24, 1), down)
-        for a in range(3):
-            plane = v[a, x]
-            up = jnp.where(within(lane, 32 * a + 8, 8), pltpu.roll(plane, 32 * a + 16, 1), up)
-            down = jnp.where(within(lane, 32 * a + 16, 8), pltpu.roll(plane, 32 * a + 16, 1), down)
+        for a in range(4):
+            plane = pltpu.roll(v[a, x] if a < 3 else fz[...], 32 * a + 16, 1)
+            up = jnp.where(within(lane, 32 * a + 8, 8), plane, up)
+            down = jnp.where(within(lane, 32 * a + 16, 8), plane, down)
         z_up[x] = up
         z_down[x] = down
         return carry
@@ -82,36 +85,45 @@
     lax.fori_loop(0, 8, plane_edges, 0)
 
 
-def pack_y(f, v, z_left, z_right, y_up, y_down):
-    for out, row in ((y_up, 24), (y_down, 0)):
+def pack_y(f, v, fy, z_left, z_right, y_up, y_down):
+    for out, row, row4 in ((y_up, 24, 28), (y_down, 0, 0)):
         for x in range(8):
+            half = slice(4 * (x % 2), 4 * (x % 2) + 4)
             for i in range(4):
                 out[i * 8 + x] = f[i, x, row : row + 8]
             for a in range(3):
-                out[32 + a * 8 + x] = v[a, x, row : row + 8]
-            out[56 + x] = z_left[x, row : row + 8] + z_right[x, row : row + 8]
-
-
-def pack_x2(z_left, z_right, y_low, y_high, up, down):
-    for out, first, first4 in ((up, 2, 4), (down, 0, 0)):
+                out[32 + a * 4 + x // 2, half] = v[a, x, row4 : row4 + 4]
+            out[44 + x // 2, half] = z_left[x, row4 : row4 + 4] + z_right[x, row4 : row4 + 4]
+        out[48] = padded(fy[row : row + 8])
+
+
+def pack_x2(z_left, z_right, y_low, y_high, fx, up, down):
+    for out, near, far, first in ((up, 6, 4, 4), (down, 0, 2, 0)):
         for side, rows in ((0, y_low), (1, y_high)):
-            for i in range(4):
-                for j in range(6):
-                    out[(i * 6 + j) * 2 + side] = rows[i * 8 + first + j]
-            for a in range(3):
-                for j in range(4):
-                    out[48 + (a * 4 + j) * 2 + side] = rows[32 + a * 8 + first4 + j]
-            for j in range(4):
-                out[96 + j * 2 + side] = rows[56 + first4 + j]
-        for j in range(6):
+            four = slice(4, 8) if side == 0 else slice(0, 4)
+            two = slice(6, 8) if side == 0 else slice(0, 2)
+            for j in range(2):
+                for i in range(4):
+                    out[i * 2 + side, 4 * j : 4 * j + 4] = rows[i * 8 + near + j, four]
+                    at = 4 * (i % 2) + 2 * j
+                    out[8 + i // 2 * 2 + side, at : at + 2] = rows[i * 8 + far + j, two]
+                x = near + j
+                at = 4 * (x % 2) + (2 if side == 0 else 0)
+                for a in range(3):
+                    to = 4 * (a % 2) + 2 * j
+                    out[12 + a // 2 * 2 + side, to : to + 2] = rows[32 + a * 4 + x // 2, at : at + 2]
+                to = 4 * side + 2 * j
+                out[32, to : to + 2] = rows[44 + x // 2, at : at + 2]
+        for j in range(4):
             halo = z_left[first + j] + z_right[first + j]
             for t in range(4):
-                out[72 + j * 4 + t] = halo[8 * t : 8 * t + 8]
+                out[16 + j * 4 + t] = halo[8 * t : 8 * t + 8]
+        out[33] = padded(fx[...])
 
 
 def advance(
     d, c, f, v, z_left, z_right, x_low, x_high, y_low, y_high, e_low, e_high, fz, fy,
-    out, state, section, edge, edge2, wind, edge_wind, zm, final, mixed, rhs,
+    out, state, section, edge, edge2, wind, edge_wind, zm, final, faces, mixed, rhs, fye,
 ):
     gx, gy, gz = (lax.axis_index(n) for n in ("gx", "gy", "gz"))
     last_x, last_y, last_z = (lax.axis_size(n) - 1 for n in ("gx", "gy", "gz"))
@@ -122,38 +134,44 @@
     for i in range(4):
         for x in range(8):
             state[i, 8 + x, 16:48] = f[i, x]
-            state[i, x, 16:48] = x_low[i * 8 + x]
-            state[i, 16 + x, 16:48] = x_high[i * 8 + x]
             state[i, 8 + x, 8:16] = y_low[i * 8 + x]
             state[i, 8 + x, 48:56] = y_high[i * 8 + x]
         for j in range(6):
-            for first, e in ((2, e_low), (16, e_high)):
-                state[i, first + j, 8:16] = e[(i * 6 + j) * 2]
-                state[i, first + j, 48:56] = e[(i * 6 + j) * 2 + 1]
+            state[i, 2 + j, 16:48] = x_low[i * 6 + j]
+            state[i, 16 + j, 16:48] = x_high[i * 6 + j]
+        for e, near, far in ((e_low, 6, 4), (e_high, 16, 18)):
+            for j in range(2):
+                state[i, near + j, 12:16] = e[i * 2, 4 * j : 4 * j + 4]
+                state[i, near + j, 48:52] = e[i * 2 + 1, 4 * j : 4 * j + 4]
+                at = 4 * (i % 2) + 2 * j
+                state[i, far + j, 14:16] = e[8 + i // 2 * 2, at : at + 2]
+                state[i, far + j, 48:50] = e[9 + i // 2 * 2, at : at + 2]
     for a in range(3):
         for x in range(8):
+            half_tile = slice(4 * (x % 2), 4 * (x % 2) + 4)
             wind[a, 8 + x, 16:48] = v[a, x] * scale
-            wind[a, 8 + x, 8:16] = y_low[32 + a * 8 + x] * scale
-            wind[a, 8 + x, 48:56] = y_high[32 + a * 8 + x] * scale
-        for j in range(6):
-            wind[a, 2 + j, 16:48] = x_low[32 + a * 6 + j] * scale
-            wind[a, 16 + j, 16:48] = x_high[32 + a * 6 + j] * scale
+            wind[a, 8 + x, 12:16] = y_low[32 + a * 4 + x // 2, half_tile] * scale
+            wind[a, 8 + x, 48:52] = y_high[32 + a * 4 + x // 2, half_tile] * scale
         for j in range(4):
-            for first, e in ((4, e_low), (16, e_high)):
-                wind[a, first + j, 8:16] = e[48 + (a * 4 + j) * 2] * scale
-                wind[a, first + j, 48:56] = e[48 + (a * 4 + j) * 2 + 1] * scale
+            wind[a, 4 + j, 16:48] = x_low[24 + a * 4 + j] * scale
+            wind[a, 16 + j, 16:48] = x_high[24 + a * 4 + j] * scale
+        for e, near in ((e_low, 6), (e_high, 16)):
+            for j in range(2):
+                at = 4 * (a % 2) + 2 * j
+                wind[a, near + j, 14:16] = e[12 + a // 2 * 2, at : at + 2] * scale
+                wind[a, near + j, 48:50] = e[13 + a // 2 * 2, at : at + 2] * scale
     for x in range(8):
+        half_tile = slice(4 * (x % 2), 4 * (x % 2) + 4)
         zm[8 + x, 16:48] = z_left[x] + z_right[x]
-        zm[8 + x, 8:16] = y_low[56 + x]
-        zm[8 + x, 48:56] = y_high[56 + x]
-    for j in range(6):
-        for first, e in ((2, e_low), (16, e_high)):
+        zm[8 + x, 12:16] = y_low[44 + x // 2, half_tile]
+        zm[8 + x, 48:52] = y_high[44 + x // 2, half_tile]
+    for e, near, first in ((e_low, 6, 4), (e_high, 16, 16)):
+        for j in range(4):
             for t in range(4):
-                zm[first + j, 16 + 8 * t : 24 + 8 * t] = e[72 + j * 4 + t]
-    for j in range(4):
-        for first, e in ((4, e_low), (16, e_high)):
-            zm[first + j, 8:16] = e[96 + j * 2]
-            zm[first + j, 48:56] = e[96 + j * 2 + 1]
+                zm[first + j, 16 + 8 * t : 24 + 8 * t] = e[16 + j * 4 + t]
+        for j in range(2):
+            zm[near + j, 14:16] = e[32, 2 * j : 2 * j + 2]
+            zm[near + j, 48:50] = e[32, 4 + 2 * j : 6 + 2 * j]
 
     def chunk(rows):
         lane = lanes_of(rows)
@@ -183,16 +201,17 @@
                 one = one + roll(one, 32)
                 edge_wind[a, x, r : r + rows] = one + roll(one, 64)
 
-    @pl.loop(4, 20)
+    full, own = (8, 24, 40), (16, 32)
+
+    @pl.loop(6, 18)
     def _(x):
-        for r in (8, 24, 40):
+        for r in full:
             slabs(x, r, 16, True)
 
     @pl.loop(0, 4)
     def _(j):
-        x = jnp.where(j < 2, 2 + j, 18 + j)
-        for r in (16, 32):
-            slabs(x, r, 16, False)
+        for r in own:
+            slabs(jnp.where(j < 2, 4 + j, 16 + j), r, 16, False)
 
     dd = [d[i] * TIME_STEP for i in range(4)]
     cc = [[c[i, w] * TIME_STEP for w in range(4)] for i in range(4)]
@@ -267,64 +286,119 @@
             new = half(slab_dst[x, at], q, t) if mean else q + t
             slab_dst[x, at] = jnp.where(ok & z_ok, new, 0.0)
 
-    full, own = (8, 24, 40), (16, 32)
-
-    @pl.loop(4, 20)
+    @pl.loop(6, 18)
     def _(x):
         stage(x, full, full, state, edge, section, edge2, False)
 
     @pl.loop(0, 4)
     def _(j):
-        stage(jnp.where(j < 2, 2 + j, 18 + j), own, (), state, edge, section, edge2, False)
-
-    @pl.loop(6, 18)
+        stage(jnp.where(j < 2, 4 + j, 16 + j), own, (), state, edge, section, edge2, False)
+
+    @pl.loop(8, 16)
     def _(x):
-        stage(x, full, full, section, edge2, state, edge, True)
+        stage(x, full, own, section, edge2, state, edge, True)
 
     @pl.loop(0, 4)
     def _(j):
-        stage(jnp.where(j < 2, 4 + j, 16 + j), own, (), section, edge2, state, edge, True)
+        stage(jnp.where(j < 2, 6 + j, 14 + j), own, (), section, edge2, state, edge, True)
 
     @pl.loop(8, 16)
     def _(x):
-        stage(x, full, own, state, edge, section, edge2, False)
-
-    @pl.loop(0, 4)
-    def _(j):
-        stage(jnp.where(j < 2, 6 + j, 14 + j), own, (), state, edge, section, edge2, False)
+        stage(x, own, (), state, edge, section, edge2, False)
+
+    for i in range(4):
+        for x in (6, 7, 16, 17):
+            section[i, x, 16:48] = jnp.zeros((32, 128), F32)
+        for x in range(8):
+            section[i, 8 + x, 0:16] = jnp.zeros((16, 128), F32)
+            section[i, 8 + x, 48:64] = jnp.zeros((16, 128), F32)
 
     @pl.loop(0, 8)
     def _(x):
+        base = pl.multiple_of(x * 48, 16)
         for r in own:
-            q, t = tendencies(section, edge2, 8 + x, r, 16)
+            lane, _, _ = chunk(16)
+            at = slice(r, r + 16)
+            u = [wind[a, 8 + x, at] for a in range(3)]
+            u_out = roll(zm[8 + x, at], 48) * (0.5 * scale)
+            q = [section[i, 8 + x, at] for i in range(4)]
             for i in range(4):
-                row = pl.multiple_of(x * 32 + (r - 16), 16)
-                final[i, pl.ds(row, 16)] = half(state[i, 8 + x, r : r + 16], q[i], t[i])
-
-    rhs[...] = jnp.zeros((4, 128, 128), F32)
+                plus, minus, plus2, minus2 = (roll(q[i], o) for o in (-1, 1, -2, 2))
+                src = section
+                gz_, lz = terms(
+                    jnp.where(lane == 127, 0.0, plus),
+                    jnp.where(lane == 0, 0.0, minus),
+                    jnp.where(lane >= 126, 0.0, plus2),
+                    jnp.where(lane < 2, 0.0, minus2),
+                )
+                gx_, lx = terms(*(src[i, 8 + x + o, at] for o in (1, -1, 2, -2)))
+                gy_, ly = terms(*(src[i, 8 + x, r + o : r + o + 16] for o in (1, -1, 2, -2)))
+                mix = cc[i][0] * q[0] + cc[i][1] * q[1] + (cc[i][2] * q[2] + cc[i][3] * q[3])
+                moved = u[0] * gx_ + u[1] * gy_ + u[2] * gz_
+                t = dd[i] * (lx + ly + lz) - moved + q[i] * (mix - 6.0 * dd[i])
+                row = pl.multiple_of(base + (r - 8), 8)
+                final[i, pl.ds(row, 16), 0:128] = half(state[i, 8 + x, at], q[i], t)
+                one = jnp.where(lane == 127, plus, jnp.where(lane == 0, -minus, 0.0))
+                two = jnp.where(lane >= 126, plus2, jnp.where(lane < 2, -minus2, 0.0))
+                spread = jnp.where(lane == 127, plus, jnp.where(lane == 0, minus, 0.0))
+                beyond = (0.5 * dd[i]) * spread - u_out * (8.0 * one - two)
+                final[i, pl.ds(row, 16), 128:256] = jnp.where((lane >= 126) | (lane < 2), beyond, 0.0)
+        row8 = lax.broadcasted_iota(jnp.int32, (8, 128), 0)
+        for r, to, kept in ((8, 0, row8 >= 6), (48, 40, row8 < 2)):
+            u_y = wind[1, 8 + x, r : r + 8]
+            for i in range(4):
+                gy_, ly = terms(*(section[i, 8 + x, r + o : r + o + 8] for o in (1, -1, 2, -2)))
+                row = pl.multiple_of(base + to, 8)
+                face = jnp.where(kept, 0.5 * (dd[i] * ly - u_y * gy_), 0.0)
+                final[i, pl.ds(row, 8), 0:128] = face
+                final[i, pl.ds(row, 8), 128:256] = jnp.zeros((8, 128), F32)
+    for i in range(4):
+        first, second = section[i, 8, 16:48], section[i, 9, 16:48]
+        last, before = section[i, 15, 16:48], section[i, 14, 16:48]
+        u = [wind[0, x, 16:48] for x in (6, 7, 16, 17)]
+        faces[i, 0:32] = 0.5 * (u[0] * first)
+        faces[i, 32:64] = 0.5 * (dd[i] * first - u[1] * (8.0 * first - second))
+        faces[i, 64:96] = 0.5 * (dd[i] * last + u[2] * (8.0 * last - before))
+        faces[i, 96:128] = -0.5 * (u[3] * last)
+
+    lane32 = lanes_of(32)
+    outer = jnp.where((lane32 >= 126) | (lane32 < 2), roll(zm[8, 16:48], 16), 0.0)
+    rhs[...] = jnp.zeros((4, 128, 256), F32)
     for i in range(4):
         for k in range(4):
-            rhs[i, 32 * k + 8 * i : 32 * k + 8 * i + 8] = fz[8 * k : 8 * k + 8]
+            at = slice(32 * k + 8 * i, 32 * k + 8 * i + 8)
+            rhs[i, at, 0:128] = fz[8 * k : 8 * k + 8]
+            rhs[i, at, 128:256] = outer[8 * k : 8 * k + 8]
+    fye[0:8] = y_low[48, :, 0:32]
+    fye[8:40] = fy[...]
+    fye[40:48] = y_high[48, :, 0:32]
     total = dot(final[0], rhs[0], 1, 1)
+    total_faces = dot(faces[0], rhs[0, :, 0:128], 1, 1)
     for i in range(1, 4):
         total = total + dot(final[i], rhs[i], 1, 1)
+        total_faces = total_faces + dot(faces[i], rhs[i, :, 0:128], 1, 1)
     for x in range(8):
-        mixed[x * 32 : x * 32 + 32] = dot(fy[...], total[x * 32 : x * 32 + 32], 0, 0)
-    lane = lanes_of(8)
+        mixed[x * 32 : x * 32 + 32] = dot(fye[...], total[x * 48 : x * 48 + 48], 0, 0)
+    for x in range(4):
+        mixed[256 + x * 32 : 288 + x * 32] = dot(fy[...], total_faces[x * 32 : x * 32 + 32], 0, 0)
+    lane = lanes_of(4)
     for j in range(8):
-        tiles = [mixed[pl.ds(4 * j + b, 8, stride=32), :] for b in range(4)]
-        for k in range(4):
-            tile = jnp.zeros((8, 128), F32)
-            for b in range(4):
-                tile = jnp.where(within(lane, 32 * b, 32), roll(tiles[b], 32 * (b - k)), tile)
-            out[j * 4 + k] = tile
-
-
-def contract_x(parts, fx, out):
+        for t in range(3):
+            tiles = [mixed[pl.ds(128 * t + 4 * j + b, 4, stride=32), :] for b in range(4)]
+            for k in range(4):
+                tile = jnp.zeros((4, 128), F32)
+                for b in range(4):
+                    tile = jnp.where(within(lane, 32 * b, 32), roll(tiles[b], 32 * (b - k)), tile)
+                out[j * 4 + k, :, 128 * t : 128 * t + 128] = tile
+
+
+def contract_x(parts, fx, e_low, e_high, out):
     total = parts[0]
     for p in range(1, parts.shape[0]):
         total = total + parts[p]
-    out[...] = dot(fx[...], total, 0, 0)
+    outer = jnp.concatenate([e_low[33, 6:8, 0:32], e_high[33, 0:2, 0:32]], axis=0)
+    result = dot(fx[0:4], total[:, 0:128], 0, 0) + dot(fx[4:8], total[:, 128:256], 0, 0)
+    out[...] = result + dot(outer, total[:, 256:384], 0, 0)
 
 
 def local(fields, velocity, diffusivity, coupling, factor_x, factor_y, factor_z):
@@ -336,16 +410,16 @@
         )
 
     x_up, x_down, z_up, z_down = call(
-        pack_xz, [f32(50, 32, 128)] * 2 + [f32(8, 32, 128)] * 2, [vmem()] * 2, "pack_xz"
-    )(fields, velocity)
+        pack_xz, [f32(36, 32, 128)] * 2 + [f32(8, 32, 128)] * 2, [vmem()] * 3, "pack_xz"
+    )(fields, velocity, factor_z.T)
     x_low, x_high = both_ways("gx", x_up, x_down)
     z_left, z_right = both_ways("gz", z_up, z_down)
-    y_up, y_down = call(pack_y, [f32(64, 8, 128)] * 2, [vmem()] * 4, "pack_y")(
-        fields, velocity, z_left, z_right
+    y_up, y_down = call(pack_y, [f32(49, 8, 128)] * 2, [vmem()] * 5, "pack_y")(
+        fields, velocity, factor_y, z_left, z_right
     )
     y_low, y_high = both_ways("gy", y_up, y_down)
-    e_up, e_down = call(pack_x2, [f32(104, 8, 128)] * 2, [vmem()] * 4, "pack_x2")(
-        z_left, z_right, y_low, y_high
+    e_up, e_down = call(pack_x2, [f32(34, 8, 128)] * 2, [vmem()] * 5, "pack_x2")(
+        z_left, z_right, y_low, y_high, factor_x
     )
     e_low, e_high = both_ways("gx", e_up, e_down)
 
@@ -355,14 +429,14 @@
     gy, gz, gx = (lax.axis_size(n) for n in ("gy", "gz", "gx"))
     parts = call(
         advance,
-        f32(32, 8, 128),
+        f32(32, 4, 384),
         [smem()] * 2 + [vmem()] * 12,
         "advance",
         scratch=[
             tiles(4, PLANES), tiles(4, PLANES), tiles(PLANES), tiles(PLANES),
             tiles(3, PLANES), tiles(3, PLANES), tiles(PLANES),
-            pltpu.VMEM((4, 256, 128), F32), pltpu.VMEM((256, 128), F32),
-            pltpu.VMEM((4, 128, 128), F32),
+            pltpu.VMEM((4, 384, 256), F32), pltpu.VMEM((4, 128, 128), F32), pltpu.VMEM((384, 128), F32),
+            pltpu.VMEM((4, 128, 256), F32), pltpu.VMEM((48, 32), F32),
         ],
         work=10000000,
         mib=24,
@@ -371,7 +445,9 @@
         e_low, e_high, factor_z.T, factor_y,
     )
     parts = lax.all_to_all(parts, ("gy", "gz"), 0, 0, tiled=True)
-    slices = call(contract_x, f32(32, 128), [vmem()] * 2, "contract_x")(parts, factor_x)
+    slices = call(contract_x, f32(32, 128), [vmem()] * 4, "contract_x")(
+        parts, factor_x, e_low, e_high
+    )
     slices = lax.all_to_all(slices, "gx", 0, 0, tiled=True)
     core = jnp.sum(slices.reshape(gx, 32 // gx, 4, 4, 8), axis=0)
     return core.transpose(2, 0, 1, 3)

time: 123 us -> 107 us (0.87)
  blocking collectives: 51.4 us -> 38.3 us
  Pallas kernels: 26.7 us -> 21.7 us
  waiting for transfers between devices: 14.6 us -> 15.9 us
    all_to_all x1, blocking collectives: 26.8 us -> 17.3 us  [local(): slices = lax.all_to_all(slices, 'gx', 0, 0, tiled=True)]
    pallas_call x5, Pallas kernels: 26.7 us -> 21.7 us  [the longest x1 20.3 us: local(): call(advance, f32(32, 4, 384), [smem()] * 2 + [vmem()] * 12, 'advance', s...]
    ppermute x4, waiting for transfers between devices: 9.87 us -> 13.9 us  [both_ways(): lax.ppermute(down, axis, [(b, a) for a, b in pairs])]
    all_to_all x1, blocking collectives: 24.6 us -> 21 us  [local(): parts = lax.all_to_all(parts, ('gy', 'gz'), 0, 0, tiled=True)]
    ppermute x4, waiting for transfers between devices: 4.75 us -> 2.02 us  [both_ways(): lax.ppermute(up, axis, pairs)]
    unnamed x18 -> x20, local copies, waits for them, and re-layouts: 2.08 us -> 2.79 us
  transfers between devices with their start and end apart: 8 -> 8, of which waited for: 4 -> 6; matrix products, arithmetic and copies ran while one was open for 0% -> 0% of each run, Pallas kernels for 0% -> 0%
where the time goes in v3:
time: 107 us; the launch traced here: 106 us
  blocking collectives  38.3 us (36%)
  starting transfers between devices  26.7 us (25%)
  Pallas kernels  21.7 us (20%)
  waiting for transfers between devices  15.9 us (15%)
  local copies, waits for them, and re-layouts  3.5 us (3%)
    all_to_all x1, blocking collectives, local(): parts = lax.all_to_all(parts, ('gy', 'gz'), 0, 0, tiled=True)  21 us
    ppermute x4, starting transfers between devices, both_ways(): lax.ppermute(up, axis, pairs)  20.9 us
    pallas_call x1, Pallas kernels, local(): call(advance, f32(32, 4, 384), [smem()] * 2 + [vmem()] * 12, 'advance', s...  20.3 us
    all_to_all x1, blocking collectives, local(): slices = lax.all_to_all(slices, 'gx', 0, 0, tiled=True)  17.3 us
    ppermute x4, waiting for transfers between devices, both_ways(): lax.ppermute(down, axis, [(b, a) for a, b in pairs])  13.9 us
    ppermute x4, starting transfers between devices, both_ways(): lax.ppermute(down, axis, [(b, a) for a, b in pairs])  5.8 us
    unnamed x20, local copies, waits for them, and re-layouts  2.79 us
  transfers between devices with their start and end apart: 8, of which 6 were waited for; matrix products, arithmetic and copies ran while one was open for 0% of the time, Pallas kernels for 0%

profile of v3, /device:TPU:1, one launch (start us, length us, event | category | flops | bytes accessed | tf_op | source)
XLA Modules:
  0.0 106.4 jit_solution(7190890651745195754)
XLA Ops:
  0.0 1.0 copy-done
  1.0 1.0 copy-done.2
  2.0 0.7 copy-done.4
  2.8 1.0 pack_xz.1
  3.8 4.9 %collective-permute-start.2 = (f32[36,32,128]{2,1,0:T(8,128)S(1)}, f32[36,32,128]{2,1,0:T(8,128)S(1)}, u32[]{:S(2)}, u32[]{:S(2)}) collective-permute-start(f32[36,32,128]{2,1,0:T(8,128)S(1)} %get-tuple-element.15), channel_id=1, source_target_pairs={{0,32},{32,64},{64,96},{96,128},{128,160},{160,192},{192,224},{224... | collective-permute-start | bytes 1769480 | tf_op jit(solution)/shard_map/ppermute | solution.py:408
  8.6 1.3 %collective-permute-start.3 = (f32[36,32,128]{2,1,0:T(8,128)S(1)}, f32[36,32,128]{2,1,0:T(8,128)S(1)}, u32[]{:S(2)}, u32[]{:S(2)}) collective-permute-start(f32[36,32,128]{2,1,0:T(8,128)S(1)} %get-tuple-element.16), channel_id=1, source_target_pairs={{32,0},{64,32},{96,64},{128,96},{160,128},{192,160},{224,192},{256... | collective-permute-start | bytes 1769480 | tf_op jit(solution)/shard_map/ppermute | solution.py:409
  9.9 3.1 %collective-permute-start = (f32[8,32,128]{2,1,0:T(8,128)S(1)}, f32[8,32,128]{2,1,0:T(8,128)S(1)}, u32[]{:S(2)}, u32[]{:S(2)}) collective-permute-start(f32[8,32,128]{2,1,0:T(8,128)S(1)} %get-tuple-element.13), channel_id=1, source_target_pairs={{0,1},{1,2},{2,3},{4,5},{5,6},{6,7},{8,9},{9,10},{10,11},{12,13},{... | collective-permute-start | bytes 393224 | tf_op jit(solution)/shard_map/ppermute | solution.py:408
  13.1 1.3 %collective-permute-start.1 = (f32[8,32,128]{2,1,0:T(8,128)S(1)}, f32[8,32,128]{2,1,0:T(8,128)S(1)}, u32[]{:S(2)}, u32[]{:S(2)}) collective-permute-start(f32[8,32,128]{2,1,0:T(8,128)S(1)} %get-tuple-element.14), channel_id=1, source_target_pairs={{1,0},{2,1},{3,2},{5,4},{6,5},{7,6},{9,8},{10,9},{11,10},{13,12},{... | collective-permute-start | bytes 393224 | tf_op jit(solution)/shard_map/ppermute | solution.py:409
  14.4 0.6 collective-permute-done.z_left
  15.0 4.1 %collective-permute-done.1.z_right = f32[8,32,128]{2,1,0:T(8,128)S(1)} collective-permute-done((f32[8,32,128]{2,1,0:T(8,128)S(1)}, f32[8,32,128]{2,1,0:T(8,128)S(1)}, u32[]{:S(2)}, u32[]{:S(2)}) %collective-permute-start.1) | collective-permute-done | bytes 131104 | tf_op jit(solution)/shard_map/ppermute | solution.py:409
  19.2 6.3 %collective-permute-start.4 = (f32[49,8,128]{2,1,0:T(8,128)S(1)}, f32[49,8,128]{2,1,0:T(8,128)S(1)}, u32[]{:S(2)}, u32[]{:S(2)}) collective-permute-start(f32[49,8,128]{2,1,0:T(8,128)S(1)} %get-tuple-element.17), channel_id=1, source_target_pairs={{0,4},{4,8},{8,12},{12,16},{16,20},{20,24},{24,28},{1,5},{5,9},{9,... | collective-permute-start | bytes 602120 | tf_op jit(solution)/shard_map/ppermute | solution.py:408
  25.5 1.9 %collective-permute-start.5 = (f32[49,8,128]{2,1,0:T(8,128)S(1)}, f32[49,8,128]{2,1,0:T(8,128)S(1)}, u32[]{:S(2)}, u32[]{:S(2)}) collective-permute-start(f32[49,8,128]{2,1,0:T(8,128)S(1)} %get-tuple-element.18), channel_id=1, source_target_pairs={{4,0},{8,4},{12,8},{16,12},{20,16},{24,20},{28,24},{5,1},{9,5},{13... | collective-permute-start | bytes 602120 | tf_op jit(solution)/shard_map/ppermute | solution.py:409
  27.4 0.7 collective-permute-done.4.y_low
  28.1 5.4 %collective-permute-done.5.y_high = f32[49,8,128]{2,1,0:T(8,128)S(1)} collective-permute-done((f32[49,8,128]{2,1,0:T(8,128)S(1)}, f32[49,8,128]{2,1,0:T(8,128)S(1)}, u32[]{:S(2)}, u32[]{:S(2)}) %collective-permute-start.5) | collective-permute-done | bytes 200736 | tf_op jit(solution)/shard_map/ppermute | solution.py:409
  33.6 6.7 %collective-permute-start.6 = (f32[34,8,128]{2,1,0:T(8,128)S(1)}, f32[34,8,128]{2,1,0:T(8,128)S(1)}, u32[]{:S(2)}, u32[]{:S(2)}) collective-permute-start(f32[34,8,128]{2,1,0:T(8,128)S(1)} %get-tuple-element.19), channel_id=1, source_target_pairs={{0,32},{32,64},{64,96},{96,128},{128,160},{160,192},{192,224},{224... | collective-permute-start | bytes 417800 | tf_op jit(solution)/shard_map/ppermute | solution.py:408
  40.3 1.3 %collective-permute-start.7 = (f32[34,8,128]{2,1,0:T(8,128)S(1)}, f32[34,8,128]{2,1,0:T(8,128)S(1)}, u32[]{:S(2)}, u32[]{:S(2)}) collective-permute-start(f32[34,8,128]{2,1,0:T(8,128)S(1)} %get-tuple-element.20), channel_id=1, source_target_pairs={{32,0},{64,32},{96,64},{128,96},{160,128},{192,160},{224,192},{256... | collective-permute-start | bytes 417800 | tf_op jit(solution)/shard_map/ppermute | solution.py:409
  41.6 0.7 collective-permute-done.6.e_low
  42.3 4.4 %collective-permute-done.7.e_high = f32[34,8,128]{2,1,0:T(8,128)S(1)} collective-permute-done((f32[34,8,128]{2,1,0:T(8,128)S(1)}, f32[34,8,128]{2,1,0:T(8,128)S(1)}, u32[]{:S(2)}, u32[]{:S(2)}) %collective-permute-start.7) | collective-permute-done | bytes 139296 | tf_op jit(solution)/shard_map/ppermute | solution.py:409
  46.8 20.3 %advance.1 = f32[32,4,384]{2,1,0:T(4,128)S(1)} custom-call(f32[4]{0:T(128)S(1)} %copy-done.9, f32[4,4]{1,0:T(4,128)S(1)} %copy-done.8, f32[4,8,32,128]{3,2,1,0:T(8,128)S(1)} %copy-done.1, f32[3,8,32,128]{3,2,1,0:T(8,128)S(1)} %copy-done.3, f32[8,32,128]{2,1,0:T(8,128)S(1)} %collective-permute-done.z_left, f32[8,32,128]{2,1,0:T(8,128)S(1)} %collective-permute-done.1.z_right, ...), custom_call_target="tpu_custom_call" | custom-call | flops 10000000 | bytes 10000000 | tf_op jit(solution)/shard_map/advance/pallas_call | solution.py:430
  67.1 21.0 %all_to_all.14.parts = f32[32,4,384]{2,1,0:T(4,128)S(1)} all-to-all(f32[32,4,384]{2,1,0:T(4,128)S(1)} %advance.1), channel_id=1, replica_groups=mesh['gx'=16,'gy'=8,'gz'=4] {'gy','gz'}, dimensions={0} | all-to-all | bytes 393216 | tf_op jit(solution)/shard_map/all_to_all | solution.py:447
  88.1 0.2 contract_x.1
  88.4 17.3 %all_to_all.15 = f32[16,2,128]{2,1,0:T(2,128)S(1)} all-to-all(f32[16,2,128]{2,1,0:T(2,128)S(1)} %bitcast.5), channel_id=1, replica_groups=mesh['gx'=16,'gy'=8,'gz'=4] {'gx'}, dimensions={0} | all-to-all | bytes 32768 | tf_op jit(solution)/shard_map/all_to_all | solution.py:451
  105.7 0.1 reduce_sum.12
  105.8 0.6 copy.8
  (22 shorter events, 0.2 us)
Async XLA Ops:
  0.0 1.0 copy-start
  1.0 1.0 copy-start.2
  2.0 0.7 copy-start.4
  2.8 16.3 %copy-start.6 = (f32[32,32]{1,0:T(8,128)S(1)}, f32[32,32]{1,0:T(8,128)}, u32[]{:S(2)}) copy-start(f32[32,32]{1,0:T(8,128)} %fy.3) | copy-start | bytes 12292
  3.8 42.9 %collective-permute-start.2 = (f32[36,32,128]{2,1,0:T(8,128)S(1)}, f32[36,32,128]{2,1,0:T(8,128)S(1)}, u32[]{:S(2)}, u32[]{:S(2)}) collective-permute-start(f32[36,32,128]{2,1,0:T(8,128)S(1)} %get-tuple-element.15), channel_id=1, source_target_pairs={{0,32},{32,64},{64,96},{96,128},{128,160},{160,192},{192,224},{224... | collective-permute-start | bytes 1769480 | tf_op jit(solution)/shard_map/ppermute | solution.py:408
  8.6 38.1 %collective-permute-start.3 = (f32[36,32,128]{2,1,0:T(8,128)S(1)}, f32[36,32,128]{2,1,0:T(8,128)S(1)}, u32[]{:S(2)}, u32[]{:S(2)}) collective-permute-start(f32[36,32,128]{2,1,0:T(8,128)S(1)} %get-tuple-element.16), channel_id=1, source_target_pairs={{32,0},{64,32},{96,64},{128,96},{160,128},{192,160},{224,192},{256... | collective-permute-start | bytes 1769480 | tf_op jit(solution)/shard_map/ppermute | solution.py:409
  9.9 5.1 %collective-permute-start = (f32[8,32,128]{2,1,0:T(8,128)S(1)}, f32[8,32,128]{2,1,0:T(8,128)S(1)}, u32[]{:S(2)}, u32[]{:S(2)}) collective-permute-start(f32[8,32,128]{2,1,0:T(8,128)S(1)} %get-tuple-element.13), channel_id=1, source_target_pairs={{0,1},{1,2},{2,3},{4,5},{5,6},{6,7},{8,9},{9,10},{10,11},{12,13},{... | collective-permute-start | bytes 393224 | tf_op jit(solution)/shard_map/ppermute | solution.py:408
  13.1 6.0 %collective-permute-start.1 = (f32[8,32,128]{2,1,0:T(8,128)S(1)}, f32[8,32,128]{2,1,0:T(8,128)S(1)}, u32[]{:S(2)}, u32[]{:S(2)}) collective-permute-start(f32[8,32,128]{2,1,0:T(8,128)S(1)} %get-tuple-element.14), channel_id=1, source_target_pairs={{1,0},{2,1},{3,2},{5,4},{6,5},{7,6},{9,8},{10,9},{11,10},{13,12},{... | collective-permute-start | bytes 393224 | tf_op jit(solution)/shard_map/ppermute | solution.py:409
  19.1 14.5 %copy-start.7 = (f32[8,32]{1,0:T(8,128)S(1)}, f32[8,32]{1,0:T(8,128)}, u32[]{:S(2)}) copy-start(f32[8,32]{1,0:T(8,128)} %fx.3) | copy-start | bytes 3076
  19.1 27.6 %copy-start.3 = (f32[3,8,32,128]{3,2,1,0:T(8,128)S(1)}, f32[3,8,32,128]{3,2,1,0:T(8,128)}, u32[]{:S(2)}) copy-start(f32[3,8,32,128]{3,2,1,0:T(8,128)} %v.5) | copy-start | bytes 1179652
  19.1 27.6 %copy-start.1 = (f32[4,8,32,128]{3,2,1,0:T(8,128)S(1)}, f32[4,8,32,128]{3,2,1,0:T(8,128)}, u32[]{:S(2)}) copy-start(f32[4,8,32,128]{3,2,1,0:T(8,128)} %f.5) | copy-start | bytes 1572868
  19.2 9.0 %collective-permute-start.4 = (f32[49,8,128]{2,1,0:T(8,128)S(1)}, f32[49,8,128]{2,1,0:T(8,128)S(1)}, u32[]{:S(2)}, u32[]{:S(2)}) collective-permute-start(f32[49,8,128]{2,1,0:T(8,128)S(1)} %get-tuple-element.17), channel_id=1, source_target_pairs={{0,4},{4,8},{8,12},{12,16},{16,20},{20,24},{24,28},{1,5},{5,9},{9,... | collective-permute-start | bytes 602120 | tf_op jit(solution)/shard_map/ppermute | solution.py:408
  25.5 21.2 %copy-start.5 = (f32[128,32]{0,1:T(8,128)S(1)}, f32[128,32]{0,1:T(8,128)}, u32[]{:S(2)}) copy-start(f32[128,32]{0,1:T(8,128)} %param.13) | copy-start | bytes 49156
  25.5 8.0 %collective-permute-start.5 = (f32[49,8,128]{2,1,0:T(8,128)S(1)}, f32[49,8,128]{2,1,0:T(8,128)S(1)}, u32[]{:S(2)}, u32[]{:S(2)}) collective-permute-start(f32[49,8,128]{2,1,0:T(8,128)S(1)} %get-tuple-element.18), channel_id=1, source_target_pairs={{4,0},{8,4},{12,8},{16,12},{20,16},{24,20},{28,24},{5,1},{9,5},{13... | collective-permute-start | bytes 602120 | tf_op jit(solution)/shard_map/ppermute | solution.py:409
  33.6 13.2 %copy-start.8 = (f32[4,4]{1,0:T(4,128)S(1)}, f32[4,4]{1,0:T(4,128)}, u32[]{:S(2)}) copy-start(f32[4,4]{1,0:T(4,128)} %c.1) | copy-start | bytes 196
  33.6 13.2 %copy-start.9 = (f32[4]{0:T(128)S(1)}, f32[4]{0:T(128)}, u32[]{:S(2)}) copy-start(f32[4]{0:T(128)} %d.1) | copy-start | bytes 52
  33.6 8.7 %collective-permute-start.6 = (f32[34,8,128]{2,1,0:T(8,128)S(1)}, f32[34,8,128]{2,1,0:T(8,128)S(1)}, u32[]{:S(2)}, u32[]{:S(2)}) collective-permute-start(f32[34,8,128]{2,1,0:T(8,128)S(1)} %get-tuple-element.19), channel_id=1, source_target_pairs={{0,32},{32,64},{64,96},{96,128},{128,160},{160,192},{192,224},{224... | collective-permute-start | bytes 417800 | tf_op jit(solution)/shard_map/ppermute | solution.py:408
  40.3 6.4 %collective-permute-start.7 = (f32[34,8,128]{2,1,0:T(8,128)S(1)}, f32[34,8,128]{2,1,0:T(8,128)S(1)}, u32[]{:S(2)}, u32[]{:S(2)}) collective-permute-start(f32[34,8,128]{2,1,0:T(8,128)S(1)} %get-tuple-element.20), channel_id=1, source_target_pairs={{32,0},{64,32},{96,64},{128,96},{160,128},{192,160},{224,192},{256... | collective-permute-start | bytes 417800 | tf_op jit(solution)/shard_map/ppermute | solution.py:409

commit v4 on v3

--- a/solution.py
+++ b/solution.py
@@ -7,7 +7,6 @@
 
 TIME_STEP = 0.2
 F32 = jnp.float32
-HIGHEST = lax.Precision.HIGHEST
 PLANES, ROWS = 24, 64
 LOW, HIGH = 8, 16
 
@@ -46,26 +45,38 @@
     return (lane >= first) & (lane < first + size)
 
 
+def halves(a):
+    high = a.astype(jnp.bfloat16)
+    return high, (a - high.astype(F32)).astype(jnp.bfloat16)
+
+
 def dot(a, b, a_dim, b_dim):
-    return lax.dot_general(
-        a, b, (((a_dim,), (b_dim,)), ((), ())), precision=HIGHEST, preferred_element_type=F32
-    )
+    def product(p, q):
+        return lax.dot_general(p, q, (((a_dim,), (b_dim,)), ((), ())), preferred_element_type=F32)
+
+    (a_high, a_low), (b_high, b_low) = halves(a), halves(b)
+    return product(a_high, b_high) + (product(a_high, b_low) + product(a_low, b_high))
 
 
 def padded(rows):
     return jnp.concatenate([rows, jnp.zeros((rows.shape[0], 128 - rows.shape[1]), F32)], axis=1)
 
 
-def pack_xz(f, v, fz, x_up, x_down, z_up, z_down):
+def ways(axis):
+    odd = lax.rem(lax.axis_index(axis), 2)
+    return 1 - odd, odd
+
+
+def pack_xz(f, v, fz, x_even, x_odd, z_even, z_odd):
     lane = lanes_of(32)
-    for j in range(6):
-        for i in range(4):
-            x_up[i * 6 + j] = f[i, 2 + j]
-            x_down[i * 6 + j] = f[i, j]
-    for j in range(4):
-        for a in range(3):
-            x_up[24 + a * 4 + j] = v[a, 4 + j]
-            x_down[24 + a * 4 + j] = v[a, j]
+    for out, up in zip((x_even, x_odd), ways("gx")):
+        for j in range(6):
+            for i in range(4):
+                out[i * 6 + j] = f[i, 2 * up + j]
+        for j in range(4):
+            for a in range(3):
+                out[24 + a * 4 + j] = v[a, 4 * up + j]
+    even_up, _ = ways("gz")
 
     def plane_edges(x, carry):
         up = jnp.zeros((32, 128), F32)
@@ -78,51 +89,70 @@
             plane = pltpu.roll(v[a, x] if a < 3 else fz[...], 32 * a + 16, 1)
             up = jnp.where(within(lane, 32 * a + 8, 8), plane, up)
             down = jnp.where(within(lane, 32 * a + 16, 8), plane, down)
-        z_up[x] = up
-        z_down[x] = down
+        z_even[x] = jnp.where(even_up == 1, up, down)
+        z_odd[x] = jnp.where(even_up == 1, down, up)
         return carry
 
     lax.fori_loop(0, 8, plane_edges, 0)
 
 
-def pack_y(f, v, fy, z_left, z_right, y_up, y_down):
-    for out, row, row4 in ((y_up, 24, 28), (y_down, 0, 0)):
+def pack_y(f, v, fy, z_even, z_odd, y_even, y_odd):
+    for out, up in zip((y_even, y_odd), ways("gy")):
+
+        def edge_rows(high, low):
+            return jnp.where(up == 1, high, low)
+
         for x in range(8):
             half = slice(4 * (x % 2), 4 * (x % 2) + 4)
             for i in range(4):
-                out[i * 8 + x] = f[i, x, row : row + 8]
+                out[i * 8 + x] = edge_rows(f[i, x, 24:32], f[i, x, 0:8])
             for a in range(3):
-                out[32 + a * 4 + x // 2, half] = v[a, x, row4 : row4 + 4]
-            out[44 + x // 2, half] = z_left[x, row4 : row4 + 4] + z_right[x, row4 : row4 + 4]
-        out[48] = padded(fy[row : row + 8])
-
-
-def pack_x2(z_left, z_right, y_low, y_high, fx, up, down):
-    for out, near, far, first in ((up, 6, 4, 4), (down, 0, 2, 0)):
+                out[32 + a * 4 + x // 2, half] = edge_rows(v[a, x, 28:32], v[a, x, 0:4])
+            out[44 + x // 2, half] = edge_rows(
+                z_even[x, 28:32] + z_odd[x, 28:32], z_even[x, 0:4] + z_odd[x, 0:4]
+            )
+        out[48] = padded(edge_rows(fy[24:32], fy[0:8]))
+
+
+def sides(axis, even, odd):
+    low_is_odd = ways(axis)[0] == 1
+
+    def low(*at):
+        return jnp.where(low_is_odd, odd[at], even[at])
+
+    def high(*at):
+        return jnp.where(low_is_odd, even[at], odd[at])
+
+    return low, high
+
+
+def pack_x2(z_even, z_odd, y_even, y_odd, fx, even, odd):
+    y_low, y_high = sides("gy", y_even, y_odd)
+    for out, up in zip((even, odd), ways("gx")):
+        near, far, first = 6 * up, 2 + 2 * up, 4 * up
         for side, rows in ((0, y_low), (1, y_high)):
             four = slice(4, 8) if side == 0 else slice(0, 4)
             two = slice(6, 8) if side == 0 else slice(0, 2)
             for j in range(2):
                 for i in range(4):
-                    out[i * 2 + side, 4 * j : 4 * j + 4] = rows[i * 8 + near + j, four]
+                    out[i * 2 + side, 4 * j : 4 * j + 4] = rows(i * 8 + near + j, four)
                     at = 4 * (i % 2) + 2 * j
-                    out[8 + i // 2 * 2 + side, at : at + 2] = rows[i * 8 + far + j, two]
-                x = near + j
-                at = 4 * (x % 2) + (2 if side == 0 else 0)
+                    out[8 + i // 2 * 2 + side, at : at + 2] = rows(i * 8 + far + j, two)
+                at = 4 * j + (2 if side == 0 else 0)
                 for a in range(3):
                     to = 4 * (a % 2) + 2 * j
-                    out[12 + a // 2 * 2 + side, to : to + 2] = rows[32 + a * 4 + x // 2, at : at + 2]
+                    out[12 + a // 2 * 2 + side, to : to + 2] = rows(32 + a * 4 + 3 * up, slice(at, at + 2))
                 to = 4 * side + 2 * j
-                out[32, to : to + 2] = rows[44 + x // 2, at : at + 2]
+                out[32, to : to + 2] = rows(44 + 3 * up, slice(at, at + 2))
         for j in range(4):
-            halo = z_left[first + j] + z_right[first + j]
+            halo = z_even[first + j] + z_odd[first + j]
             for t in range(4):
                 out[16 + j * 4 + t] = halo[8 * t : 8 * t + 8]
         out[33] = padded(fx[...])
 
 
 def advance(
-    d, c, f, v, z_left, z_right, x_low, x_high, y_low, y_high, e_low, e_high, fz, fy,
+    d, c, f, v, z_even, z_odd, x_even, x_odd, y_even, y_odd, e_even, e_odd, fz, fy,
     out, state, section, edge, edge2, wind, edge_wind, zm, final, faces, mixed, rhs, fye,
 ):
     gx, gy, gz = (lax.axis_index(n) for n in ("gx", "gy", "gz"))
@@ -131,15 +161,18 @@
     y_first, y_end = jnp.where(gy == 0, 16, 0), jnp.where(gy == last_y, 48, ROWS)
     scale = TIME_STEP / 12.0
 
+    y_low, y_high = sides("gy", y_even, y_odd)
+    even_up, odd_up = ways("gx")
     for i in range(4):
         for x in range(8):
             state[i, 8 + x, 16:48] = f[i, x]
-            state[i, 8 + x, 8:16] = y_low[i * 8 + x]
-            state[i, 8 + x, 48:56] = y_high[i * 8 + x]
-        for j in range(6):
-            state[i, 2 + j, 16:48] = x_low[i * 6 + j]
-            state[i, 16 + j, 16:48] = x_high[i * 6 + j]
-        for e, near, far in ((e_low, 6, 4), (e_high, 16, 18)):
+            state[i, 8 + x, 8:16] = y_low(i * 8 + x)
+            state[i, 8 + x, 48:56] = y_high(i * 8 + x)
+        for halo, above in ((x_even, even_up), (x_odd, odd_up)):
+            for j in range(6):
+                state[i, 2 + 14 * above + j, 16:48] = halo[i * 6 + j]
+        for e, above in ((e_even, even_up), (e_odd, odd_up)):
+            near, far = 6 + 10 * above, 4 + 14 * above
             for j in range(2):
                 state[i, near + j, 12:16] = e[i * 2, 4 * j : 4 * j + 4]
                 state[i, near + j, 48:52] = e[i * 2 + 1, 4 * j : 4 * j + 4]
@@ -150,22 +183,24 @@
         for x in range(8):
             half_tile = slice(4 * (x % 2), 4 * (x % 2) + 4)
             wind[a, 8 + x, 16:48] = v[a, x] * scale
-            wind[a, 8 + x, 12:16] = y_low[32 + a * 4 + x // 2, half_tile] * scale
-            wind[a, 8 + x, 48:52] = y_high[32 + a * 4 + x // 2, half_tile] * scale
-        for j in range(4):
-            wind[a, 4 + j, 16:48] = x_low[24 + a * 4 + j] * scale
-            wind[a, 16 + j, 16:48] = x_high[24 + a * 4 + j] * scale
-        for e, near in ((e_low, 6), (e_high, 16)):
+            wind[a, 8 + x, 12:16] = y_low(32 + a * 4 + x // 2, half_tile) * scale
+            wind[a, 8 + x, 48:52] = y_high(32 + a * 4 + x // 2, half_tile) * scale
+        for halo, above in ((x_even, even_up), (x_odd, odd_up)):
+            for j in range(4):
+                wind[a, 4 + 12 * above + j, 16:48] = halo[24 + a * 4 + j] * scale
+        for e, above in ((e_even, even_up), (e_odd, odd_up)):
+            near = 6 + 10 * above
             for j in range(2):
                 at = 4 * (a % 2) + 2 * j
                 wind[a, near + j, 14:16] = e[12 + a // 2 * 2, at : at + 2] * scale
                 wind[a, near + j, 48:50] = e[13 + a // 2 * 2, at : at + 2] * scale
     for x in range(8):
         half_tile = slice(4 * (x % 2), 4 * (x % 2) + 4)
-        zm[8 + x, 16:48] = z_left[x] + z_right[x]
-        zm[8 + x, 12:16] = y_low[44 + x // 2, half_tile]
-        zm[8 + x, 48:52] = y_high[44 + x // 2, half_tile]
-    for e, near, first in ((e_low, 6, 4), (e_high, 16, 16)):
+        zm[8 + x, 16:48] = z_even[x] + z_odd[x]
+        zm[8 + x, 12:16] = y_low(44 + x // 2, half_tile)
+        zm[8 + x, 48:52] = y_high(44 + x // 2, half_tile)
+    for e, above in ((e_even, even_up), (e_odd, odd_up)):
+        near, first = 6 + 10 * above, 4 + 12 * above
         for j in range(4):
             for t in range(4):
                 zm[first + j, 16 + 8 * t : 24 + 8 * t] = e[16 + j * 4 + t]
@@ -369,9 +404,9 @@
             at = slice(32 * k + 8 * i, 32 * k + 8 * i + 8)
             rhs[i, at, 0:128] = fz[8 * k : 8 * k + 8]
             rhs[i, at, 128:256] = outer[8 * k : 8 * k + 8]
-    fye[0:8] = y_low[48, :, 0:32]
+    fye[0:8] = y_low(48, slice(0, 8), slice(0, 32))
     fye[8:40] = fy[...]
-    fye[40:48] = y_high[48, :, 0:32]
+    fye[40:48] = y_high(48, slice(0, 8), slice(0, 32))
     total = dot(final[0], rhs[0], 1, 1)
     total_faces = dot(faces[0], rhs[0, :, 0:128], 1, 1)
     for i in range(1, 4):
@@ -392,36 +427,37 @@
                 out[j * 4 + k, :, 128 * t : 128 * t + 128] = tile
 
 
-def contract_x(parts, fx, e_low, e_high, out):
+def contract_x(parts, fx, e_even, e_odd, out):
     total = parts[0]
     for p in range(1, parts.shape[0]):
         total = total + parts[p]
-    outer = jnp.concatenate([e_low[33, 6:8, 0:32], e_high[33, 0:2, 0:32]], axis=0)
+    e_low, e_high = sides("gx", e_even, e_odd)
+    outer = [e_low(33, slice(6, 8), slice(0, 32)), e_high(33, slice(0, 2), slice(0, 32))]
+    outer = jnp.concatenate(outer, axis=0)
     result = dot(fx[0:4], total[:, 0:128], 0, 0) + dot(fx[4:8], total[:, 128:256], 0, 0)
     out[...] = result + dot(outer, total[:, 256:384], 0, 0)
 
 
 def local(fields, velocity, diffusivity, coupling, factor_x, factor_y, factor_z):
-    def both_ways(axis, up, down):
-        pairs = [(i, i + 1) for i in range(lax.axis_size(axis) - 1)]
-        return (
-            lax.ppermute(up, axis, pairs),
-            lax.ppermute(down, axis, [(b, a) for a, b in pairs]),
-        )
-
-    x_up, x_down, z_up, z_down = call(
+    def swapped(axis, even, odd):
+        last = lax.axis_size(axis) - 1
+        pairs = [[(i, i + 1) for i in range(first, last, 2)] for first in (0, 1)]
+        even_pairs, odd_pairs = ([*p, *((b, a) for a, b in p)] for p in pairs)
+        return lax.ppermute(even, axis, even_pairs), lax.ppermute(odd, axis, odd_pairs)
+
+    x_even, x_odd, z_even, z_odd = call(
         pack_xz, [f32(36, 32, 128)] * 2 + [f32(8, 32, 128)] * 2, [vmem()] * 3, "pack_xz"
     )(fields, velocity, factor_z.T)
-    x_low, x_high = both_ways("gx", x_up, x_down)
-    z_left, z_right = both_ways("gz", z_up, z_down)
-    y_up, y_down = call(pack_y, [f32(49, 8, 128)] * 2, [vmem()] * 5, "pack_y")(
-        fields, velocity, factor_y, z_left, z_right
+    x_even, x_odd = swapped("gx", x_even, x_odd)
+    z_even, z_odd = swapped("gz", z_even, z_odd)
+    y_even, y_odd = call(pack_y, [f32(49, 8, 128)] * 2, [vmem()] * 5, "pack_y")(
+        fields, velocity, factor_y, z_even, z_odd
     )
-    y_low, y_high = both_ways("gy", y_up, y_down)
-    e_up, e_down = call(pack_x2, [f32(34, 8, 128)] * 2, [vmem()] * 5, "pack_x2")(
-        z_left, z_right, y_low, y_high, factor_x
+    y_even, y_odd = swapped("gy", y_even, y_odd)
+    e_even, e_odd = call(pack_x2, [f32(34, 8, 128)] * 2, [vmem()] * 5, "pack_x2")(
+        z_even, z_odd, y_even, y_odd, factor_x
     )
-    e_low, e_high = both_ways("gx", e_up, e_down)
+    e_even, e_odd = swapped("gx", e_even, e_odd)
 
     def tiles(*lead):
         return pltpu.VMEM((*lead, ROWS, 128), F32)
@@ -441,12 +477,12 @@
         work=10000000,
         mib=24,
     )(
-        diffusivity, coupling, fields, velocity, z_left, z_right, x_low, x_high, y_low, y_high,
-        e_low, e_high, factor_z.T, factor_y,
+        diffusivity, coupling, fields, velocity, z_even, z_odd, x_even, x_odd, y_even, y_odd,
+        e_even, e_odd, factor_z.T, factor_y,
     )
     parts = lax.all_to_all(parts, ("gy", "gz"), 0, 0, tiled=True)
     slices = call(contract_x, f32(32, 128), [vmem()] * 4, "contract_x")(
-        parts, factor_x, e_low, e_high
+        parts, factor_x, e_even, e_odd
     )
     slices = lax.all_to_all(slices, "gx", 0, 0, tiled=True)
     core = jnp.sum(slices.reshape(gx, 32 // gx, 4, 4, 8), axis=0)

time: 107 us -> 106 us (level)
  blocking collectives: 38.3 us -> 45.6 us
  waiting for transfers between devices: 15.9 us -> 9.77 us
  Pallas kernels: 21.7 us -> 20.5 us
    ppermute x8, waiting for transfers between devices: 15.9 us -> 9.77 us  [the longest x4 6.1 us: swapped(): lax.ppermute(odd, axis, odd_pairs)]
    all_to_all x1, blocking collectives: 21 us -> 26.2 us  [local(): parts = lax.all_to_all(parts, ('gy', 'gz'), 0, 0, tiled=True)]
    all_to_all x1, blocking collectives: 17.3 us -> 19.4 us  [local(): slices = lax.all_to_all(slices, 'gx', 0, 0, tiled=True)]
    pallas_call x1, Pallas kernels: 20.3 us -> 19.2 us  [local(): call(advance, f32(32, 4, 384), [smem()] * 2 + [vmem()] * 12, 'advance', s...]
  transfers between devices with their start and end apart: 8 -> 8, of which waited for: 6 -> 3; matrix products, arithmetic and copies ran while one was open for 0% -> 0% of each run, Pallas kernels for 0% -> 0%
where the time goes in v4:
time: 106 us
  blocking collectives  45.6 us (43%)
  starting transfers between devices  25.9 us (24%)
  Pallas kernels  20.5 us (19%)
  waiting for transfers between devices  9.77 us (9%)
  local copies, waits for them, and re-layouts  3.5 us (3%)
    all_to_all x1, blocking collectives, local(): parts = lax.all_to_all(parts, ('gy', 'gz'), 0, 0, tiled=True)  26.2 us
    ppermute x4, starting transfers between devices, swapped(): lax.ppermute(even, axis, even_pairs)  22 us
    all_to_all x1, blocking collectives, local(): slices = lax.all_to_all(slices, 'gx', 0, 0, tiled=True)  19.4 us
    pallas_call x1, Pallas kernels, local(): call(advance, f32(32, 4, 384), [smem()] * 2 + [vmem()] * 12, 'advance', s...  19.2 us
    ppermute x4, waiting for transfers between devices, swapped(): lax.ppermute(odd, axis, odd_pairs)  6.1 us
    ppermute x4, starting transfers between devices, swapped(): lax.ppermute(odd, axis, odd_pairs)  3.96 us
    ppermute x4, waiting for transfers between devices, swapped(): lax.ppermute(even, axis, even_pairs)  3.67 us
    unnamed x20, local copies, waits for them, and re-layouts  2.79 us
  transfers between devices with their start and end apart: 8, of which 3 were waited for; matrix products, arithmetic and copies ran while one was open for 0% of the time, Pallas kernels for 0%

profile of v4, /device:TPU:1, one launch (start us, length us, event | category | flops | bytes accessed | tf_op | source)
XLA Modules:
  0.0 105.5 jit_solution(7811813188599010789)
XLA Ops:
  0.0 1.0 copy-done
  1.0 1.0 copy-done.2
  2.0 0.7 copy-done.4
  2.8 1.0 pack_xz.1
  3.8 4.8 %collective-permute-start.2 = (f32[36,32,128]{2,1,0:T(8,128)S(1)}, f32[36,32,128]{2,1,0:T(8,128)S(1)}, u32[]{:S(2)}, u32[]{:S(2)}) collective-permute-start(f32[36,32,128]{2,1,0:T(8,128)S(1)} %get-tuple-element.15), channel_id=1, source_target_pairs={{0,32},{64,96},{128,160},{192,224},{256,288},{320,352},{384,416},{... | collective-permute-start | bytes 1769480 | tf_op jit(solution)/shard_map/ppermute | solution.py:446
  8.6 0.7 collective-permute-start.3
  9.3 3.1 %collective-permute-start = (f32[8,32,128]{2,1,0:T(8,128)S(1)}, f32[8,32,128]{2,1,0:T(8,128)S(1)}, u32[]{:S(2)}, u32[]{:S(2)}) collective-permute-start(f32[8,32,128]{2,1,0:T(8,128)S(1)} %get-tuple-element.13), channel_id=1, source_target_pairs={{0,1},{2,3},{1,0},{3,2},{4,5},{6,7},{5,4},{7,6},{8,9},{10,11},{9,8... | collective-permute-start | bytes 393224 | tf_op jit(solution)/shard_map/ppermute | solution.py:446
  12.5 0.7 collective-permute-start.1
  13.1 1.9 %collective-permute-done.z_even = f32[8,32,128]{2,1,0:T(8,128)S(1)} collective-permute-done((f32[8,32,128]{2,1,0:T(8,128)S(1)}, f32[8,32,128]{2,1,0:T(8,128)S(1)}, u32[]{:S(2)}, u32[]{:S(2)}) %collective-permute-start) | collective-permute-done | bytes 131104 | tf_op jit(solution)/shard_map/ppermute | solution.py:446
  15.1 0.1 pack_y.1
  15.1 0.0 copy-start.1
  15.2 7.1 %collective-permute-start.4 = (f32[49,8,128]{2,1,0:T(8,128)S(1)}, f32[49,8,128]{2,1,0:T(8,128)S(1)}, u32[]{:S(2)}, u32[]{:S(2)}) collective-permute-start(f32[49,8,128]{2,1,0:T(8,128)S(1)} %get-tuple-element.17), channel_id=1, source_target_pairs={{0,4},{8,12},{16,20},{24,28},{4,0},{12,8},{20,16},{28,24},{1,5},{9... | collective-permute-start | bytes 602120 | tf_op jit(solution)/shard_map/ppermute | solution.py:446
  22.3 1.9 %collective-permute-start.5 = (f32[49,8,128]{2,1,0:T(8,128)S(1)}, f32[49,8,128]{2,1,0:T(8,128)S(1)}, u32[]{:S(2)}, u32[]{:S(2)}) collective-permute-start(f32[49,8,128]{2,1,0:T(8,128)S(1)} %get-tuple-element.18), channel_id=1, source_target_pairs={{4,8},{12,16},{20,24},{8,4},{16,12},{24,20},{5,9},{13,17},{21,25},... | collective-permute-start | bytes 602120 | tf_op jit(solution)/shard_map/ppermute | solution.py:446
  24.2 6.1 %collective-permute-done.5.y_odd = f32[49,8,128]{2,1,0:T(8,128)S(1)} collective-permute-done((f32[49,8,128]{2,1,0:T(8,128)S(1)}, f32[49,8,128]{2,1,0:T(8,128)S(1)}, u32[]{:S(2)}, u32[]{:S(2)}) %collective-permute-start.5) | collective-permute-done | bytes 200736 | tf_op jit(solution)/shard_map/ppermute | solution.py:446
  30.3 0.1 pack_x2.1
  30.4 6.9 %collective-permute-start.6 = (f32[34,8,128]{2,1,0:T(8,128)S(1)}, f32[34,8,128]{2,1,0:T(8,128)S(1)}, u32[]{:S(2)}, u32[]{:S(2)}) collective-permute-start(f32[34,8,128]{2,1,0:T(8,128)S(1)} %get-tuple-element.19), channel_id=1, source_target_pairs={{0,32},{64,96},{128,160},{192,224},{256,288},{320,352},{384,416},{... | collective-permute-start | bytes 417800 | tf_op jit(solution)/shard_map/ppermute | solution.py:446
  37.4 0.7 collective-permute-start.7
  38.0 1.8 %collective-permute-done.6.e_even = f32[34,8,128]{2,1,0:T(8,128)S(1)} collective-permute-done((f32[34,8,128]{2,1,0:T(8,128)S(1)}, f32[34,8,128]{2,1,0:T(8,128)S(1)}, u32[]{:S(2)}, u32[]{:S(2)}) %collective-permute-start.6) | collective-permute-done | bytes 139296 | tf_op jit(solution)/shard_map/ppermute | solution.py:446
  39.9 19.2 %advance.1 = f32[32,4,384]{2,1,0:T(4,128)S(1)} custom-call(f32[4]{0:T(128)S(1)} %copy-done.9, f32[4,4]{1,0:T(4,128)S(1)} %copy-done.8, f32[4,8,32,128]{3,2,1,0:T(8,128)S(1)} %copy-done.1, f32[3,8,32,128]{3,2,1,0:T(8,128)S(1)} %copy-done.3, f32[8,32,128]{2,1,0:T(8,128)S(1)} %collective-permute-done.z_even, f32[8,32,128]{2,1,0:T(8,128)S(1)} %collective-permute-done.1.z_odd, ...), custom_call_target="tpu_custom_call" | custom-call | flops 10000000 | bytes 10000000 | tf_op jit(solution)/shard_map/advance/pallas_call | solution.py:466
  59.0 26.2 %all_to_all.14.parts = f32[32,4,384]{2,1,0:T(4,128)S(1)} all-to-all(f32[32,4,384]{2,1,0:T(4,128)S(1)} %advance.1), channel_id=1, replica_groups=mesh['gx'=16,'gy'=8,'gz'=4] {'gy','gz'}, dimensions={0} | all-to-all | bytes 393216 | tf_op jit(solution)/shard_map/all_to_all | solution.py:483
  85.2 0.2 contract_x.1
  85.4 19.4 %all_to_all.15 = f32[16,2,128]{2,1,0:T(2,128)S(1)} all-to-all(f32[16,2,128]{2,1,0:T(2,128)S(1)} %bitcast.5), channel_id=1, replica_groups=mesh['gx'=16,'gy'=8,'gz'=4] {'gx'}, dimensions={0} | all-to-all | bytes 32768 | tf_op jit(solution)/shard_map/all_to_all | solution.py:487
  104.8 0.1 reduce_sum.12
  104.9 0.6 copy.8
  (22 shorter events, 0.1 us)
Async XLA Ops:
  0.0 1.0 copy-start
  1.0 1.0 copy-start.2
  2.0 0.7 copy-start.4
  2.8 12.3 %copy-start.6 = (f32[32,32]{1,0:T(8,128)S(1)}, f32[32,32]{1,0:T(8,128)}, u32[]{:S(2)}) copy-start(f32[32,32]{1,0:T(8,128)} %fy.3) | copy-start | bytes 12292
  3.8 36.0 %collective-permute-start.2 = (f32[36,32,128]{2,1,0:T(8,128)S(1)}, f32[36,32,128]{2,1,0:T(8,128)S(1)}, u32[]{:S(2)}, u32[]{:S(2)}) collective-permute-start(f32[36,32,128]{2,1,0:T(8,128)S(1)} %get-tuple-element.15), channel_id=1, source_target_pairs={{0,32},{64,96},{128,160},{192,224},{256,288},{320,352},{384,416},{... | collective-permute-start | bytes 1769480 | tf_op jit(solution)/shard_map/ppermute | solution.py:446
  8.6 31.2 %collective-permute-start.3 = (f32[36,32,128]{2,1,0:T(8,128)S(1)}, f32[36,32,128]{2,1,0:T(8,128)S(1)}, u32[]{:S(2)}, u32[]{:S(2)}) collective-permute-start(f32[36,32,128]{2,1,0:T(8,128)S(1)} %get-tuple-element.16), channel_id=1, source_target_pairs={{32,64},{96,128},{160,192},{224,256},{288,320},{352,384},{416,448}... | collective-permute-start | bytes 1769480 | tf_op jit(solution)/shard_map/ppermute | solution.py:446
  9.3 5.7 %collective-permute-start = (f32[8,32,128]{2,1,0:T(8,128)S(1)}, f32[8,32,128]{2,1,0:T(8,128)S(1)}, u32[]{:S(2)}, u32[]{:S(2)}) collective-permute-start(f32[8,32,128]{2,1,0:T(8,128)S(1)} %get-tuple-element.13), channel_id=1, source_target_pairs={{0,1},{2,3},{1,0},{3,2},{4,5},{6,7},{5,4},{7,6},{8,9},{10,11},{9,8... | collective-permute-start | bytes 393224 | tf_op jit(solution)/shard_map/ppermute | solution.py:446
  12.5 2.6 %collective-permute-start.1 = (f32[8,32,128]{2,1,0:T(8,128)S(1)}, f32[8,32,128]{2,1,0:T(8,128)S(1)}, u32[]{:S(2)}, u32[]{:S(2)}) collective-permute-start(f32[8,32,128]{2,1,0:T(8,128)S(1)} %get-tuple-element.14), channel_id=1, source_target_pairs={{1,2},{2,1},{5,6},{6,5},{9,10},{10,9},{13,14},{14,13},{17,18},{18,... | collective-permute-start | bytes 393224 | tf_op jit(solution)/shard_map/ppermute | solution.py:446
  15.0 15.3 %copy-start.7 = (f32[8,32]{1,0:T(8,128)S(1)}, f32[8,32]{1,0:T(8,128)}, u32[]{:S(2)}) copy-start(f32[8,32]{1,0:T(8,128)} %fx.3) | copy-start | bytes 3076
  15.0 24.8 %copy-start.3 = (f32[3,8,32,128]{3,2,1,0:T(8,128)S(1)}, f32[3,8,32,128]{3,2,1,0:T(8,128)}, u32[]{:S(2)}) copy-start(f32[3,8,32,128]{3,2,1,0:T(8,128)} %v.5) | copy-start | bytes 1179652
  15.1 24.7 %copy-start.1 = (f32[4,8,32,128]{3,2,1,0:T(8,128)S(1)}, f32[4,8,32,128]{3,2,1,0:T(8,128)}, u32[]{:S(2)}) copy-start(f32[4,8,32,128]{3,2,1,0:T(8,128)} %f.5) | copy-start | bytes 1572868
  15.2 9.1 %collective-permute-start.4 = (f32[49,8,128]{2,1,0:T(8,128)S(1)}, f32[49,8,128]{2,1,0:T(8,128)S(1)}, u32[]{:S(2)}, u32[]{:S(2)}) collective-permute-start(f32[49,8,128]{2,1,0:T(8,128)S(1)} %get-tuple-element.17), channel_id=1, source_target_pairs={{0,4},{8,12},{16,20},{24,28},{4,0},{12,8},{20,16},{28,24},{1,5},{9... | collective-permute-start | bytes 602120 | tf_op jit(solution)/shard_map/ppermute | solution.py:446
  22.3 17.5 %copy-start.5 = (f32[128,32]{0,1:T(8,128)S(1)}, f32[128,32]{0,1:T(8,128)}, u32[]{:S(2)}) copy-start(f32[128,32]{0,1:T(8,128)} %param.13) | copy-start | bytes 49156
  22.3 8.0 %collective-permute-start.5 = (f32[49,8,128]{2,1,0:T(8,128)S(1)}, f32[49,8,128]{2,1,0:T(8,128)S(1)}, u32[]{:S(2)}, u32[]{:S(2)}) collective-permute-start(f32[49,8,128]{2,1,0:T(8,128)S(1)} %get-tuple-element.18), channel_id=1, source_target_pairs={{4,8},{12,16},{20,24},{8,4},{16,12},{24,20},{5,9},{13,17},{21,25},... | collective-permute-start | bytes 602120 | tf_op jit(solution)/shard_map/ppermute | solution.py:446
  30.4 9.4 %copy-start.8 = (f32[4,4]{1,0:T(4,128)S(1)}, f32[4,4]{1,0:T(4,128)}, u32[]{:S(2)}) copy-start(f32[4,4]{1,0:T(4,128)} %c.1) | copy-start | bytes 196
  30.4 9.4 %copy-start.9 = (f32[4]{0:T(128)S(1)}, f32[4]{0:T(128)}, u32[]{:S(2)}) copy-start(f32[4]{0:T(128)} %d.1) | copy-start | bytes 52
  30.4 9.4 %collective-permute-start.6 = (f32[34,8,128]{2,1,0:T(8,128)S(1)}, f32[34,8,128]{2,1,0:T(8,128)S(1)}, u32[]{:S(2)}, u32[]{:S(2)}) collective-permute-start(f32[34,8,128]{2,1,0:T(8,128)S(1)} %get-tuple-element.19), channel_id=1, source_target_pairs={{0,32},{64,96},{128,160},{192,224},{256,288},{320,352},{384,416},{... | collective-permute-start | bytes 417800 | tf_op jit(solution)/shard_map/ppermute | solution.py:446
  37.4 2.4 %collective-permute-start.7 = (f32[34,8,128]{2,1,0:T(8,128)S(1)}, f32[34,8,128]{2,1,0:T(8,128)S(1)}, u32[]{:S(2)}, u32[]{:S(2)}) collective-permute-start(f32[34,8,128]{2,1,0:T(8,128)S(1)} %get-tuple-element.20), channel_id=1, source_target_pairs={{32,64},{96,128},{160,192},{224,256},{288,320},{352,384},{416,448}... | collective-permute-start | bytes 417800 | tf_op jit(solution)/shard_map/ppermute | solution.py:446

commit v5 on v4

--- a/solution.py
+++ b/solution.py
@@ -5,6 +5,7 @@
 from jax.experimental.pallas import tpu as pltpu
 from jax.sharding import PartitionSpec as P
 
+
 TIME_STEP = 0.2
 F32 = jnp.float32
 PLANES, ROWS = 24, 64
@@ -23,7 +24,7 @@
     return jax.ShapeDtypeStruct(shape, F32)
 
 
-def call(kernel, out_shape, in_specs, name, scratch=(), work=1000000, mib=8):
+def call(kernel, out_shape, in_specs, scratch=(), work=1000000, mib=8):
     many = isinstance(out_shape, (list, tuple))
     return pl.pallas_call(
         kernel,
@@ -33,7 +34,6 @@
         scratch_shapes=list(scratch),
         compiler_params=pltpu.CompilerParams(vmem_limit_bytes=mib << 20),
         cost_estimate=pl.CostEstimate(flops=work, bytes_accessed=work, transcendentals=0),
-        name=name,
     )
 
 
@@ -67,7 +67,13 @@
     return 1 - odd, odd
 
 
-def pack_xz(f, v, fz, x_even, x_odd, z_even, z_odd):
+def pack_xz(f_in, v_in, fz_in, x_even, x_odd, z_even, z_odd, f, v, fz, arrived):
+    pairs = ((f_in, f), (v_in, v), (fz_in, fz))
+    copies = [pltpu.make_async_copy(a, b, arrived.at[n]) for n, (a, b) in enumerate(pairs)]
+    for copy in copies:
+        copy.start()
+    for copy in copies:
+        copy.wait()
     lane = lanes_of(32)
     for out, up in zip((x_even, x_odd), ways("gx")):
         for j in range(6):
@@ -387,6 +393,7 @@
                 face = jnp.where(kept, 0.5 * (dd[i] * ly - u_y * gy_), 0.0)
                 final[i, pl.ds(row, 8), 0:128] = face
                 final[i, pl.ds(row, 8), 128:256] = jnp.zeros((8, 128), F32)
+
     for i in range(4):
         first, second = section[i, 8, 16:48], section[i, 9, 16:48]
         last, before = section[i, 15, 16:48], section[i, 14, 16:48]
@@ -443,18 +450,23 @@
         last = lax.axis_size(axis) - 1
         pairs = [[(i, i + 1) for i in range(first, last, 2)] for first in (0, 1)]
         even_pairs, odd_pairs = ([*p, *((b, a) for a, b in p)] for p in pairs)
-        return lax.ppermute(even, axis, even_pairs), lax.ppermute(odd, axis, odd_pairs)
-
-    x_even, x_odd, z_even, z_odd = call(
-        pack_xz, [f32(36, 32, 128)] * 2 + [f32(8, 32, 128)] * 2, [vmem()] * 3, "pack_xz"
-    )(fields, velocity, factor_z.T)
-    x_even, x_odd = swapped("gx", x_even, x_odd)
+        even = lax.ppermute(even, axis, even_pairs)
+        return even, lax.ppermute(odd, axis, odd_pairs)
+
+    x_even, x_odd, z_even, z_odd, fields, velocity, fz = call(
+        pack_xz,
+        [f32(36, 32, 128)] * 2 + [f32(8, 32, 128)] * 2
+        + [f32(4, 8, 32, 128), f32(3, 8, 32, 128), f32(32, 128)],
+        [pl.BlockSpec(memory_space=pltpu.HBM)] * 3,
+        scratch=[pltpu.SemaphoreType.DMA((3,))],
+    )(*(pltpu.with_memory_space_constraint(a, pltpu.HBM) for a in (fields, velocity, factor_z.T)))
     z_even, z_odd = swapped("gz", z_even, z_odd)
-    y_even, y_odd = call(pack_y, [f32(49, 8, 128)] * 2, [vmem()] * 5, "pack_y")(
+    y_even, y_odd = call(pack_y, [f32(49, 8, 128)] * 2, [vmem()] * 5)(
         fields, velocity, factor_y, z_even, z_odd
     )
     y_even, y_odd = swapped("gy", y_even, y_odd)
-    e_even, e_odd = call(pack_x2, [f32(34, 8, 128)] * 2, [vmem()] * 5, "pack_x2")(
+    x_even, x_odd = swapped("gx", x_even, x_odd)
+    e_even, e_odd = call(pack_x2, [f32(34, 8, 128)] * 2, [vmem()] * 5)(
         z_even, z_odd, y_even, y_odd, factor_x
     )
     e_even, e_odd = swapped("gx", e_even, e_odd)
@@ -462,12 +474,11 @@
     def tiles(*lead):
         return pltpu.VMEM((*lead, ROWS, 128), F32)
 
-    gy, gz, gx = (lax.axis_size(n) for n in ("gy", "gz", "gx"))
+    _, _, gx = (lax.axis_size(n) for n in ("gy", "gz", "gx"))
     parts = call(
         advance,
         f32(32, 4, 384),
         [smem()] * 2 + [vmem()] * 12,
-        "advance",
         scratch=[
             tiles(4, PLANES), tiles(4, PLANES), tiles(PLANES), tiles(PLANES),
             tiles(3, PLANES), tiles(3, PLANES), tiles(PLANES),
@@ -478,12 +489,10 @@
         mib=24,
     )(
         diffusivity, coupling, fields, velocity, z_even, z_odd, x_even, x_odd, y_even, y_odd,
-        e_even, e_odd, factor_z.T, factor_y,
+        e_even, e_odd, fz, factor_y,
     )
     parts = lax.all_to_all(parts, ("gy", "gz"), 0, 0, tiled=True)
-    slices = call(contract_x, f32(32, 128), [vmem()] * 4, "contract_x")(
-        parts, factor_x, e_even, e_odd
-    )
+    slices = call(contract_x, f32(32, 128), [vmem()] * 4)(parts, factor_x, e_even, e_odd)
     slices = lax.all_to_all(slices, "gx", 0, 0, tiled=True)
     core = jnp.sum(slices.reshape(gx, 32 // gx, 4, 4, 8), axis=0)
     return core.transpose(2, 0, 1, 3)

time: 106 us -> 104 us (0.981)
  local copies, waits for them, and re-layouts: 3.5 us -> 0.73 us
  Pallas kernels: 20.5 us -> 21.7 us
    unnamed x20 -> x8, local copies, waits for them, and re-layouts: 2.79 us -> 0.02 us
    pallas_call x5, Pallas kernels: 20.5 us -> 21.7 us  [the longest x1 19.2 us: local(): call(advance, f32(32, 4, 384), [smem()] * 2 + [vmem()] * 12, scratch=[til...]
where the time goes in v5:
time: 104 us
  blocking collectives  45.6 us (44%)
  starting transfers between devices  25.8 us (25%)
  Pallas kernels  21.7 us (21%)
  waiting for transfers between devices  9.76 us (9%)
    all_to_all x1, blocking collectives, local(): parts = lax.all_to_all(parts, ('gy', 'gz'), 0, 0, tiled=True)  26.2 us
    ppermute x4, starting transfers between devices, swapped(): even = lax.ppermute(even, axis, even_pairs)  21.8 us
    all_to_all x1, blocking collectives, local(): slices = lax.all_to_all(slices, 'gx', 0, 0, tiled=True)  19.4 us
    pallas_call x1, Pallas kernels, local(): call(advance, f32(32, 4, 384), [smem()] * 2 + [vmem()] * 12, scratch=[til...  19.2 us
    ppermute x4, waiting for transfers between devices, swapped(): return (even, lax.ppermute(odd, axis, odd_pairs))  6.1 us
    ppermute x4, starting transfers between devices, swapped(): return (even, lax.ppermute(odd, axis, odd_pairs))  3.96 us
    ppermute x4, waiting for transfers between devices, swapped(): even = lax.ppermute(even, axis, even_pairs)  3.65 us
    pallas_call x1, Pallas kernels, local(): call(pack_xz, [f32(36, 32, 128)] * 2 + [f32(8, 32, 128)] * 2 + [f32(4, 8,...  2.22 us
  transfers between devices with their start and end apart: 8, of which 3 were waited for; matrix products, arithmetic and copies ran while one was open for 0% of the time, Pallas kernels for 0%

profile of v5, /device:TPU:1, one launch (start us, length us, event | category | flops | bytes accessed | tf_op | source)
XLA Modules:
  0.0 103.8 jit_solution(2519043392352503497)
XLA Ops:
  0.0 2.2 %shard_map.73 = (f32[36,32,128]{2,1,0:T(8,128)S(1)}, f32[36,32,128]{2,1,0:T(8,128)S(1)}, f32[8,32,128]{2,1,0:T(8,128)S(1)}, f32[8,32,128]{2,1,0:T(8,128)S(1)}, f...) custom-call(f32[4,8,32,128]{3,2,1,0:T(8,128)} %f_in.1, f32[3,8,32,128]{3,2,1,0:T(8,128)} %v_in.1, ...), custom_call_target="tpu_custom_call" | custom-call | flops 1000000 | bytes 1000000 | tf_op jit(solution)/shard_map/pallas_call | solution.py:456
  2.2 4.8 %collective-permute-start.2 = (f32[36,32,128]{2,1,0:T(8,128)S(1)}, f32[36,32,128]{2,1,0:T(8,128)S(1)}, u32[]{:S(2)}, u32[]{:S(2)}) collective-permute-start(f32[36,32,128]{2,1,0:T(8,128)S(1)} %get-tuple-element.20), channel_id=1, source_target_pairs={{0,32},{64,96},{128,160},{192,224},{256,288},{320,352},{384,416},{... | collective-permute-start | bytes 1769480 | tf_op jit(solution)/shard_map/ppermute | solution.py:453
  7.1 0.7 collective-permute-start.3
  7.8 3.1 %collective-permute-start = (f32[8,32,128]{2,1,0:T(8,128)S(1)}, f32[8,32,128]{2,1,0:T(8,128)S(1)}, u32[]{:S(2)}, u32[]{:S(2)}) collective-permute-start(f32[8,32,128]{2,1,0:T(8,128)S(1)} %get-tuple-element.18), channel_id=1, source_target_pairs={{0,1},{2,3},{1,0},{3,2},{4,5},{6,7},{5,4},{7,6},{8,9},{10,11},{9,8... | collective-permute-start | bytes 393224 | tf_op jit(solution)/shard_map/ppermute | solution.py:453
  10.9 0.7 collective-permute-start.1
  11.6 1.9 %collective-permute-done.z_even = f32[8,32,128]{2,1,0:T(8,128)S(1)} collective-permute-done((f32[8,32,128]{2,1,0:T(8,128)S(1)}, f32[8,32,128]{2,1,0:T(8,128)S(1)}, u32[]{:S(2)}, u32[]{:S(2)}) %collective-permute-start) | collective-permute-done | bytes 131104 | tf_op jit(solution)/shard_map/ppermute | solution.py:453
  13.5 0.0 collective-permute-done.1.z_odd
  13.5 0.1 shard_map.74
  13.6 7.0 %collective-permute-start.4 = (f32[49,8,128]{2,1,0:T(8,128)S(1)}, f32[49,8,128]{2,1,0:T(8,128)S(1)}, u32[]{:S(2)}, u32[]{:S(2)}) collective-permute-start(f32[49,8,128]{2,1,0:T(8,128)S(1)} %get-tuple-element.22), channel_id=1, source_target_pairs={{0,4},{8,12},{16,20},{24,28},{4,0},{12,8},{20,16},{28,24},{1,5},{9... | collective-permute-start | bytes 602120 | tf_op jit(solution)/shard_map/ppermute | solution.py:453
  20.6 1.9 %collective-permute-start.5 = (f32[49,8,128]{2,1,0:T(8,128)S(1)}, f32[49,8,128]{2,1,0:T(8,128)S(1)}, u32[]{:S(2)}, u32[]{:S(2)}) collective-permute-start(f32[49,8,128]{2,1,0:T(8,128)S(1)} %get-tuple-element.23), channel_id=1, source_target_pairs={{4,8},{12,16},{20,24},{8,4},{16,12},{24,20},{5,9},{13,17},{21,25},... | collective-permute-start | bytes 602120 | tf_op jit(solution)/shard_map/ppermute | solution.py:454
  22.5 6.1 %collective-permute-done.5.y_odd = f32[49,8,128]{2,1,0:T(8,128)S(1)} collective-permute-done((f32[49,8,128]{2,1,0:T(8,128)S(1)}, f32[49,8,128]{2,1,0:T(8,128)S(1)}, u32[]{:S(2)}, u32[]{:S(2)}) %collective-permute-start.5) | collective-permute-done | bytes 200736 | tf_op jit(solution)/shard_map/ppermute | solution.py:454
  28.6 0.1 shard_map.75
  28.7 0.0 copy-start.2
  28.7 6.9 %collective-permute-start.6 = (f32[34,8,128]{2,1,0:T(8,128)S(1)}, f32[34,8,128]{2,1,0:T(8,128)S(1)}, u32[]{:S(2)}, u32[]{:S(2)}) collective-permute-start(f32[34,8,128]{2,1,0:T(8,128)S(1)} %get-tuple-element.24), channel_id=1, source_target_pairs={{0,32},{64,96},{128,160},{192,224},{256,288},{320,352},{384,416},{... | collective-permute-start | bytes 417800 | tf_op jit(solution)/shard_map/ppermute | solution.py:453
  35.6 0.0 copy-start.3
  35.6 0.7 collective-permute-start.7
  36.3 1.7 %collective-permute-done.6.e_even = f32[34,8,128]{2,1,0:T(8,128)S(1)} collective-permute-done((f32[34,8,128]{2,1,0:T(8,128)S(1)}, f32[34,8,128]{2,1,0:T(8,128)S(1)}, u32[]{:S(2)}, u32[]{:S(2)}) %collective-permute-start.6) | collective-permute-done | bytes 139296 | tf_op jit(solution)/shard_map/ppermute | solution.py:453
  38.1 0.0 collective-permute-done.3.x_odd
  38.1 19.2 %shard_map.76 = f32[32,4,384]{2,1,0:T(4,128)S(1)} custom-call(f32[4]{0:T(128)S(1)} %copy-done.3, f32[4,4]{1,0:T(4,128)S(1)} %copy-done.2, f32[4,8,32,128]{3,2,1,0:T(8,128)S(1)} %get-tuple-element.16.f, f32[3,8,32,128]{3,2,1,0:T(8,128)S(1)} %get-tuple-element.17.v, f32[8,32,128]{2,1,0:T(8,128)S(1)} %collective-permute-done.z_even, ...), custom_call_target="tpu_custom_call" | custom-call | flops 10000000 | bytes 10000000 | tf_op jit(solution)/shard_map/pallas_call | solution.py:478
  57.3 26.2 %all_to_all.14.parts = f32[32,4,384]{2,1,0:T(4,128)S(1)} all-to-all(f32[32,4,384]{2,1,0:T(4,128)S(1)} %shard_map.76), channel_id=1, replica_groups=mesh['gx'=16,'gy'=8,'gz'=4] {'gy','gz'}, dimensions={0} | all-to-all | bytes 393216 | tf_op jit(solution)/shard_map/all_to_all | solution.py:494
  83.4 0.2 shard_map.77
  83.6 19.4 %all_to_all.15 = f32[16,2,128]{2,1,0:T(2,128)S(1)} all-to-all(f32[16,2,128]{2,1,0:T(2,128)S(1)} %bitcast.3), channel_id=1, replica_groups=mesh['gx'=16,'gy'=8,'gz'=4] {'gx'}, dimensions={0} | all-to-all | bytes 32768 | tf_op jit(solution)/shard_map/all_to_all | solution.py:496
  103.1 0.1 reduce_sum.12
  103.2 0.6 copy.8
  (10 shorter events, 0.0 us)
Async XLA Ops:
  0.0 13.5 %copy-start = (f32[32,32]{1,0:T(8,128)S(1)}, f32[32,32]{1,0:T(8,128)}, u32[]{:S(2)}) copy-start(f32[32,32]{1,0:T(8,128)} %fy.3) | copy-start | bytes 12292
  2.2 35.8 %collective-permute-start.2 = (f32[36,32,128]{2,1,0:T(8,128)S(1)}, f32[36,32,128]{2,1,0:T(8,128)S(1)}, u32[]{:S(2)}, u32[]{:S(2)}) collective-permute-start(f32[36,32,128]{2,1,0:T(8,128)S(1)} %get-tuple-element.20), channel_id=1, source_target_pairs={{0,32},{64,96},{128,160},{192,224},{256,288},{320,352},{384,416},{... | collective-permute-start | bytes 1769480 | tf_op jit(solution)/shard_map/ppermute | solution.py:453
  7.1 31.0 %collective-permute-start.3 = (f32[36,32,128]{2,1,0:T(8,128)S(1)}, f32[36,32,128]{2,1,0:T(8,128)S(1)}, u32[]{:S(2)}, u32[]{:S(2)}) collective-permute-start(f32[36,32,128]{2,1,0:T(8,128)S(1)} %get-tuple-element.21), channel_id=1, source_target_pairs={{32,64},{96,128},{160,192},{224,256},{288,320},{352,384},{416,448}... | collective-permute-start | bytes 1769480 | tf_op jit(solution)/shard_map/ppermute | solution.py:454
  7.8 5.7 %collective-permute-start = (f32[8,32,128]{2,1,0:T(8,128)S(1)}, f32[8,32,128]{2,1,0:T(8,128)S(1)}, u32[]{:S(2)}, u32[]{:S(2)}) collective-permute-start(f32[8,32,128]{2,1,0:T(8,128)S(1)} %get-tuple-element.18), channel_id=1, source_target_pairs={{0,1},{2,3},{1,0},{3,2},{4,5},{6,7},{5,4},{7,6},{8,9},{10,11},{9,8... | collective-permute-start | bytes 393224 | tf_op jit(solution)/shard_map/ppermute | solution.py:453
  10.9 2.6 %collective-permute-start.1 = (f32[8,32,128]{2,1,0:T(8,128)S(1)}, f32[8,32,128]{2,1,0:T(8,128)S(1)}, u32[]{:S(2)}, u32[]{:S(2)}) collective-permute-start(f32[8,32,128]{2,1,0:T(8,128)S(1)} %get-tuple-element.19), channel_id=1, source_target_pairs={{1,2},{2,1},{5,6},{6,5},{9,10},{10,9},{13,14},{14,13},{17,18},{18,... | collective-permute-start | bytes 393224 | tf_op jit(solution)/shard_map/ppermute | solution.py:454
  13.5 15.1 %copy-start.1 = (f32[8,32]{1,0:T(8,128)S(1)}, f32[8,32]{1,0:T(8,128)}, u32[]{:S(2)}) copy-start(f32[8,32]{1,0:T(8,128)} %fx.3) | copy-start | bytes 3076
  13.6 8.9 %collective-permute-start.4 = (f32[49,8,128]{2,1,0:T(8,128)S(1)}, f32[49,8,128]{2,1,0:T(8,128)S(1)}, u32[]{:S(2)}, u32[]{:S(2)}) collective-permute-start(f32[49,8,128]{2,1,0:T(8,128)S(1)} %get-tuple-element.22), channel_id=1, source_target_pairs={{0,4},{8,12},{16,20},{24,28},{4,0},{12,8},{20,16},{28,24},{1,5},{9... | collective-permute-start | bytes 602120 | tf_op jit(solution)/shard_map/ppermute | solution.py:453
  20.6 8.0 %collective-permute-start.5 = (f32[49,8,128]{2,1,0:T(8,128)S(1)}, f32[49,8,128]{2,1,0:T(8,128)S(1)}, u32[]{:S(2)}, u32[]{:S(2)}) collective-permute-start(f32[49,8,128]{2,1,0:T(8,128)S(1)} %get-tuple-element.23), channel_id=1, source_target_pairs={{4,8},{12,16},{20,24},{8,4},{16,12},{24,20},{5,9},{13,17},{21,25},... | collective-permute-start | bytes 602120 | tf_op jit(solution)/shard_map/ppermute | solution.py:454
  28.7 9.4 %copy-start.2 = (f32[4,4]{1,0:T(4,128)S(1)}, f32[4,4]{1,0:T(4,128)}, u32[]{:S(2)}) copy-start(f32[4,4]{1,0:T(4,128)} %c.1) | copy-start | bytes 196
  28.7 9.3 %collective-permute-start.6 = (f32[34,8,128]{2,1,0:T(8,128)S(1)}, f32[34,8,128]{2,1,0:T(8,128)S(1)}, u32[]{:S(2)}, u32[]{:S(2)}) collective-permute-start(f32[34,8,128]{2,1,0:T(8,128)S(1)} %get-tuple-element.24), channel_id=1, source_target_pairs={{0,32},{64,96},{128,160},{192,224},{256,288},{320,352},{384,416},{... | collective-permute-start | bytes 417800 | tf_op jit(solution)/shard_map/ppermute | solution.py:453
  35.6 2.5 %copy-start.3 = (f32[4]{0:T(128)S(1)}, f32[4]{0:T(128)}, u32[]{:S(2)}) copy-start(f32[4]{0:T(128)} %d.1) | copy-start | bytes 52
  35.6 2.4 %collective-permute-start.7 = (f32[34,8,128]{2,1,0:T(8,128)S(1)}, f32[34,8,128]{2,1,0:T(8,128)S(1)}, u32[]{:S(2)}, u32[]{:S(2)}) collective-permute-start(f32[34,8,128]{2,1,0:T(8,128)S(1)} %get-tuple-element.25), channel_id=1, source_target_pairs={{32,64},{96,128},{160,192},{224,256},{288,320},{352,384},{416,448}... | collective-permute-start | bytes 417800 | tf_op jit(solution)/shard_map/ppermute | solution.py:454

commit v6 on v5

--- a/solution.py
+++ b/solution.py
@@ -24,7 +24,7 @@
     return jax.ShapeDtypeStruct(shape, F32)
 
 
-def call(kernel, out_shape, in_specs, scratch=(), work=1000000, mib=8):
+def call(kernel, out_shape, in_specs, scratch=(), work=1000000, mib=8, aliases=None):
     many = isinstance(out_shape, (list, tuple))
     return pl.pallas_call(
         kernel,
@@ -32,6 +32,7 @@
         in_specs=in_specs,
         out_specs=[vmem() for _ in out_shape] if many else vmem(),
         scratch_shapes=list(scratch),
+        input_output_aliases=aliases or {},
         compiler_params=pltpu.CompilerParams(vmem_limit_bytes=mib << 20),
         cost_estimate=pl.CostEstimate(flops=work, bytes_accessed=work, transcendentals=0),
     )
@@ -157,110 +158,61 @@
         out[33] = padded(fx[...])
 
 
-def advance(
-    d, c, f, v, z_even, z_odd, x_even, x_odd, y_even, y_odd, e_even, e_odd, fz, fy,
-    out, state, section, edge, edge2, wind, edge_wind, zm, final, faces, mixed, rhs, fye,
-):
-    gx, gy, gz = (lax.axis_index(n) for n in ("gx", "gy", "gz"))
-    last_x, last_y, last_z = (lax.axis_size(n) - 1 for n in ("gx", "gy", "gz"))
-    x_first, x_end = jnp.where(gx == 0, LOW, 0), jnp.where(gx == last_x, HIGH, PLANES)
-    y_first, y_end = jnp.where(gy == 0, 16, 0), jnp.where(gy == last_y, 48, ROWS)
-    scale = TIME_STEP / 12.0
-
-    y_low, y_high = sides("gy", y_even, y_odd)
-    even_up, odd_up = ways("gx")
+FULL, OWN = (8, 24, 40), (16, 32)
+SCALE = TIME_STEP / 12.0
+
+
+def chunk(rows):
+    lane = lanes_of(rows)
+    return lane, lane % 32, lax.broadcasted_iota(jnp.int32, (rows, 128), 0)
+
+
+def roll(value, by):
+    return pltpu.roll(value, by % 128, 1)
+
+
+def slabs(state, wind, zm, edge, edge_wind, x, r, rows, winds):
+    lane, in_group, _ = chunk(rows)
+    halo = zm[x, r : r + rows]
+    tile = halo
     for i in range(4):
-        for x in range(8):
-            state[i, 8 + x, 16:48] = f[i, x]
-            state[i, 8 + x, 8:16] = y_low(i * 8 + x)
-            state[i, 8 + x, 48:56] = y_high(i * 8 + x)
-        for halo, above in ((x_even, even_up), (x_odd, odd_up)):
-            for j in range(6):
-                state[i, 2 + 14 * above + j, 16:48] = halo[i * 6 + j]
-        for e, above in ((e_even, even_up), (e_odd, odd_up)):
-            near, far = 6 + 10 * above, 4 + 14 * above
-            for j in range(2):
-                state[i, near + j, 12:16] = e[i * 2, 4 * j : 4 * j + 4]
-                state[i, near + j, 48:52] = e[i * 2 + 1, 4 * j : 4 * j + 4]
-                at = 4 * (i % 2) + 2 * j
-                state[i, far + j, 14:16] = e[8 + i // 2 * 2, at : at + 2]
-                state[i, far + j, 48:50] = e[9 + i // 2 * 2, at : at + 2]
-    for a in range(3):
-        for x in range(8):
-            half_tile = slice(4 * (x % 2), 4 * (x % 2) + 4)
-            wind[a, 8 + x, 16:48] = v[a, x] * scale
-            wind[a, 8 + x, 12:16] = y_low(32 + a * 4 + x // 2, half_tile) * scale
-            wind[a, 8 + x, 48:52] = y_high(32 + a * 4 + x // 2, half_tile) * scale
-        for halo, above in ((x_even, even_up), (x_odd, odd_up)):
-            for j in range(4):
-                wind[a, 4 + 12 * above + j, 16:48] = halo[24 + a * 4 + j] * scale
-        for e, above in ((e_even, even_up), (e_odd, odd_up)):
-            near = 6 + 10 * above
-            for j in range(2):
-                at = 4 * (a % 2) + 2 * j
-                wind[a, near + j, 14:16] = e[12 + a // 2 * 2, at : at + 2] * scale
-                wind[a, near + j, 48:50] = e[13 + a // 2 * 2, at : at + 2] * scale
-    for x in range(8):
-        half_tile = slice(4 * (x % 2), 4 * (x % 2) + 4)
-        zm[8 + x, 16:48] = z_even[x] + z_odd[x]
-        zm[8 + x, 12:16] = y_low(44 + x // 2, half_tile)
-        zm[8 + x, 48:52] = y_high(44 + x // 2, half_tile)
-    for e, above in ((e_even, even_up), (e_odd, odd_up)):
-        near, first = 6 + 10 * above, 4 + 12 * above
-        for j in range(4):
-            for t in range(4):
-                zm[first + j, 16 + 8 * t : 24 + 8 * t] = e[16 + j * 4 + t]
-        for j in range(2):
-            zm[near + j, 14:16] = e[32, 2 * j : 2 * j + 2]
-            zm[near + j, 48:50] = e[32, 4 + 2 * j : 6 + 2 * j]
-
-    def chunk(rows):
-        lane = lanes_of(rows)
-        return lane, lane % 32, lax.broadcasted_iota(jnp.int32, (rows, 128), 0)
-
-    def roll(value, by):
-        return pltpu.roll(value, by % 128, 1)
-
-    def slabs(x, r, rows, winds):
-        lane, in_group, _ = chunk(rows)
-        halo = zm[x, r : r + rows]
-        tile = halo
-        for i in range(4):
-            q = state[i, x, r : r + rows]
-            tile = jnp.where(within(lane, 32 * i + 8, 8), roll(q, 32 * i + 8), tile)
-            tile = jnp.where(within(lane, 32 * i + 16, 8), roll(q, 32 * i + 24), tile)
-        edge[x, r : r + rows] = tile
-        if winds:
-            halo = halo * scale
-            packed = jnp.where(in_group < 8, roll(halo, -8), roll(halo, 8))
-            for a in range(3):
-                q = wind[a, x, r : r + rows]
-                packed = jnp.where(within(lane, 32 * a + 8, 8), roll(q, 32 * a + 8), packed)
-                packed = jnp.where(within(lane, 32 * a + 16, 8), roll(q, 32 * a + 24), packed)
-            for a in range(3):
-                one = jnp.where(within(lane, 32 * a, 32), packed, 0.0)
-                one = one + roll(one, 32)
-                edge_wind[a, x, r : r + rows] = one + roll(one, 64)
-
-    full, own = (8, 24, 40), (16, 32)
-
-    @pl.loop(6, 18)
-    def _(x):
-        for r in full:
-            slabs(x, r, 16, True)
-
-    @pl.loop(0, 4)
-    def _(j):
-        for r in own:
-            slabs(jnp.where(j < 2, 4 + j, 16 + j), r, 16, False)
-
-    dd = [d[i] * TIME_STEP for i in range(4)]
-    cc = [[c[i, w] * TIME_STEP for w in range(4)] for i in range(4)]
-
-    def terms(plus, minus, plus2, minus2):
-        return 8.0 * (plus - minus) - (plus2 - minus2), plus + minus
-
-    def tendencies(src, slab, x, r, rows):
+        q = state[i, x, r : r + rows]
+        tile = jnp.where(within(lane, 32 * i + 8, 8), roll(q, 32 * i + 8), tile)
+        tile = jnp.where(within(lane, 32 * i + 16, 8), roll(q, 32 * i + 24), tile)
+    edge[x, r : r + rows] = tile
+    if winds:
+        halo = halo * SCALE
+        packed = jnp.where(in_group < 8, roll(halo, -8), roll(halo, 8))
+        for a in range(3):
+            q = wind[a, x, r : r + rows]
+            packed = jnp.where(within(lane, 32 * a + 8, 8), roll(q, 32 * a + 8), packed)
+            packed = jnp.where(within(lane, 32 * a + 16, 8), roll(q, 32 * a + 24), packed)
+        for a in range(3):
+            one = jnp.where(within(lane, 32 * a, 32), packed, 0.0)
+            one = one + roll(one, 32)
+            edge_wind[a, x, r : r + rows] = one + roll(one, 64)
+
+
+def terms(plus, minus, plus2, minus2):
+    return 8.0 * (plus - minus) - (plus2 - minus2), plus + minus
+
+
+def half(base, q, t):
+    return 0.5 * (base + q + t)
+
+
+class Stencil:
+    def __init__(self, d, c, wind, edge_wind):
+        self.wind, self.edge_wind = wind, edge_wind
+        self.dd = [d[i] * TIME_STEP for i in range(4)]
+        self.cc = [[c[i, w] * TIME_STEP for w in range(4)] for i in range(4)]
+        gx, gy, self.gz = (lax.axis_index(n) for n in ("gx", "gy", "gz"))
+        last_x, last_y, self.last_z = (lax.axis_size(n) - 1 for n in ("gx", "gy", "gz"))
+        self.x_first, self.x_end = jnp.where(gx == 0, LOW, 0), jnp.where(gx == last_x, HIGH, PLANES)
+        self.y_first, self.y_end = jnp.where(gy == 0, 16, 0), jnp.where(gy == last_y, 48, ROWS)
+
+    def tendencies(self, src, slab, x, r, rows):
+        dd, cc, wind = self.dd, self.cc, self.wind
         lane, in_group, _ = chunk(rows)
         at = slice(r, r + rows)
         u = [wind[a, x, at] for a in range(3)]
@@ -283,7 +235,8 @@
             results.append(dd[i] * (lx + ly + lz) - moved + q[i] * (mix - 6.0 * dd[i]))
         return q, results
 
-    def slab_tendency(slab, x, r, rows):
+    def slab_tendency(self, slab, x, r, rows):
+        dd, cc, edge_wind = self.dd, self.cc, self.edge_wind
         lane, _, _ = chunk(rows)
         group = lane // 32
         at = slice(r, r + rows)
@@ -302,33 +255,118 @@
         moved = edge_wind[0, x, at] * gx_ + edge_wind[1, x, at] * gy_ + edge_wind[2, x, at] * gz_
         return q, by_group(dd) * (lx + ly + lz) - moved + q * mix
 
-    def inside(x, r, rows):
+    def inside(self, x, r, rows):
         _, in_group, row = chunk(rows)
-        first = jnp.where((x >= x_first) & (x < x_end), y_first, ROWS)
-        ok = (row + r >= first) & (row + r < y_end)
-        z_ok = ((in_group >= 8) | (gz != 0)) & ((in_group < 24) | (gz != last_z))
+        first = jnp.where((x >= self.x_first) & (x < self.x_end), self.y_first, ROWS)
+        ok = (row + r >= first) & (row + r < self.y_end)
+        z_ok = ((in_group >= 8) | (self.gz != 0)) & ((in_group < 24) | (self.gz != self.last_z))
         return ok, z_ok
 
-    def half(base, q, t):
-        return 0.5 * (base + q + t)
-
-    def stage(x, rows_at, slab_rows, src, slab, dst, slab_dst, mean):
+    def stage(self, x, rows_at, slab_rows, src, slab, dst, slab_dst, mean):
         for r in rows_at:
             at = slice(r, r + 16)
-            ok, _ = inside(x, r, 16)
-            q, t = tendencies(src, slab, x, r, 16)
+            ok, _ = self.inside(x, r, 16)
+            q, t = self.tendencies(src, slab, x, r, 16)
             for i in range(4):
                 new = half(dst[i, x, at], q[i], t[i]) if mean else q[i] + t[i]
                 dst[i, x, at] = jnp.where(ok, new, 0.0)
         for r in slab_rows:
             at = slice(r, r + 16)
-            ok, z_ok = inside(x, r, 16)
-            q, t = slab_tendency(slab, x, r, 16)
+            ok, z_ok = self.inside(x, r, 16)
+            q, t = self.slab_tendency(slab, x, r, 16)
             new = half(slab_dst[x, at], q, t) if mean else q + t
             slab_dst[x, at] = jnp.where(ok & z_ok, new, 0.0)
 
-    @pl.loop(6, 18)
+
+def prepare(
+    d, c, f, v, z_even, z_odd, y_even, y_odd, fz, fy,
+    state, section, edge, edge2, wind, edge_wind, zm, rhs, fye,
+):
+    y_low, y_high = sides("gy", y_even, y_odd)
+    for i in range(4):
+        for x in range(8):
+            state[i, 8 + x, 16:48] = f[i, x]
+            state[i, 8 + x, 8:16] = y_low(i * 8 + x)
+            state[i, 8 + x, 48:56] = y_high(i * 8 + x)
+    for x in range(8):
+        half_tile = slice(4 * (x % 2), 4 * (x % 2) + 4)
+        for a in range(3):
+            wind[a, 8 + x, 16:48] = v[a, x] * SCALE
+            wind[a, 8 + x, 12:16] = y_low(32 + a * 4 + x // 2, half_tile) * SCALE
+            wind[a, 8 + x, 48:52] = y_high(32 + a * 4 + x // 2, half_tile) * SCALE
+        zm[8 + x, 16:48] = z_even[x] + z_odd[x]
+        zm[8 + x, 12:16] = y_low(44 + x // 2, half_tile)
+        zm[8 + x, 48:52] = y_high(44 + x // 2, half_tile)
+    lane = lanes_of(32)
+    outer = jnp.where((lane >= 126) | (lane < 2), roll(zm[8, 16:48], 16), 0.0)
+    rhs[...] = jnp.zeros((4, 128, 256), F32)
+    for i in range(4):
+        for k in range(4):
+            at = slice(32 * k + 8 * i, 32 * k + 8 * i + 8)
+            rhs[i, at, 0:128] = fz[8 * k : 8 * k + 8]
+            rhs[i, at, 128:256] = outer[8 * k : 8 * k + 8]
+    fye[0:8] = y_low(48, slice(0, 8), slice(0, 32))
+    fye[8:40] = fy[...]
+    fye[40:48] = y_high(48, slice(0, 8), slice(0, 32))
+
+    @pl.loop(8, 16)
     def _(x):
+        for r in FULL:
+            slabs(state, wind, zm, edge, edge_wind, x, r, 16, True)
+
+    stencil = Stencil(d, c, wind, edge_wind)
+
+    @pl.loop(10, 14)
+    def _(x):
+        stencil.stage(x, FULL, FULL, state, edge, section, edge2, False)
+
+
+def advance(
+    d, c, x_even, x_odd, e_even, e_odd, fy, rhs, fye, *refs
+):
+    out, state, section, edge, edge2, wind, edge_wind, zm, final, faces, mixed = refs[7:]
+    stencil = Stencil(d, c, wind, edge_wind)
+    dd, cc, stage, scale = stencil.dd, stencil.cc, stencil.stage, SCALE
+    full, own = FULL, OWN
+    even_up, odd_up = ways("gx")
+    for halo, above in ((x_even, even_up), (x_odd, odd_up)):
+        for j in range(6):
+            for i in range(4):
+                state[i, 2 + 14 * above + j, 16:48] = halo[i * 6 + j]
+        for j in range(4):
+            for a in range(3):
+                wind[a, 4 + 12 * above + j, 16:48] = halo[24 + a * 4 + j] * scale
+    for e, above in ((e_even, even_up), (e_odd, odd_up)):
+        near, far, first = 6 + 10 * above, 4 + 14 * above, 4 + 12 * above
+        for j in range(2):
+            for i in range(4):
+                state[i, near + j, 12:16] = e[i * 2, 4 * j : 4 * j + 4]
+                state[i, near + j, 48:52] = e[i * 2 + 1, 4 * j : 4 * j + 4]
+                at = 4 * (i % 2) + 2 * j
+                state[i, far + j, 14:16] = e[8 + i // 2 * 2, at : at + 2]
+                state[i, far + j, 48:50] = e[9 + i // 2 * 2, at : at + 2]
+            for a in range(3):
+                at = 4 * (a % 2) + 2 * j
+                wind[a, near + j, 14:16] = e[12 + a // 2 * 2, at : at + 2] * scale
+                wind[a, near + j, 48:50] = e[13 + a // 2 * 2, at : at + 2] * scale
+            zm[near + j, 14:16] = e[32, 2 * j : 2 * j + 2]
+            zm[near + j, 48:50] = e[32, 4 + 2 * j : 6 + 2 * j]
+        for j in range(4):
+            for t in range(4):
+                zm[first + j, 16 + 8 * t : 24 + 8 * t] = e[16 + j * 4 + t]
+
+    @pl.loop(0, 4)
+    def _(j):
+        x = jnp.where(j < 2, 6 + j, 14 + j)
+        for r in full:
+            slabs(state, wind, zm, edge, edge_wind, x, r, 16, True)
+        x = jnp.where(j < 2, 4 + j, 16 + j)
+        for r in own:
+            slabs(state, wind, zm, edge, edge_wind, x, r, 16, False)
+
+    @pl.loop(0, 8)
+    def _(j):
+        x = jnp.where(j < 4, 6 + j, 10 + j)
         stage(x, full, full, state, edge, section, edge2, False)
 
     @pl.loop(0, 4)
@@ -403,17 +441,6 @@
         faces[i, 64:96] = 0.5 * (dd[i] * last + u[2] * (8.0 * last - before))
         faces[i, 96:128] = -0.5 * (u[3] * last)
 
-    lane32 = lanes_of(32)
-    outer = jnp.where((lane32 >= 126) | (lane32 < 2), roll(zm[8, 16:48], 16), 0.0)
-    rhs[...] = jnp.zeros((4, 128, 256), F32)
-    for i in range(4):
-        for k in range(4):
-            at = slice(32 * k + 8 * i, 32 * k + 8 * i + 8)
-            rhs[i, at, 0:128] = fz[8 * k : 8 * k + 8]
-            rhs[i, at, 128:256] = outer[8 * k : 8 * k + 8]
-    fye[0:8] = y_low(48, slice(0, 8), slice(0, 32))
-    fye[8:40] = fy[...]
-    fye[40:48] = y_high(48, slice(0, 8), slice(0, 32))
     total = dot(final[0], rhs[0], 1, 1)
     total_faces = dot(faces[0], rhs[0, :, 0:128], 1, 1)
     for i in range(1, 4):
@@ -461,38 +488,37 @@
         scratch=[pltpu.SemaphoreType.DMA((3,))],
     )(*(pltpu.with_memory_space_constraint(a, pltpu.HBM) for a in (fields, velocity, factor_z.T)))
     z_even, z_odd = swapped("gz", z_even, z_odd)
-    y_even, y_odd = call(pack_y, [f32(49, 8, 128)] * 2, [vmem()] * 5)(
-        fields, velocity, factor_y, z_even, z_odd
-    )
+    y_even, y_odd = call(pack_y, [f32(49, 8, 128)] * 2, [vmem()] * 5)(fields, velocity, factor_y, z_even, z_odd)
     y_even, y_odd = swapped("gy", y_even, y_odd)
     x_even, x_odd = swapped("gx", x_even, x_odd)
-    e_even, e_odd = call(pack_x2, [f32(34, 8, 128)] * 2, [vmem()] * 5)(
-        z_even, z_odd, y_even, y_odd, factor_x
-    )
+    e_even, e_odd = call(pack_x2, [f32(34, 8, 128)] * 2, [vmem()] * 5)(z_even, z_odd, y_even, y_odd, factor_x)
     e_even, e_odd = swapped("gx", e_even, e_odd)
 
     def tiles(*lead):
-        return pltpu.VMEM((*lead, ROWS, 128), F32)
-
-    _, _, gx = (lax.axis_size(n) for n in ("gy", "gz", "gx"))
-    parts = call(
+        return f32(*lead, ROWS, 128)
+
+    gx = lax.axis_size("gx")
+    buffers = [
+        tiles(4, PLANES), tiles(4, PLANES), tiles(PLANES), tiles(PLANES),
+        tiles(3, PLANES), tiles(3, PLANES), tiles(PLANES),
+    ]
+    *filled, rhs, fye = call(
+        prepare, [*buffers, f32(4, 128, 256), f32(48, 32)], [smem()] * 2 + [vmem()] * 8, work=3000000
+    )(diffusivity, coupling, fields, velocity, z_even, z_odd, y_even, y_odd, fz, factor_y)
+    parts, *_ = call(
         advance,
-        f32(32, 4, 384),
-        [smem()] * 2 + [vmem()] * 12,
+        [f32(32, 4, 384), *buffers],
+        [smem()] * 2 + [vmem()] * 14,
         scratch=[
-            tiles(4, PLANES), tiles(4, PLANES), tiles(PLANES), tiles(PLANES),
-            tiles(3, PLANES), tiles(3, PLANES), tiles(PLANES),
-            pltpu.VMEM((4, 384, 256), F32), pltpu.VMEM((4, 128, 128), F32), pltpu.VMEM((384, 128), F32),
-            pltpu.VMEM((4, 128, 256), F32), pltpu.VMEM((48, 32), F32),
+            pltpu.VMEM((4, 384, 256), F32), pltpu.VMEM((4, 128, 128), F32), pltpu.VMEM((384, 128), F32)
         ],
         work=10000000,
-        mib=24,
-    )(
-        diffusivity, coupling, fields, velocity, z_even, z_odd, x_even, x_odd, y_even, y_odd,
-        e_even, e_odd, fz, factor_y,
+        aliases={9 + n: 1 + n for n in range(7)},
+    )(diffusivity, coupling, x_even, x_odd, e_even, e_odd, factor_y, rhs, fye, *filled)
+    parts = lax.all_to_all(parts, ("gy", "gz"), 0, 0, tiled=True)
+    slices = call(contract_x, f32(32, 128), [vmem()] * 4)(
+        parts, factor_x, e_even, e_odd
     )
-    parts = lax.all_to_all(parts, ("gy", "gz"), 0, 0, tiled=True)
-    slices = call(contract_x, f32(32, 128), [vmem()] * 4)(parts, factor_x, e_even, e_odd)
     slices = lax.all_to_all(slices, "gx", 0, 0, tiled=True)
     core = jnp.sum(slices.reshape(gx, 32 // gx, 4, 4, 8), axis=0)
     return core.transpose(2, 0, 1, 3)

time: 104 us -> 102 us (0.981)
  blocking collectives: 45.6 us -> 41.7 us
  local copies, waits for them, and re-layouts: 0.73 us -> 3.45 us
  waiting for transfers between devices: 9.76 us -> 8.02 us
    all_to_all x1, blocking collectives: 19.4 us -> 16.6 us  [local(): slices = lax.all_to_all(slices, 'gx', 0, 0, tiled=True)]
    unnamed x8, local copies, waits for them, and re-layouts: 0.02 us -> 2.74 us
    ppermute x4, waiting for transfers between devices: 3.65 us -> 1.92 us  [swapped(): even = lax.ppermute(even, axis, even_pairs)]
    all_to_all x1, blocking collectives: 26.2 us -> 25.1 us  [local(): parts = lax.all_to_all(parts, ('gy', 'gz'), 0, 0, tiled=True)]
    pallas_call x1 -> x2, Pallas kernels: 19.2 us -> 19.7 us  [the longest x1 15.2 us: local(): call(advance, [f32(32, 4, 384), *buffers], [smem()] * 2 + [vmem()] * 14,...]
  transfers between devices with their start and end apart: 8 -> 8, of which waited for: 3 -> 2; matrix products, arithmetic and copies ran while one was open for 0% -> 0% of each run, Pallas kernels for 0% -> 5%
where the time goes in v6:
time: 102 us; the launch traced here: 101 us
  blocking collectives  41.7 us (41%)
  starting transfers between devices  25.8 us (25%)
  Pallas kernels  22.2 us (22%)
  waiting for transfers between devices  8.02 us (8%)
  local copies, waits for them, and re-layouts  3.45 us (3%)
    all_to_all x1, blocking collectives, local(): parts = lax.all_to_all(parts, ('gy', 'gz'), 0, 0, tiled=True)  25.1 us
    ppermute x4, starting transfers between devices, swapped(): even = lax.ppermute(even, axis, even_pairs)  21.9 us
    all_to_all x1, blocking collectives, local(): slices = lax.all_to_all(slices, 'gx', 0, 0, tiled=True)  16.6 us
    pallas_call x1, Pallas kernels, local(): call(advance, [f32(32, 4, 384), *buffers], [smem()] * 2 + [vmem()] * 14,...  15.2 us
    ppermute x4, waiting for transfers between devices, swapped(): return (even, lax.ppermute(odd, axis, odd_pairs))  6.1 us
    pallas_call x1, Pallas kernels, local(): call(prepare, [*buffers, f32(4, 128, 256), f32(48, 32)], [smem()] * 2 + [...  4.45 us
    ppermute x4, starting transfers between devices, swapped(): return (even, lax.ppermute(odd, axis, odd_pairs))  3.96 us
    unnamed x8, local copies, waits for them, and re-layouts  2.74 us
  transfers between devices with their start and end apart: 8, of which 2 were waited for; matrix products, arithmetic and copies ran while one was open for 0% of the time, Pallas kernels for 5%

profile of v6, /device:TPU:1, one launch (start us, length us, event | category | flops | bytes accessed | tf_op | source)
XLA Modules:
  0.0 101.3 jit_solution(16293173853673257420)
XLA Ops:
  0.0 2.2 %shard_map.73 = (f32[36,32,128]{2,1,0:T(8,128)S(1)}, f32[36,32,128]{2,1,0:T(8,128)S(1)}, f32[8,32,128]{2,1,0:T(8,128)S(1)}, f32[8,32,128]{2,1,0:T(8,128)S(1)}, f...) custom-call(f32[4,8,32,128]{3,2,1,0:T(8,128)} %f_in.1, f32[3,8,32,128]{3,2,1,0:T(8,128)} %v_in.1, ...), custom_call_target="tpu_custom_call" | custom-call | flops 1000000 | bytes 1000000 | tf_op jit(solution)/shard_map/pallas_call | solution.py:483
  2.2 4.8 %collective-permute-start = (f32[36,32,128]{2,1,0:T(8,128)S(1)}, f32[36,32,128]{2,1,0:T(8,128)S(1)}, u32[]{:S(2)}, u32[]{:S(2)}) collective-permute-start(f32[36,32,128]{2,1,0:T(8,128)S(1)} %get-tuple-element.26), channel_id=1, source_target_pairs={{0,32},{64,96},{128,160},{192,224},{256,288},{320,352},{384,416},{... | collective-permute-start | bytes 1769480 | tf_op jit(solution)/shard_map/ppermute | solution.py:480
  7.0 0.7 collective-permute-start.1
  7.8 3.1 %collective-permute-start.2 = (f32[8,32,128]{2,1,0:T(8,128)S(1)}, f32[8,32,128]{2,1,0:T(8,128)S(1)}, u32[]{:S(2)}, u32[]{:S(2)}) collective-permute-start(f32[8,32,128]{2,1,0:T(8,128)S(1)} %get-tuple-element.28), channel_id=1, source_target_pairs={{0,1},{2,3},{1,0},{3,2},{4,5},{6,7},{5,4},{7,6},{8,9},{10,11},{9,8... | collective-permute-start | bytes 393224 | tf_op jit(solution)/shard_map/ppermute | solution.py:480
  10.9 0.7 collective-permute-start.3
  11.6 1.9 %collective-permute-done.2.z_even = f32[8,32,128]{2,1,0:T(8,128)S(1)} collective-permute-done((f32[8,32,128]{2,1,0:T(8,128)S(1)}, f32[8,32,128]{2,1,0:T(8,128)S(1)}, u32[]{:S(2)}, u32[]{:S(2)}) %collective-permute-start.2) | collective-permute-done | bytes 131104 | tf_op jit(solution)/shard_map/ppermute | solution.py:480
  13.5 0.7 copy-done
  14.2 0.1 shard_map.74
  14.3 7.0 %collective-permute-start.4 = (f32[49,8,128]{2,1,0:T(8,128)S(1)}, f32[49,8,128]{2,1,0:T(8,128)S(1)}, u32[]{:S(2)}, u32[]{:S(2)}) collective-permute-start(f32[49,8,128]{2,1,0:T(8,128)S(1)} %get-tuple-element.32), channel_id=1, source_target_pairs={{0,4},{8,12},{16,20},{24,28},{4,0},{12,8},{20,16},{28,24},{1,5},{9... | collective-permute-start | bytes 602120 | tf_op jit(solution)/shard_map/ppermute | solution.py:480
  21.3 1.9 %collective-permute-start.5 = (f32[49,8,128]{2,1,0:T(8,128)S(1)}, f32[49,8,128]{2,1,0:T(8,128)S(1)}, u32[]{:S(2)}, u32[]{:S(2)}) collective-permute-start(f32[49,8,128]{2,1,0:T(8,128)S(1)} %get-tuple-element.33), channel_id=1, source_target_pairs={{4,8},{12,16},{20,24},{8,4},{16,12},{24,20},{5,9},{13,17},{21,25},... | collective-permute-start | bytes 602120 | tf_op jit(solution)/shard_map/ppermute | solution.py:481
  23.2 6.1 %collective-permute-done.5.y_odd = f32[49,8,128]{2,1,0:T(8,128)S(1)} collective-permute-done((f32[49,8,128]{2,1,0:T(8,128)S(1)}, f32[49,8,128]{2,1,0:T(8,128)S(1)}, u32[]{:S(2)}, u32[]{:S(2)}) %collective-permute-start.5) | collective-permute-done | bytes 200736 | tf_op jit(solution)/shard_map/ppermute | solution.py:481
  29.3 0.7 copy-done.1
  30.0 0.1 shard_map.75
  30.1 6.9 %collective-permute-start.6 = (f32[34,8,128]{2,1,0:T(8,128)S(1)}, f32[34,8,128]{2,1,0:T(8,128)S(1)}, u32[]{:S(2)}, u32[]{:S(2)}) collective-permute-start(f32[34,8,128]{2,1,0:T(8,128)S(1)} %get-tuple-element.34), channel_id=1, source_target_pairs={{0,32},{64,96},{128,160},{192,224},{256,288},{320,352},{384,416},{... | collective-permute-start | bytes 417800 | tf_op jit(solution)/shard_map/ppermute | solution.py:480
  37.0 0.7 collective-permute-start.7
  37.7 0.7 copy-done.2
  38.4 0.7 copy-done.3
  39.0 4.5 %shard_map.76 = (f32[4,24,64,128]{3,2,1,0:T(8,128)S(1)}, f32[4,24,64,128]{3,2,1,0:T(8,128)S(1)}, f32[24,64,128]{2,1,0:T(8,128)S(1)}, f32[24,64,128]{2,1,0:T(8,12...) custom-call(f32[4]{0:T(128)S(1)} %copy-done.3, ...), custom_call_target="tpu_custom_call" | custom-call | flops 3000000 | bytes 3000000 | tf_op jit(solution)/shard_map/pallas_call | solution.py:505
  43.5 15.2 %shard_map.77 = (f32[32,4,384]{2,1,0:T(4,128)S(1)}, f32[4,24,64,128]{3,2,1,0:T(8,128)S(1)}, f32[4,24,64,128]{3,2,1,0:T(8,128)S(1)}, f32[24,64,128]{2,1,0:T(8,128...) custom-call(f32[4]{0:T(128)S(1)} %copy-done.3, ...), custom_call_target="tpu_custom_call", output_to_operand_aliasing={{1}: (9, {}), {2}: (10, {}), {3}: (11, {}), {4}: (12, {}), ... | custom-call | flops 10000000 | bytes 10000000 | tf_op jit(solution)/shard_map/pallas_call | solution.py:508
  58.7 25.1 %all_to_all.14.parts = f32[32,4,384]{2,1,0:T(4,128)S(1)} all-to-all(f32[32,4,384]{2,1,0:T(4,128)S(1)} %get-tuple-element.46), channel_id=1, replica_groups=mesh['gx'=16,'gy'=8,'gz'=4] {'gy','gz'}, dimensions={0} | all-to-all | bytes 393216 | tf_op jit(solution)/shard_map/all_to_all | solution.py:518
  83.9 0.2 shard_map.78
  84.0 16.6 %all_to_all.15 = f32[16,2,128]{2,1,0:T(2,128)S(1)} all-to-all(f32[16,2,128]{2,1,0:T(2,128)S(1)} %bitcast.3), channel_id=1, replica_groups=mesh['gx'=16,'gy'=8,'gz'=4] {'gx'}, dimensions={0} | all-to-all | bytes 32768 | tf_op jit(solution)/shard_map/all_to_all | solution.py:522
  100.6 0.1 reduce_sum.12
  100.7 0.6 copy.15
  (11 shorter events, 0.1 us)
Async XLA Ops:
  2.2 41.3 %collective-permute-start = (f32[36,32,128]{2,1,0:T(8,128)S(1)}, f32[36,32,128]{2,1,0:T(8,128)S(1)}, u32[]{:S(2)}, u32[]{:S(2)}) collective-permute-start(f32[36,32,128]{2,1,0:T(8,128)S(1)} %get-tuple-element.26), channel_id=1, source_target_pairs={{0,32},{64,96},{128,160},{192,224},{256,288},{320,352},{384,416},{... | collective-permute-start | bytes 1769480 | tf_op jit(solution)/shard_map/ppermute | solution.py:480
  7.0 36.5 %collective-permute-start.1 = (f32[36,32,128]{2,1,0:T(8,128)S(1)}, f32[36,32,128]{2,1,0:T(8,128)S(1)}, u32[]{:S(2)}, u32[]{:S(2)}) collective-permute-start(f32[36,32,128]{2,1,0:T(8,128)S(1)} %get-tuple-element.27), channel_id=1, source_target_pairs={{32,64},{96,128},{160,192},{224,256},{288,320},{352,384},{416,448}... | collective-permute-start | bytes 1769480 | tf_op jit(solution)/shard_map/ppermute | solution.py:481
  7.8 5.7 %collective-permute-start.2 = (f32[8,32,128]{2,1,0:T(8,128)S(1)}, f32[8,32,128]{2,1,0:T(8,128)S(1)}, u32[]{:S(2)}, u32[]{:S(2)}) collective-permute-start(f32[8,32,128]{2,1,0:T(8,128)S(1)} %get-tuple-element.28), channel_id=1, source_target_pairs={{0,1},{2,3},{1,0},{3,2},{4,5},{6,7},{5,4},{7,6},{8,9},{10,11},{9,8... | collective-permute-start | bytes 393224 | tf_op jit(solution)/shard_map/ppermute | solution.py:480
  10.9 2.6 %collective-permute-start.3 = (f32[8,32,128]{2,1,0:T(8,128)S(1)}, f32[8,32,128]{2,1,0:T(8,128)S(1)}, u32[]{:S(2)}, u32[]{:S(2)}) collective-permute-start(f32[8,32,128]{2,1,0:T(8,128)S(1)} %get-tuple-element.29), channel_id=1, source_target_pairs={{1,2},{2,1},{5,6},{6,5},{9,10},{10,9},{13,14},{14,13},{17,18},{18,... | collective-permute-start | bytes 393224 | tf_op jit(solution)/shard_map/ppermute | solution.py:481
  13.5 0.7 copy-start
  14.3 8.9 %collective-permute-start.4 = (f32[49,8,128]{2,1,0:T(8,128)S(1)}, f32[49,8,128]{2,1,0:T(8,128)S(1)}, u32[]{:S(2)}, u32[]{:S(2)}) collective-permute-start(f32[49,8,128]{2,1,0:T(8,128)S(1)} %get-tuple-element.32), channel_id=1, source_target_pairs={{0,4},{8,12},{16,20},{24,28},{4,0},{12,8},{20,16},{28,24},{1,5},{9... | collective-permute-start | bytes 602120 | tf_op jit(solution)/shard_map/ppermute | solution.py:480
  21.3 8.0 %collective-permute-start.5 = (f32[49,8,128]{2,1,0:T(8,128)S(1)}, f32[49,8,128]{2,1,0:T(8,128)S(1)}, u32[]{:S(2)}, u32[]{:S(2)}) collective-permute-start(f32[49,8,128]{2,1,0:T(8,128)S(1)} %get-tuple-element.33), channel_id=1, source_target_pairs={{4,8},{12,16},{20,24},{8,4},{16,12},{24,20},{5,9},{13,17},{21,25},... | collective-permute-start | bytes 602120 | tf_op jit(solution)/shard_map/ppermute | solution.py:481
  29.3 0.7 copy-start.1
  30.1 13.4 %collective-permute-start.6 = (f32[34,8,128]{2,1,0:T(8,128)S(1)}, f32[34,8,128]{2,1,0:T(8,128)S(1)}, u32[]{:S(2)}, u32[]{:S(2)}) collective-permute-start(f32[34,8,128]{2,1,0:T(8,128)S(1)} %get-tuple-element.34), channel_id=1, source_target_pairs={{0,32},{64,96},{128,160},{192,224},{256,288},{320,352},{384,416},{... | collective-permute-start | bytes 417800 | tf_op jit(solution)/shard_map/ppermute | solution.py:480
  37.0 6.5 %collective-permute-start.7 = (f32[34,8,128]{2,1,0:T(8,128)S(1)}, f32[34,8,128]{2,1,0:T(8,128)S(1)}, u32[]{:S(2)}, u32[]{:S(2)}) collective-permute-start(f32[34,8,128]{2,1,0:T(8,128)S(1)} %get-tuple-element.35), channel_id=1, source_target_pairs={{32,64},{96,128},{160,192},{224,256},{288,320},{352,384},{416,448}... | collective-permute-start | bytes 417800 | tf_op jit(solution)/shard_map/ppermute | solution.py:481
  37.7 0.7 copy-start.2
  38.4 0.7 copy-start.3

commit v7 on v6

--- a/solution.py
+++ b/solution.py
@@ -56,7 +56,8 @@
         return lax.dot_general(p, q, (((a_dim,), (b_dim,)), ((), ())), preferred_element_type=F32)
 
     (a_high, a_low), (b_high, b_low) = halves(a), halves(b)
-    return product(a_high, b_high) + (product(a_high, b_low) + product(a_low, b_high))
+    both = product(a_high, jnp.concatenate([b_high, b_low], axis=1 - b_dim))
+    return both[:, 0:128] + (both[:, 128:256] + product(a_low, b_high))
 
 
 def padded(rows):
@@ -68,8 +69,8 @@
     return 1 - odd, odd
 
 
-def pack_xz(f_in, v_in, fz_in, x_even, x_odd, z_even, z_odd, f, v, fz, arrived):
-    pairs = ((f_in, f), (v_in, v), (fz_in, fz))
+def pack_xz(f_in, v_in, fz_in, fy_in, fx_in, x_even, x_odd, z_even, z_odd, f, v, fz, fy, fx, arrived):
+    pairs = ((f_in, f), (v_in, v), (fz_in, fz), (fy_in, fy), (fx_in, fx))
     copies = [pltpu.make_async_copy(a, b, arrived.at[n]) for n, (a, b) in enumerate(pairs)]
     for copy in copies:
         copy.start()
@@ -369,7 +370,7 @@
         x = jnp.where(j < 4, 6 + j, 10 + j)
         stage(x, full, full, state, edge, section, edge2, False)
 
-    @pl.loop(0, 4)
+    @pl.loop(0, 4, unroll=2)
     def _(j):
         stage(jnp.where(j < 2, 4 + j, 16 + j), own, (), state, edge, section, edge2, False)
 
@@ -377,11 +378,11 @@
     def _(x):
         stage(x, full, own, section, edge2, state, edge, True)
 
-    @pl.loop(0, 4)
+    @pl.loop(0, 4, unroll=2)
     def _(j):
         stage(jnp.where(j < 2, 6 + j, 14 + j), own, (), section, edge2, state, edge, True)
 
-    @pl.loop(8, 16)
+    @pl.loop(8, 16, unroll=2)
     def _(x):
         stage(x, own, (), state, edge, section, edge2, False)
 
@@ -392,7 +393,7 @@
             section[i, 8 + x, 0:16] = jnp.zeros((16, 128), F32)
             section[i, 8 + x, 48:64] = jnp.zeros((16, 128), F32)
 
-    @pl.loop(0, 8)
+    @pl.loop(0, 8, unroll=2)
     def _(x):
         base = pl.multiple_of(x * 48, 16)
         for r in own:
@@ -450,15 +451,18 @@
         mixed[x * 32 : x * 32 + 32] = dot(fye[...], total[x * 48 : x * 48 + 48], 0, 0)
     for x in range(4):
         mixed[256 + x * 32 : 288 + x * 32] = dot(fy[...], total_faces[x * 32 : x * 32 + 32], 0, 0)
-    lane = lanes_of(4)
-    for j in range(8):
-        for t in range(3):
-            tiles = [mixed[pl.ds(128 * t + 4 * j + b, 4, stride=32), :] for b in range(4)]
+    for planes, first in ((8, 0), (4, 8)):
+        lane = lanes_of(planes)
+        for j in range(8):
+            rows = [pl.ds(32 * first + 4 * j + b, planes, stride=32) for b in range(4)]
+            tiles = [mixed[at, :] for at in rows]
             for k in range(4):
-                tile = jnp.zeros((4, 128), F32)
+                tile = jnp.zeros((planes, 128), F32)
                 for b in range(4):
                     tile = jnp.where(within(lane, 32 * b, 32), roll(tiles[b], 32 * (b - k)), tile)
-                out[j * 4 + k, :, 128 * t : 128 * t + 128] = tile
+                for t in range(planes // 4):
+                    at = 32 * first + 128 * t
+                    out[j * 4 + k, :, at : at + 128] = tile[4 * t : 4 * t + 4]
 
 
 def contract_x(parts, fx, e_even, e_odd, out):
@@ -480,18 +484,22 @@
         even = lax.ppermute(even, axis, even_pairs)
         return even, lax.ppermute(odd, axis, odd_pairs)
 
-    x_even, x_odd, z_even, z_odd, fields, velocity, fz = call(
+    inputs = (fields, velocity, factor_z.T, factor_y, factor_x)
+    x_even, x_odd, z_even, z_odd, fields, velocity, fz, fy, fx = call(
         pack_xz,
-        [f32(36, 32, 128)] * 2 + [f32(8, 32, 128)] * 2
-        + [f32(4, 8, 32, 128), f32(3, 8, 32, 128), f32(32, 128)],
-        [pl.BlockSpec(memory_space=pltpu.HBM)] * 3,
-        scratch=[pltpu.SemaphoreType.DMA((3,))],
-    )(*(pltpu.with_memory_space_constraint(a, pltpu.HBM) for a in (fields, velocity, factor_z.T)))
+        [f32(36, 32, 128)] * 2 + [f32(8, 32, 128)] * 2 + [f32(*a.shape) for a in inputs],
+        [pl.BlockSpec(memory_space=pltpu.HBM)] * 5,
+        scratch=[pltpu.SemaphoreType.DMA((5,))],
+    )(*(pltpu.with_memory_space_constraint(a, pltpu.HBM) for a in inputs))
     z_even, z_odd = swapped("gz", z_even, z_odd)
-    y_even, y_odd = call(pack_y, [f32(49, 8, 128)] * 2, [vmem()] * 5)(fields, velocity, factor_y, z_even, z_odd)
+    y_even, y_odd = call(pack_y, [f32(49, 8, 128)] * 2, [vmem()] * 5)(
+        fields, velocity, fy, z_even, z_odd
+    )
     y_even, y_odd = swapped("gy", y_even, y_odd)
     x_even, x_odd = swapped("gx", x_even, x_odd)
-    e_even, e_odd = call(pack_x2, [f32(34, 8, 128)] * 2, [vmem()] * 5)(z_even, z_odd, y_even, y_odd, factor_x)
+    e_even, e_odd = call(pack_x2, [f32(34, 8, 128)] * 2, [vmem()] * 5)(
+        z_even, z_odd, y_even, y_odd, fx
+    )
     e_even, e_odd = swapped("gx", e_even, e_odd)
 
     def tiles(*lead):
@@ -504,20 +512,21 @@
     ]
     *filled, rhs, fye = call(
         prepare, [*buffers, f32(4, 128, 256), f32(48, 32)], [smem()] * 2 + [vmem()] * 8, work=3000000
-    )(diffusivity, coupling, fields, velocity, z_even, z_odd, y_even, y_odd, fz, factor_y)
+    )(diffusivity, coupling, fields, velocity, z_even, z_odd, y_even, y_odd, fz, fy)
     parts, *_ = call(
         advance,
         [f32(32, 4, 384), *buffers],
         [smem()] * 2 + [vmem()] * 14,
         scratch=[
-            pltpu.VMEM((4, 384, 256), F32), pltpu.VMEM((4, 128, 128), F32), pltpu.VMEM((384, 128), F32)
+            pltpu.VMEM((4, 384, 256), F32), pltpu.VMEM((4, 128, 128), F32),
+            pltpu.VMEM((384, 128), F32),
         ],
         work=10000000,
         aliases={9 + n: 1 + n for n in range(7)},
-    )(diffusivity, coupling, x_even, x_odd, e_even, e_odd, factor_y, rhs, fye, *filled)
+    )(diffusivity, coupling, x_even, x_odd, e_even, e_odd, fy, rhs, fye, *filled)
     parts = lax.all_to_all(parts, ("gy", "gz"), 0, 0, tiled=True)
     slices = call(contract_x, f32(32, 128), [vmem()] * 4)(
-        parts, factor_x, e_even, e_odd
+        parts, fx, e_even, e_odd
     )
     slices = lax.all_to_all(slices, "gx", 0, 0, tiled=True)
     core = jnp.sum(slices.reshape(gx, 32 // gx, 4, 4, 8), axis=0)

time: 102 us -> 98.2 us (0.963)
  Pallas kernels: 22.2 us -> 20.1 us
  local copies, waits for them, and re-layouts: 3.45 us -> 2.04 us
    pallas_call x1, Pallas kernels: 15.2 us -> 13.1 us  [local(): call(advance, [f32(32, 4, 384), *buffers], [smem()] * 2 + [vmem()] * 14,...]
    unnamed x8 -> x4, local copies, waits for them, and re-layouts: 2.74 us -> 1.33 us
where the time goes in v7:
time: 98.2 us; the launch traced here: 97.8 us
  blocking collectives  41.6 us (42%)
  starting transfers between devices  25.8 us (26%)
  Pallas kernels  20.1 us (20%)
  waiting for transfers between devices  8.02 us (8%)
  local copies, waits for them, and re-layouts  2.04 us (2%)
    all_to_all x1, blocking collectives, local(): parts = lax.all_to_all(parts, ('gy', 'gz'), 0, 0, tiled=True)  25.1 us
    ppermute x4, starting transfers between devices, swapped(): even = lax.ppermute(even, axis, even_pairs)  21.9 us
    all_to_all x1, blocking collectives, local(): slices = lax.all_to_all(slices, 'gx', 0, 0, tiled=True)  16.5 us
    pallas_call x1, Pallas kernels, local(): call(advance, [f32(32, 4, 384), *buffers], [smem()] * 2 + [vmem()] * 14,...  13.1 us
    ppermute x4, waiting for transfers between devices, swapped(): return (even, lax.ppermute(odd, axis, odd_pairs))  6.1 us
    pallas_call x1, Pallas kernels, local(): call(prepare, [*buffers, f32(4, 128, 256), f32(48, 32)], [smem()] * 2 + [...  4.47 us
    ppermute x4, starting transfers between devices, swapped(): return (even, lax.ppermute(odd, axis, odd_pairs))  3.96 us
    pallas_call x1, Pallas kernels, local(): call(pack_xz, [f32(36, 32, 128)] * 2 + [f32(8, 32, 128)] * 2 + [f32(*a.sh...  2.23 us
  transfers between devices with their start and end apart: 8, of which 2 were waited for; matrix products, arithmetic and copies ran while one was open for 0% of the time, Pallas kernels for 5%

profile of v7, /device:TPU:1, one launch (start us, length us, event | category | flops | bytes accessed | tf_op | source)
XLA Modules:
  0.0 97.8 jit_solution(13085751616743431712)
XLA Ops:
  0.0 2.2 %shard_map.73 = (f32[36,32,128]{2,1,0:T(8,128)S(1)}, f32[36,32,128]{2,1,0:T(8,128)S(1)}, f32[8,32,128]{2,1,0:T(8,128)S(1)}, f32[8,32,128]{2,1,0:T(8,128)S(1)}, f...) custom-call(f32[4,8,32,128]{3,2,1,0:T(8,128)} %f_in.1, ...), custom_call_target="tpu_custom_call" | custom-call | flops 1000000 | bytes 1000000 | tf_op jit(solution)/shard_map/pallas_call | solution.py:488
  2.2 4.8 %collective-permute-start = (f32[36,32,128]{2,1,0:T(8,128)S(1)}, f32[36,32,128]{2,1,0:T(8,128)S(1)}, u32[]{:S(2)}, u32[]{:S(2)}) collective-permute-start(f32[36,32,128]{2,1,0:T(8,128)S(1)} %get-tuple-element.28), channel_id=1, source_target_pairs={{0,32},{64,96},{128,160},{192,224},{256,288},{320,352},{384,416},{... | collective-permute-start | bytes 1769480 | tf_op jit(solution)/shard_map/ppermute | solution.py:484
  7.1 0.7 collective-permute-start.1
  7.8 3.1 %collective-permute-start.2 = (f32[8,32,128]{2,1,0:T(8,128)S(1)}, f32[8,32,128]{2,1,0:T(8,128)S(1)}, u32[]{:S(2)}, u32[]{:S(2)}) collective-permute-start(f32[8,32,128]{2,1,0:T(8,128)S(1)} %get-tuple-element.30), channel_id=1, source_target_pairs={{0,1},{2,3},{1,0},{3,2},{4,5},{6,7},{5,4},{7,6},{8,9},{10,11},{9,8... | collective-permute-start | bytes 393224 | tf_op jit(solution)/shard_map/ppermute | solution.py:484
  10.9 0.7 collective-permute-start.3
  11.6 1.9 %collective-permute-done.2.z_even = f32[8,32,128]{2,1,0:T(8,128)S(1)} collective-permute-done((f32[8,32,128]{2,1,0:T(8,128)S(1)}, f32[8,32,128]{2,1,0:T(8,128)S(1)}, u32[]{:S(2)}, u32[]{:S(2)}) %collective-permute-start.2) | collective-permute-done | bytes 131104 | tf_op jit(solution)/shard_map/ppermute | solution.py:484
  13.5 0.0 collective-permute-done.3.z_odd
  13.5 0.1 shard_map.74
  13.6 7.0 %collective-permute-start.4 = (f32[49,8,128]{2,1,0:T(8,128)S(1)}, f32[49,8,128]{2,1,0:T(8,128)S(1)}, u32[]{:S(2)}, u32[]{:S(2)}) collective-permute-start(f32[49,8,128]{2,1,0:T(8,128)S(1)} %get-tuple-element.35), channel_id=1, source_target_pairs={{0,4},{8,12},{16,20},{24,28},{4,0},{12,8},{20,16},{28,24},{1,5},{9... | collective-permute-start | bytes 602120 | tf_op jit(solution)/shard_map/ppermute | solution.py:484
  20.6 1.9 %collective-permute-start.5 = (f32[49,8,128]{2,1,0:T(8,128)S(1)}, f32[49,8,128]{2,1,0:T(8,128)S(1)}, u32[]{:S(2)}, u32[]{:S(2)}) collective-permute-start(f32[49,8,128]{2,1,0:T(8,128)S(1)} %get-tuple-element.36), channel_id=1, source_target_pairs={{4,8},{12,16},{20,24},{8,4},{16,12},{24,20},{5,9},{13,17},{21,25},... | collective-permute-start | bytes 602120 | tf_op jit(solution)/shard_map/ppermute | solution.py:485
  22.5 6.1 %collective-permute-done.5.y_odd = f32[49,8,128]{2,1,0:T(8,128)S(1)} collective-permute-done((f32[49,8,128]{2,1,0:T(8,128)S(1)}, f32[49,8,128]{2,1,0:T(8,128)S(1)}, u32[]{:S(2)}, u32[]{:S(2)}) %collective-permute-start.5) | collective-permute-done | bytes 200736 | tf_op jit(solution)/shard_map/ppermute | solution.py:485
  28.6 0.1 shard_map.75
  28.7 6.9 %collective-permute-start.6 = (f32[34,8,128]{2,1,0:T(8,128)S(1)}, f32[34,8,128]{2,1,0:T(8,128)S(1)}, u32[]{:S(2)}, u32[]{:S(2)}) collective-permute-start(f32[34,8,128]{2,1,0:T(8,128)S(1)} %get-tuple-element.38), channel_id=1, source_target_pairs={{0,32},{64,96},{128,160},{192,224},{256,288},{320,352},{384,416},{... | collective-permute-start | bytes 417800 | tf_op jit(solution)/shard_map/ppermute | solution.py:484
  35.6 0.7 collective-permute-start.7
  36.3 0.0 copy-start
  36.3 0.7 copy-done
  37.0 0.7 copy-done.1
  37.6 4.5 %shard_map.76 = (f32[4,24,64,128]{3,2,1,0:T(8,128)S(1)}, f32[4,24,64,128]{3,2,1,0:T(8,128)S(1)}, f32[24,64,128]{2,1,0:T(8,128)S(1)}, f32[24,64,128]{2,1,0:T(8,12...) custom-call(f32[4]{0:T(128)S(1)} %copy-done.1, ...), custom_call_target="tpu_custom_call" | custom-call | flops 3000000 | bytes 3000000 | tf_op jit(solution)/shard_map/pallas_call | solution.py:513
  42.1 13.1 %shard_map.77 = (f32[32,4,384]{2,1,0:T(4,128)S(1)}, f32[4,24,64,128]{3,2,1,0:T(8,128)S(1)}, f32[4,24,64,128]{3,2,1,0:T(8,128)S(1)}, f32[24,64,128]{2,1,0:T(8,128...) custom-call(f32[4]{0:T(128)S(1)} %copy-done.1, ...), custom_call_target="tpu_custom_call", output_to_operand_aliasing={{1}: (9, {}), {2}: (10, {}), {3}: (11, {}), {4}: (12, {}), ... | custom-call | flops 10000000 | bytes 10000000 | tf_op jit(solution)/shard_map/pallas_call | solution.py:516
  55.2 25.1 %all_to_all.14.parts = f32[32,4,384]{2,1,0:T(4,128)S(1)} all-to-all(f32[32,4,384]{2,1,0:T(4,128)S(1)} %get-tuple-element.50), channel_id=1, replica_groups=mesh['gx'=16,'gy'=8,'gz'=4] {'gy','gz'}, dimensions={0} | all-to-all | bytes 393216 | tf_op jit(solution)/shard_map/all_to_all | solution.py:527
  80.3 0.2 shard_map.78
  80.5 16.5 %all_to_all.15 = f32[16,2,128]{2,1,0:T(2,128)S(1)} all-to-all(f32[16,2,128]{2,1,0:T(2,128)S(1)} %bitcast.3), channel_id=1, replica_groups=mesh['gx'=16,'gy'=8,'gz'=4] {'gx'}, dimensions={0} | all-to-all | bytes 32768 | tf_op jit(solution)/shard_map/all_to_all | solution.py:531
  97.1 0.1 reduce_sum.12
  97.2 0.6 copy.15
  (7 shorter events, 0.0 us)
Async XLA Ops:
  2.2 39.9 %collective-permute-start = (f32[36,32,128]{2,1,0:T(8,128)S(1)}, f32[36,32,128]{2,1,0:T(8,128)S(1)}, u32[]{:S(2)}, u32[]{:S(2)}) collective-permute-start(f32[36,32,128]{2,1,0:T(8,128)S(1)} %get-tuple-element.28), channel_id=1, source_target_pairs={{0,32},{64,96},{128,160},{192,224},{256,288},{320,352},{384,416},{... | collective-permute-start | bytes 1769480 | tf_op jit(solution)/shard_map/ppermute | solution.py:484
  7.1 35.1 %collective-permute-start.1 = (f32[36,32,128]{2,1,0:T(8,128)S(1)}, f32[36,32,128]{2,1,0:T(8,128)S(1)}, u32[]{:S(2)}, u32[]{:S(2)}) collective-permute-start(f32[36,32,128]{2,1,0:T(8,128)S(1)} %get-tuple-element.29), channel_id=1, source_target_pairs={{32,64},{96,128},{160,192},{224,256},{288,320},{352,384},{416,448}... | collective-permute-start | bytes 1769480 | tf_op jit(solution)/shard_map/ppermute | solution.py:485
  7.8 5.7 %collective-permute-start.2 = (f32[8,32,128]{2,1,0:T(8,128)S(1)}, f32[8,32,128]{2,1,0:T(8,128)S(1)}, u32[]{:S(2)}, u32[]{:S(2)}) collective-permute-start(f32[8,32,128]{2,1,0:T(8,128)S(1)} %get-tuple-element.30), channel_id=1, source_target_pairs={{0,1},{2,3},{1,0},{3,2},{4,5},{6,7},{5,4},{7,6},{8,9},{10,11},{9,8... | collective-permute-start | bytes 393224 | tf_op jit(solution)/shard_map/ppermute | solution.py:484
  10.9 2.6 %collective-permute-start.3 = (f32[8,32,128]{2,1,0:T(8,128)S(1)}, f32[8,32,128]{2,1,0:T(8,128)S(1)}, u32[]{:S(2)}, u32[]{:S(2)}) collective-permute-start(f32[8,32,128]{2,1,0:T(8,128)S(1)} %get-tuple-element.31), channel_id=1, source_target_pairs={{1,2},{2,1},{5,6},{6,5},{9,10},{10,9},{13,14},{14,13},{17,18},{18,... | collective-permute-start | bytes 393224 | tf_op jit(solution)/shard_map/ppermute | solution.py:485
  13.6 8.9 %collective-permute-start.4 = (f32[49,8,128]{2,1,0:T(8,128)S(1)}, f32[49,8,128]{2,1,0:T(8,128)S(1)}, u32[]{:S(2)}, u32[]{:S(2)}) collective-permute-start(f32[49,8,128]{2,1,0:T(8,128)S(1)} %get-tuple-element.35), channel_id=1, source_target_pairs={{0,4},{8,12},{16,20},{24,28},{4,0},{12,8},{20,16},{28,24},{1,5},{9... | collective-permute-start | bytes 602120 | tf_op jit(solution)/shard_map/ppermute | solution.py:484
  20.6 8.0 %collective-permute-start.5 = (f32[49,8,128]{2,1,0:T(8,128)S(1)}, f32[49,8,128]{2,1,0:T(8,128)S(1)}, u32[]{:S(2)}, u32[]{:S(2)}) collective-permute-start(f32[49,8,128]{2,1,0:T(8,128)S(1)} %get-tuple-element.36), channel_id=1, source_target_pairs={{4,8},{12,16},{20,24},{8,4},{16,12},{24,20},{5,9},{13,17},{21,25},... | collective-permute-start | bytes 602120 | tf_op jit(solution)/shard_map/ppermute | solution.py:485
  28.7 13.4 %collective-permute-start.6 = (f32[34,8,128]{2,1,0:T(8,128)S(1)}, f32[34,8,128]{2,1,0:T(8,128)S(1)}, u32[]{:S(2)}, u32[]{:S(2)}) collective-permute-start(f32[34,8,128]{2,1,0:T(8,128)S(1)} %get-tuple-element.38), channel_id=1, source_target_pairs={{0,32},{64,96},{128,160},{192,224},{256,288},{320,352},{384,416},{... | collective-permute-start | bytes 417800 | tf_op jit(solution)/shard_map/ppermute | solution.py:484
  35.6 6.5 %collective-permute-start.7 = (f32[34,8,128]{2,1,0:T(8,128)S(1)}, f32[34,8,128]{2,1,0:T(8,128)S(1)}, u32[]{:S(2)}, u32[]{:S(2)}) collective-permute-start(f32[34,8,128]{2,1,0:T(8,128)S(1)} %get-tuple-element.39), channel_id=1, source_target_pairs={{32,64},{96,128},{160,192},{224,256},{288,320},{352,384},{416,448}... | collective-permute-start | bytes 417800 | tf_op jit(solution)/shard_map/ppermute | solution.py:485
  36.3 0.7 copy-start
  37.0 0.7 copy-start.1

commit v8 on v7

--- a/solution.py
+++ b/solution.py
@@ -16,8 +16,12 @@
     return pl.BlockSpec(memory_space=pltpu.VMEM)
 
 
-def smem():
-    return pl.BlockSpec(memory_space=pltpu.SMEM)
+def hbm():
+    return pl.BlockSpec(memory_space=pltpu.HBM)
+
+
+def in_hbm(*arrays):
+    return [pltpu.with_memory_space_constraint(a, pltpu.HBM) for a in arrays]
 
 
 def f32(*shape):
@@ -279,10 +283,19 @@
             slab_dst[x, at] = jnp.where(ok & z_ok, new, 0.0)
 
 
+def fetched(d_in, c_in, d, c, arrived):
+    pairs = ((d_in, d), (c_in, c))
+    copies = [pltpu.make_async_copy(a, b, arrived.at[n]) for n, (a, b) in enumerate(pairs)]
+    for copy in copies:
+        copy.start()
+    return copies
+
+
 def prepare(
-    d, c, f, v, z_even, z_odd, y_even, y_odd, fz, fy,
-    state, section, edge, edge2, wind, edge_wind, zm, rhs, fye,
+    d_in, c_in, f, v, z_even, z_odd, y_even, y_odd, fz, fy,
+    state, section, edge, edge2, wind, edge_wind, zm, rhs, fye, d, c, arrived,
 ):
+    copies = fetched(d_in, c_in, d, c, arrived)
     y_low, y_high = sides("gy", y_even, y_odd)
     for i in range(4):
         for x in range(8):
@@ -315,6 +328,8 @@
         for r in FULL:
             slabs(state, wind, zm, edge, edge_wind, x, r, 16, True)
 
+    for copy in copies:
+        copy.wait()
     stencil = Stencil(d, c, wind, edge_wind)
 
     @pl.loop(10, 14)
@@ -322,13 +337,11 @@
         stencil.stage(x, FULL, FULL, state, edge, section, edge2, False)
 
 
-def advance(
-    d, c, x_even, x_odd, e_even, e_odd, fy, rhs, fye, *refs
-):
-    out, state, section, edge, edge2, wind, edge_wind, zm, final, faces, mixed = refs[7:]
-    stencil = Stencil(d, c, wind, edge_wind)
-    dd, cc, stage, scale = stencil.dd, stencil.cc, stencil.stage, SCALE
-    full, own = FULL, OWN
+def advance(d_in, c_in, x_even, x_odd, e_even, e_odd, fy, rhs, fye, *refs):
+    out, state, section, edge, edge2, wind, edge_wind, zm, final, faces, mixed = refs[7:18]
+    d, c, arrived = refs[18:]
+    copies = fetched(d_in, c_in, d, c, arrived)
+    scale, full, own = SCALE, FULL, OWN
     even_up, odd_up = ways("gx")
     for halo, above in ((x_even, even_up), (x_odd, odd_up)):
         for j in range(6):
@@ -364,6 +377,11 @@
         x = jnp.where(j < 2, 4 + j, 16 + j)
         for r in own:
             slabs(state, wind, zm, edge, edge_wind, x, r, 16, False)
+
+    for copy in copies:
+        copy.wait()
+    stencil = Stencil(d, c, wind, edge_wind)
+    dd, cc, stage = stencil.dd, stencil.cc, stencil.stage
 
     @pl.loop(0, 8)
     def _(j):
@@ -488,9 +506,9 @@
     x_even, x_odd, z_even, z_odd, fields, velocity, fz, fy, fx = call(
         pack_xz,
         [f32(36, 32, 128)] * 2 + [f32(8, 32, 128)] * 2 + [f32(*a.shape) for a in inputs],
-        [pl.BlockSpec(memory_space=pltpu.HBM)] * 5,
+        [hbm()] * 5,
         scratch=[pltpu.SemaphoreType.DMA((5,))],
-    )(*(pltpu.with_memory_space_constraint(a, pltpu.HBM) for a in inputs))
+    )(*in_hbm(*inputs))
     z_even, z_odd = swapped("gz", z_even, z_odd)
     y_even, y_odd = call(pack_y, [f32(49, 8, 128)] * 2, [vmem()] * 5)(
         fields, velocity, fy, z_even, z_odd
@@ -510,16 +528,22 @@
         tiles(4, PLANES), tiles(4, PLANES), tiles(PLANES), tiles(PLANES),
         tiles(3, PLANES), tiles(3, PLANES), tiles(PLANES),
     ]
+    scalars = [pltpu.SMEM((4,), F32), pltpu.SMEM((4, 4), F32), pltpu.SemaphoreType.DMA((2,))]
+    diffusivity, coupling = in_hbm(diffusivity, coupling)
     *filled, rhs, fye = call(
-        prepare, [*buffers, f32(4, 128, 256), f32(48, 32)], [smem()] * 2 + [vmem()] * 8, work=3000000
+        prepare,
+        [*buffers, f32(4, 128, 256), f32(48, 32)],
+        [hbm()] * 2 + [vmem()] * 8,
+        scratch=scalars,
+        work=3000000,
     )(diffusivity, coupling, fields, velocity, z_even, z_odd, y_even, y_odd, fz, fy)
     parts, *_ = call(
         advance,
         [f32(32, 4, 384), *buffers],
-        [smem()] * 2 + [vmem()] * 14,
+        [hbm()] * 2 + [vmem()] * 14,
         scratch=[
             pltpu.VMEM((4, 384, 256), F32), pltpu.VMEM((4, 128, 128), F32),
-            pltpu.VMEM((384, 128), F32),
+            pltpu.VMEM((384, 128), F32), *scalars,
         ],
         work=10000000,
         aliases={9 + n: 1 + n for n in range(7)},

time: 98.2 us -> 98.3 us (level)
  blocking collectives: 41.6 us -> 43.2 us
  local copies, waits for them, and re-layouts: 2.04 us -> 0.71 us
    all_to_all x1, blocking collectives: 16.5 us -> 18.1 us  [local(): slices = lax.all_to_all(slices, 'gx', 0, 0, tiled=True)]
    unnamed x4 -> x0, local copies, waits for them, and re-layouts: 1.33 us -> none
  transfers between devices with their start and end apart: 8 -> 8, of which waited for: 2 -> 2; matrix products, arithmetic and copies ran while one was open for 0% -> 0% of each run, Pallas kernels for 5% -> 4%
where the time goes in v8:
time: 98.3 us; the launch traced here: 97.9 us
  blocking collectives  43.2 us (44%)
  starting transfers between devices  25.8 us (26%)
  Pallas kernels  20 us (20%)
  waiting for transfers between devices  8.02 us (8%)
    all_to_all x1, blocking collectives, local(): parts = lax.all_to_all(parts, ('gy', 'gz'), 0, 0, tiled=True)  25.1 us
    ppermute x4, starting transfers between devices, swapped(): even = lax.ppermute(even, axis, even_pairs)  21.9 us
    all_to_all x1, blocking collectives, local(): slices = lax.all_to_all(slices, 'gx', 0, 0, tiled=True)  18.1 us
    pallas_call x1, Pallas kernels, local(): call(advance, [f32(32, 4, 384), *buffers], [hbm()] * 2 + [vmem()] * 14, s...  13.4 us
    ppermute x4, waiting for transfers between devices, swapped(): return (even, lax.ppermute(odd, axis, odd_pairs))  6.1 us
    pallas_call x1, Pallas kernels, local(): call(prepare, [*buffers, f32(4, 128, 256), f32(48, 32)], [hbm()] * 2 + [v...  4.04 us
    ppermute x4, starting transfers between devices, swapped(): return (even, lax.ppermute(odd, axis, odd_pairs))  3.96 us
    pallas_call x1, Pallas kernels, local(): call(pack_xz, [f32(36, 32, 128)] * 2 + [f32(8, 32, 128)] * 2 + [f32(*a.sh...  2.23 us
  transfers between devices with their start and end apart: 8, of which 2 were waited for; matrix products, arithmetic and copies ran while one was open for 0% of the time, Pallas kernels for 4%

profile of v8, /device:TPU:1, one launch (start us, length us, event | category | flops | bytes accessed | tf_op | source)
XLA Modules:
  0.0 97.9 jit_solution(11012504175374963870)
XLA Ops:
  0.0 2.2 %shard_map.73 = (f32[36,32,128]{2,1,0:T(8,128)S(1)}, f32[36,32,128]{2,1,0:T(8,128)S(1)}, f32[8,32,128]{2,1,0:T(8,128)S(1)}, f32[8,32,128]{2,1,0:T(8,128)S(1)}, f...) custom-call(f32[4,8,32,128]{3,2,1,0:T(8,128)} %f_in.1, ...), custom_call_target="tpu_custom_call" | custom-call | flops 1000000 | bytes 1000000 | tf_op jit(solution)/shard_map/pallas_call | solution.py:506
  2.2 4.8 %collective-permute-start = (f32[36,32,128]{2,1,0:T(8,128)S(1)}, f32[36,32,128]{2,1,0:T(8,128)S(1)}, u32[]{:S(2)}, u32[]{:S(2)}) collective-permute-start(f32[36,32,128]{2,1,0:T(8,128)S(1)} %get-tuple-element.28), channel_id=1, source_target_pairs={{0,32},{64,96},{128,160},{192,224},{256,288},{320,352},{384,416},{... | collective-permute-start | bytes 1769480 | tf_op jit(solution)/shard_map/ppermute | solution.py:502
  7.1 0.7 collective-permute-start.1
  7.8 3.1 %collective-permute-start.2 = (f32[8,32,128]{2,1,0:T(8,128)S(1)}, f32[8,32,128]{2,1,0:T(8,128)S(1)}, u32[]{:S(2)}, u32[]{:S(2)}) collective-permute-start(f32[8,32,128]{2,1,0:T(8,128)S(1)} %get-tuple-element.30), channel_id=1, source_target_pairs={{0,1},{2,3},{1,0},{3,2},{4,5},{6,7},{5,4},{7,6},{8,9},{10,11},{9,8... | collective-permute-start | bytes 393224 | tf_op jit(solution)/shard_map/ppermute | solution.py:502
  10.9 0.7 collective-permute-start.3
  11.6 1.9 %collective-permute-done.2.z_even = f32[8,32,128]{2,1,0:T(8,128)S(1)} collective-permute-done((f32[8,32,128]{2,1,0:T(8,128)S(1)}, f32[8,32,128]{2,1,0:T(8,128)S(1)}, u32[]{:S(2)}, u32[]{:S(2)}) %collective-permute-start.2) | collective-permute-done | bytes 131104 | tf_op jit(solution)/shard_map/ppermute | solution.py:502
  13.5 0.0 collective-permute-done.3.z_odd
  13.5 0.1 shard_map.74
  13.6 7.0 %collective-permute-start.4 = (f32[49,8,128]{2,1,0:T(8,128)S(1)}, f32[49,8,128]{2,1,0:T(8,128)S(1)}, u32[]{:S(2)}, u32[]{:S(2)}) collective-permute-start(f32[49,8,128]{2,1,0:T(8,128)S(1)} %get-tuple-element.35), channel_id=1, source_target_pairs={{0,4},{8,12},{16,20},{24,28},{4,0},{12,8},{20,16},{28,24},{1,5},{9... | collective-permute-start | bytes 602120 | tf_op jit(solution)/shard_map/ppermute | solution.py:502
  20.6 1.9 %collective-permute-start.5 = (f32[49,8,128]{2,1,0:T(8,128)S(1)}, f32[49,8,128]{2,1,0:T(8,128)S(1)}, u32[]{:S(2)}, u32[]{:S(2)}) collective-permute-start(f32[49,8,128]{2,1,0:T(8,128)S(1)} %get-tuple-element.36), channel_id=1, source_target_pairs={{4,8},{12,16},{20,24},{8,4},{16,12},{24,20},{5,9},{13,17},{21,25},... | collective-permute-start | bytes 602120 | tf_op jit(solution)/shard_map/ppermute | solution.py:503
  22.5 0.0 collective-permute-done.4.y_even
  22.5 6.1 %collective-permute-done.5.y_odd = f32[49,8,128]{2,1,0:T(8,128)S(1)} collective-permute-done((f32[49,8,128]{2,1,0:T(8,128)S(1)}, f32[49,8,128]{2,1,0:T(8,128)S(1)}, u32[]{:S(2)}, u32[]{:S(2)}) %collective-permute-start.5) | collective-permute-done | bytes 200736 | tf_op jit(solution)/shard_map/ppermute | solution.py:503
  28.6 0.1 shard_map.75
  28.7 6.9 %collective-permute-start.6 = (f32[34,8,128]{2,1,0:T(8,128)S(1)}, f32[34,8,128]{2,1,0:T(8,128)S(1)}, u32[]{:S(2)}, u32[]{:S(2)}) collective-permute-start(f32[34,8,128]{2,1,0:T(8,128)S(1)} %get-tuple-element.38), channel_id=1, source_target_pairs={{0,32},{64,96},{128,160},{192,224},{256,288},{320,352},{384,416},{... | collective-permute-start | bytes 417800 | tf_op jit(solution)/shard_map/ppermute | solution.py:502
  35.6 0.7 collective-permute-start.7
  36.3 4.0 %shard_map.76 = (f32[4,24,64,128]{3,2,1,0:T(8,128)S(1)}, f32[4,24,64,128]{3,2,1,0:T(8,128)S(1)}, f32[24,64,128]{2,1,0:T(8,128)S(1)}, f32[24,64,128]{2,1,0:T(8,12...) custom-call(f32[4]{0:T(128)} %d_in.3, ...), custom_call_target="tpu_custom_call" | custom-call | flops 3000000 | bytes 3000000 | tf_op jit(solution)/shard_map/pallas_call | solution.py:533
  40.3 0.0 collective-permute-done.6.e_even
  40.4 0.0 collective-permute-done.x_even
  40.4 13.4 %shard_map.77 = (f32[32,4,384]{2,1,0:T(4,128)S(1)}, f32[4,24,64,128]{3,2,1,0:T(8,128)S(1)}, f32[4,24,64,128]{3,2,1,0:T(8,128)S(1)}, f32[24,64,128]{2,1,0:T(8,128...) custom-call(f32[4]{0:T(128)} %d_in.3, ...), custom_call_target="tpu_custom_call", output_to_operand_aliasing={{1}: (9, {}), {2}: (10, {}), {3}: (11, {}), {4}: (12, {}), ... | custom-call | flops 10000000 | bytes 10000000 | tf_op jit(solution)/shard_map/pallas_call | solution.py:540
  53.7 25.1 %all_to_all.14.parts = f32[32,4,384]{2,1,0:T(4,128)S(1)} all-to-all(f32[32,4,384]{2,1,0:T(4,128)S(1)} %get-tuple-element.50), channel_id=1, replica_groups=mesh['gx'=16,'gy'=8,'gz'=4] {'gy','gz'}, dimensions={0} | all-to-all | bytes 393216 | tf_op jit(solution)/shard_map/all_to_all | solution.py:551
  78.9 0.2 shard_map.78
  79.1 18.1 %all_to_all.15 = f32[16,2,128]{2,1,0:T(2,128)S(1)} all-to-all(f32[16,2,128]{2,1,0:T(2,128)S(1)} %bitcast.3), channel_id=1, replica_groups=mesh['gx'=16,'gy'=8,'gz'=4] {'gx'}, dimensions={0} | all-to-all | bytes 32768 | tf_op jit(solution)/shard_map/all_to_all | solution.py:555
  97.2 0.1 reduce_sum.12
  97.3 0.6 copy.15
  (3 shorter events, 0.0 us)
Async XLA Ops:
  2.2 38.1 %collective-permute-start = (f32[36,32,128]{2,1,0:T(8,128)S(1)}, f32[36,32,128]{2,1,0:T(8,128)S(1)}, u32[]{:S(2)}, u32[]{:S(2)}) collective-permute-start(f32[36,32,128]{2,1,0:T(8,128)S(1)} %get-tuple-element.28), channel_id=1, source_target_pairs={{0,32},{64,96},{128,160},{192,224},{256,288},{320,352},{384,416},{... | collective-permute-start | bytes 1769480 | tf_op jit(solution)/shard_map/ppermute | solution.py:502
  7.1 33.3 %collective-permute-start.1 = (f32[36,32,128]{2,1,0:T(8,128)S(1)}, f32[36,32,128]{2,1,0:T(8,128)S(1)}, u32[]{:S(2)}, u32[]{:S(2)}) collective-permute-start(f32[36,32,128]{2,1,0:T(8,128)S(1)} %get-tuple-element.29), channel_id=1, source_target_pairs={{32,64},{96,128},{160,192},{224,256},{288,320},{352,384},{416,448}... | collective-permute-start | bytes 1769480 | tf_op jit(solution)/shard_map/ppermute | solution.py:503
  7.8 5.7 %collective-permute-start.2 = (f32[8,32,128]{2,1,0:T(8,128)S(1)}, f32[8,32,128]{2,1,0:T(8,128)S(1)}, u32[]{:S(2)}, u32[]{:S(2)}) collective-permute-start(f32[8,32,128]{2,1,0:T(8,128)S(1)} %get-tuple-element.30), channel_id=1, source_target_pairs={{0,1},{2,3},{1,0},{3,2},{4,5},{6,7},{5,4},{7,6},{8,9},{10,11},{9,8... | collective-permute-start | bytes 393224 | tf_op jit(solution)/shard_map/ppermute | solution.py:502
  10.9 2.6 %collective-permute-start.3 = (f32[8,32,128]{2,1,0:T(8,128)S(1)}, f32[8,32,128]{2,1,0:T(8,128)S(1)}, u32[]{:S(2)}, u32[]{:S(2)}) collective-permute-start(f32[8,32,128]{2,1,0:T(8,128)S(1)} %get-tuple-element.31), channel_id=1, source_target_pairs={{1,2},{2,1},{5,6},{6,5},{9,10},{10,9},{13,14},{14,13},{17,18},{18,... | collective-permute-start | bytes 393224 | tf_op jit(solution)/shard_map/ppermute | solution.py:503
  13.6 8.9 %collective-permute-start.4 = (f32[49,8,128]{2,1,0:T(8,128)S(1)}, f32[49,8,128]{2,1,0:T(8,128)S(1)}, u32[]{:S(2)}, u32[]{:S(2)}) collective-permute-start(f32[49,8,128]{2,1,0:T(8,128)S(1)} %get-tuple-element.35), channel_id=1, source_target_pairs={{0,4},{8,12},{16,20},{24,28},{4,0},{12,8},{20,16},{28,24},{1,5},{9... | collective-permute-start | bytes 602120 | tf_op jit(solution)/shard_map/ppermute | solution.py:502
  20.6 8.0 %collective-permute-start.5 = (f32[49,8,128]{2,1,0:T(8,128)S(1)}, f32[49,8,128]{2,1,0:T(8,128)S(1)}, u32[]{:S(2)}, u32[]{:S(2)}) collective-permute-start(f32[49,8,128]{2,1,0:T(8,128)S(1)} %get-tuple-element.36), channel_id=1, source_target_pairs={{4,8},{12,16},{20,24},{8,4},{16,12},{24,20},{5,9},{13,17},{21,25},... | collective-permute-start | bytes 602120 | tf_op jit(solution)/shard_map/ppermute | solution.py:503
  28.7 11.7 %collective-permute-start.6 = (f32[34,8,128]{2,1,0:T(8,128)S(1)}, f32[34,8,128]{2,1,0:T(8,128)S(1)}, u32[]{:S(2)}, u32[]{:S(2)}) collective-permute-start(f32[34,8,128]{2,1,0:T(8,128)S(1)} %get-tuple-element.38), channel_id=1, source_target_pairs={{0,32},{64,96},{128,160},{192,224},{256,288},{320,352},{384,416},{... | collective-permute-start | bytes 417800 | tf_op jit(solution)/shard_map/ppermute | solution.py:502
  35.6 4.7 %collective-permute-start.7 = (f32[34,8,128]{2,1,0:T(8,128)S(1)}, f32[34,8,128]{2,1,0:T(8,128)S(1)}, u32[]{:S(2)}, u32[]{:S(2)}) collective-permute-start(f32[34,8,128]{2,1,0:T(8,128)S(1)} %get-tuple-element.39), channel_id=1, source_target_pairs={{32,64},{96,128},{160,192},{224,256},{288,320},{352,384},{416,448}... | collective-permute-start | bytes 417800 | tf_op jit(solution)/shard_map/ppermute | solution.py:503
